TPU v7x, 128 devices: a whole 4x4x4 slice. The times are simulated.
128 devices in a mesh: tm: 16 (over y, z), table: 8 (over x, core).
Axes of the slice: x: 4, y: 4, z: 4, core: 2. Of those that a mesh axis runs over, the one named last changes fastest.
Arguments:
- item_owner: int32 [16, 12288, 1], P('table', 'tm'), may hold values from 0 to 127; in each aligned block of 768 rows (0 to 767, 768 to 1535, ..., all dimensions but the last counted through in order) at most 12 rows name the same one
- item_row: int32 [16, 12288], P('table', 'tm'), may hold values from 0 to 4095
- history_len: int32 [16], P('table'), may hold values from 3072 to 12288, as said below
- event_gap: float32 [16, 12288], P('table', 'tm'), may hold values from 0 to 36864, as said below
- item_table: bfloat16 [524288, 512], P(('tm', 'table')), may hold values from -6 to 6
- norm_gain: float32 [512], replicated, may hold values from 0.1 to 1.9
- in_weight: bfloat16 [512, 2192], replicated, may hold values from -0.25 to 0.25
- conv_weight: float32 [4, 1152], replicated, may hold values from -3 to 3
- conv_bias: float32 [1152], replicated, may hold values from -3 to 3
- dt_bias: float32 [16], replicated, may hold values from -1 to 1
- decay_rate: float32 [16], replicated, may hold values from 0 to 16, as said below
- out_gain: float32 [1024], replicated, may hold values from 0.1 to 1.9
- emitted_projection: bfloat16 [1024, 512], replicated, may hold values from -0.1875 to 0.1875
Outputs:
- layer_out: bfloat16 [16, 12288, 512], P('table', 'tm')
Inputs may be any that keep to these rules, and one draw needn't show every extreme that they name: `item_owner`: in every user's 768 events held by one device no owner is named more than 12 times, a bound that some block reaches. `history_len`: some user has all 12288 events and some user 12288 // 4. `event_gap`: Positive. `decay_rate`: Positive.
All inputs are finite; a program needn't handle non-finite values.
Results may differ from a plain program's by a relative error of at most 0.01.
Values may be sent and summed in bfloat16 or wider, within the bound.
No kernel may reach another device: no remote copies, remote signals or barrier semaphores. Data moves between devices by JAX's collectives and lax.ppermute only.
A program may use at most 192 MiB of HBM per device.

v0:
```python
import functools

import jax
import jax.numpy as jnp
from jax import lax
from jax.experimental import pallas as pl
from jax.experimental.pallas import tpu as pltpu
from jax.sharding import PartitionSpec as P

F32 = jnp.float32
BF16 = jnp.bfloat16
EPS = 1e-05
LANES = 128
CHUNK = 128
ROWS3 = 256
TABLE_STEP = 512
VMEM_LIMIT = 56 * 1024 * 1024


def params(axes):
    return pltpu.CompilerParams(
        dimension_semantics=("arbitrary",) * axes, vmem_limit_bytes=VMEM_LIMIT
    )


def full(shape):
    return pl.BlockSpec(shape, lambda *_: (0,) * len(shape))


def iota(shape, axis):
    return lax.broadcasted_iota(jnp.int32, shape, axis)


def nt(a, b):
    return lax.dot_general(a, b, (((1,), (1,)), ((), ())), preferred_element_type=F32)


def mm(a, b):
    return jnp.dot(a, b, preferred_element_type=F32)


def silu(v):
    half = 0.5 * v
    return half + half * jnp.tanh(half)


def route_kernel(owner_ref, row_ref, req_ref, place_ref, *, devices, cap, width):
    users, events = owner_ref.shape
    tri = jnp.where(
        (iota((LANES, 2 * LANES), 0) < iota((LANES, 2 * LANES), 1))
        | (iota((LANES, 2 * LANES), 1) >= LANES),
        1.0,
        0.0,
    ).astype(BF16)
    slots = users * cap
    req = jnp.zeros((devices, width), F32)
    for u in range(users):
        running = jnp.zeros((devices, LANES), F32)
        for c in range(events // LANES):
            own = owner_ref[u : u + 1, c * LANES : (c + 1) * LANES]
            row = row_ref[u : u + 1, c * LANES : (c + 1) * LANES]
            hot = iota((devices, LANES), 0) == own
            hot_b = jnp.where(hot, 1.0, 0.0).astype(BF16)
            counts = mm(hot_b, tri)
            rank = counts[:, :LANES] + running
            running = running + counts[:, LANES:]
            slot = jnp.sum(jnp.where(hot, rank, 0.0), axis=0, keepdims=True).astype(jnp.int32)
            slot = slot + u * cap
            match = iota((width, LANES), 0) == slot
            high = jnp.where(match, (row >> 6).astype(F32), 0.0).astype(BF16)
            low = jnp.where(match, (row & 63).astype(F32), 0.0).astype(BF16)
            req = req + 64.0 * nt(hot_b, high) + nt(hot_b, low)
            place = (own * (slots * 2 // 3) + slot - u * (slots // 3)).astype(F32)
            place_ref[u, c * LANES : (c + 1) * LANES, :] = jnp.broadcast_to(
                place, (LANES, LANES)
            ).T.astype(jnp.int32)
    req_ref[:, 0, :] = req.astype(jnp.int32)


def route(owners, rows, devices, cap, width):
    users, events = owners.shape
    return pl.pallas_call(
        functools.partial(route_kernel, devices=devices, cap=cap, width=width),
        out_shape=(
            jax.ShapeDtypeStruct((devices, 1, width), jnp.int32),
            jax.ShapeDtypeStruct((users, events, LANES), jnp.int32),
        ),
        compiler_params=params(0),
        name="route",
    )(owners, rows)


def fetch_kernel(idx_ref, tab_ref, out_ref, tab4, rows4, *, slots):
    i = pl.program_id(0)
    step, dim = tab_ref.shape
    tiles = dim // LANES
    for cb in range(tiles):
        tab4[pl.ds(i * step * tiles + cb, step, stride=tiles), :] = tab_ref[
            :, cb * LANES : (cb + 1) * LANES
        ].astype(F32)

    @pl.when(i == pl.num_programs(0) - 1)
    def _():
        owners = idx_ref.shape[0]

        def body(o, carry):
            base = pl.multiple_of(o * slots * tiles, 8)
            for s in range(slots):
                r = idx_ref[o, 0, s]
                rows4[pl.ds(base + tiles * s, tiles), :] = tab4[
                    pl.ds(pl.multiple_of(r * tiles, tiles), tiles), :
                ]
            return carry

        lax.fori_loop(0, owners, body, 0)

        def pack(g, carry):
            for half in range(2):
                for cb in range(tiles):
                    start = (g * 2 + half) * 16 * tiles + cb
                    out_ref[
                        pl.ds(pl.multiple_of((g * 2 + half) * 16, 16), 16),
                        cb * LANES : (cb + 1) * LANES,
                    ] = rows4[pl.ds(start, 16, stride=tiles), :].astype(BF16)
            return carry

        lax.fori_loop(0, owners * slots // 32, pack, 0)


def fetch(idx, table, slots):
    owners = idx.shape[0]
    items, dim = table.shape
    tiles = dim // LANES
    return pl.pallas_call(
        functools.partial(fetch_kernel, slots=slots),
        out_shape=jax.ShapeDtypeStruct((owners * slots, dim), BF16),
        grid=(items // TABLE_STEP,),
        in_specs=[
            pl.BlockSpec(memory_space=pltpu.SMEM),
            pl.BlockSpec((TABLE_STEP, dim), lambda i: (i, 0)),
        ],
        out_specs=full((owners * slots, dim)),
        scratch_shapes=[
            pltpu.VMEM((items * tiles, LANES), F32),
            pltpu.VMEM((owners * slots * tiles, LANES), F32),
        ],
        compiler_params=params(1),
        name="fetch",
    )(idx, table)


def project_kernel(
    got_ref, place_ref, gain_ref, w_ref, x_ref, gate_ref, conv_ref, step_ref, tail_ref, *, inner
):
    u = pl.program_id(0)
    owners, slots, dim = got_ref.shape
    window = slots * 2 // 3
    rows = place_ref.shape[1]
    shift = pl.multiple_of(u * (slots // 3), 8)
    got = got_ref[:, pl.ds(shift, window), :].reshape(owners * window, dim)
    place = place_ref[0]
    pieces = [
        jnp.where(place == iota((rows, LANES), 1) + k * LANES, 1.0, 0.0).astype(BF16)
        for k in range(owners * window // LANES)
    ]
    x = mm(jnp.concatenate(pieces, axis=1), got)
    x_ref[0] = x.astype(BF16)
    normed = x * lax.rsqrt(jnp.mean(x * x, axis=-1, keepdims=True) + EPS) * gain_ref[...]
    normed = normed.astype(BF16)
    conv_dim = conv_ref.shape[2]
    heads = step_ref.shape[1]
    conv = mm(normed, w_ref[:, inner : inner + conv_dim]).astype(BF16)
    conv_ref[0] = conv
    raw = mm(normed, w_ref[:, inner + conv_dim : inner + conv_dim + heads])
    step_ref[0] = raw.astype(BF16).astype(F32).T
    gate_ref[0] = mm(normed, w_ref[:, :inner]).astype(BF16)
    tail_ref[0] = conv[rows - 8 :, :]


def project(got, place, gain, weight, inner, conv_dim, heads):
    users, events, _ = place.shape
    dim = got.shape[2]
    rows = ROWS3
    block = lambda width: pl.BlockSpec((1, rows, width), lambda u, i: (u, i, 0))
    return pl.pallas_call(
        functools.partial(project_kernel, inner=inner),
        out_shape=(
            jax.ShapeDtypeStruct((users, events, dim), BF16),
            jax.ShapeDtypeStruct((users, events, inner), BF16),
            jax.ShapeDtypeStruct((users, events, conv_dim), BF16),
            jax.ShapeDtypeStruct((users, heads, events), F32),
            jax.ShapeDtypeStruct((users, 8, conv_dim), BF16),
        ),
        grid=(users, events // rows),
        in_specs=[full(got.shape), block(LANES), full(gain.shape), full(weight.shape)],
        out_specs=(
            block(dim),
            block(inner),
            block(conv_dim),
            pl.BlockSpec((1, heads, rows), lambda u, i: (u, 0, i)),
            pl.BlockSpec((1, 8, conv_dim), lambda u, i: (u, 0, 0)),
        ),
        compiler_params=params(2),
        name="project",
    )(got, place, gain, weight)


def lane_halves(rows_a, rows_b):
    return jnp.where(iota(rows_a.shape, rows_a.ndim - 1) < LANES // 2, rows_a, rows_b)


def running_sum(values, reverse):
    lane = iota(values.shape, 1)
    size = values.shape[1]
    k = 1
    while k < size:
        if reverse:
            values = values + jnp.where(lane < size - k, pltpu.roll(values, size - k, 1), 0.0)
        else:
            values = values + jnp.where(lane >= k, pltpu.roll(values, k, 1), 0.0)
        k *= 2
    return values


def pair_rhs(pair):
    low = iota(pair.shape, 1) < LANES // 2
    zero = jnp.zeros_like(pair)
    return jnp.concatenate([jnp.where(low, pair, zero), jnp.where(low, zero, pair)], axis=0)


def states_kernel(
    len_ref,
    pos_ref,
    conv_ref,
    edge_ref,
    step_ref,
    gap_ref,
    cw_ref,
    cb_ref,
    dt_ref,
    rate_ref,
    xbc_ref,
    cum_ref,
    steps_ref,
    hold_ref,
    decay_ref,
    end_ref,
    window,
    state,
    pref,
):
    u = pl.program_id(0)
    c = pl.program_id(1)
    heads = step_ref.shape[1]
    pairs = heads // 2
    inner = pairs * LANES
    n_state = state.shape[0]

    @pl.when(c == 0)
    def _():
        window[0:8, :] = edge_ref[0].astype(F32)
        state[...] = jnp.zeros_like(state)
        pref[...] = jnp.zeros_like(pref)

    @pl.when(c > 0)
    def _():
        window[0:8, :] = window[CHUNK : CHUNK + 8, :]

    window[8 : CHUNK + 8, :] = conv_ref[0].astype(F32)
    total = cb_ref[...]
    for k in range(4):
        total = total + cw_ref[k : k + 1, :] * window[5 + k : 5 + k + CHUNK, :]
    xbc = silu(total).astype(BF16)
    xbc_ref[0] = xbc

    position = pos_ref[0] + c * CHUNK + iota((heads, CHUNK), 1)
    alive = jnp.where(position < len_ref[u], 1.0, 0.0)
    raw = step_ref[0] + dt_ref[...]
    steps = alive * (jnp.maximum(raw, 0.0) + jnp.log1p(jnp.exp(-jnp.abs(raw))))
    log_decay = -rate_ref[...] * gap_ref[0] * steps
    cum = running_sum(log_decay, False)
    back = running_sum(log_decay, True)
    after = jnp.where(
        iota(back.shape, 1) < CHUNK - 1, pltpu.roll(back, CHUNK - 1, 1), 0.0
    )
    cum_ref[0] = cum
    steps_ref[0] = steps
    weight = jnp.exp(after) * steps
    tot = jnp.broadcast_to(back[:, 0:1], (heads, LANES))

    decay_ref[0, 0] = jnp.exp(pref[...])
    hold_ref[0, 0] = state[...].astype(BF16)
    coef_t = xbc[:, inner : inner + LANES].astype(F32).T[:n_state, :]
    for j in range(pairs):
        lanes = slice(j * LANES, (j + 1) * LANES)
        left = jnp.concatenate(
            [coef_t * weight[2 * j : 2 * j + 1, :], coef_t * weight[2 * j + 1 : 2 * j + 2, :]],
            axis=1,
        ).astype(BF16)
        add = mm(left, pair_rhs(xbc[:, lanes]))
        tot_pair = lane_halves(tot[2 * j : 2 * j + 1, :], tot[2 * j + 1 : 2 * j + 2, :])
        state[:, lanes] = jnp.exp(tot_pair) * state[:, lanes] + add
        pref[:, lanes] = pref[:, lanes] + tot_pair

    @pl.when(c == pl.num_programs(1) - 1)
    def _():
        half = LANES // 2

        def put(user):
            for h in range(heads):
                lanes = slice((h // 2) * LANES, (h // 2 + 1) * LANES)
                value = state[:, lanes]
                low = jnp.broadcast_to(pref[:, lanes], (8, LANES))
                if h % 2 != user:
                    value = pltpu.roll(value, half, 1)
                    low = pltpu.roll(low, half, 1)
                high = low.astype(BF16).astype(F32)
                row = iota((8, LANES), 0)
                extra = jnp.where(row == 0, high, jnp.where(row == 1, low - high, 0.0))
                packed = jnp.concatenate([value, extra], axis=0)
                if user:
                    packed = lane_halves(end_ref[h].astype(F32), packed)
                end_ref[h] = packed.astype(BF16)

        for user in range(2):
            pl.when(u == user)(functools.partial(put, user))


def chunk_states(lens, pos, conv, edge, step, gap, cw, cb, dt, rate, n_state):
    users, events, conv_dim = conv.shape
    heads = step.shape[1]
    inner = conv_dim - 2 * n_state
    chunks = events // CHUNK
    smem = pl.BlockSpec(memory_space=pltpu.SMEM)
    head_block = pl.BlockSpec((1, heads, CHUNK), lambda u, c: (u, 0, c))
    return pl.pallas_call(
        states_kernel,
        out_shape=(
            jax.ShapeDtypeStruct((users, events, conv_dim), BF16),
            jax.ShapeDtypeStruct((users, heads, events), F32),
            jax.ShapeDtypeStruct((users, heads, events), F32),
            jax.ShapeDtypeStruct((users, chunks, n_state, inner), BF16),
            jax.ShapeDtypeStruct((users, chunks, 1, inner), F32),
            jax.ShapeDtypeStruct((heads, n_state + 8, LANES), BF16),
        ),
        grid=(users, chunks),
        in_specs=[
            smem,
            smem,
            pl.BlockSpec((1, CHUNK, conv_dim), lambda u, c: (u, c, 0)),
            pl.BlockSpec((1, 8, conv_dim), lambda u, c: (u, 0, 0)),
            head_block,
            pl.BlockSpec((1, 1, CHUNK), lambda u, c: (u, 0, c)),
            full(cw.shape),
            full(cb.shape),
            full(dt.shape),
            full(rate.shape),
        ],
        out_specs=(
            pl.BlockSpec((1, CHUNK, conv_dim), lambda u, c: (u, c, 0)),
            head_block,
            head_block,
            pl.BlockSpec((1, 1, n_state, inner), lambda u, c: (u, c, 0, 0)),
            pl.BlockSpec((1, 1, 1, inner), lambda u, c: (u, c, 0, 0)),
            full((heads, n_state + 8, LANES)),
        ),
        scratch_shapes=[
            pltpu.VMEM((CHUNK + 8, conv_dim), F32),
            pltpu.VMEM((n_state, inner), F32),
            pltpu.VMEM((1, inner), F32),
        ],
        compiler_params=params(2),
        name="chunk_states",
    )(lens, pos, conv, edge, step, gap, cw, cb, dt, rate)


def scan_kernel(in_ref, out_ref):
    spans, rows, lanes = in_ref.shape
    n_state = rows - 8
    running = jnp.zeros((n_state, lanes), F32)
    for k in range(spans):
        out_ref[k] = running.astype(BF16)
        block = in_ref[k].astype(F32)
        log_decay = block[n_state : n_state + 1, :] + block[n_state + 1 : n_state + 2, :]
        running = jnp.exp(log_decay) * running + block[:n_state, :]


def scan_spans(ends):
    spans, rows, lanes = ends.shape
    return pl.pallas_call(
        scan_kernel,
        out_shape=jax.ShapeDtypeStruct((spans, rows - 8, lanes), BF16),
        compiler_params=params(0),
        name="scan_spans",
    )(ends)


def local_kernel(xbc_ref, cum_ref, steps_ref, y_ref):
    heads = cum_ref.shape[1]
    pairs = heads // 2
    inner = pairs * LANES
    half = LANES // 2
    xbc = xbc_ref[0]
    in_coef = xbc[:, inner : inner + half]
    out_coef = xbc[:, inner + half : inner + LANES]
    scores = nt(out_coef, in_coef)
    causal = iota((CHUNK, CHUNK), 0) >= iota((CHUNK, CHUNK), 1)
    scores = jnp.where(causal, scores, 0.0)
    cum = cum_ref[0]
    steps = steps_ref[0]
    cum_t = jnp.concatenate([cum, jnp.zeros((LANES - heads, CHUNK), F32)], axis=0).T

    def mixing(h):
        spread = jnp.broadcast_to(cum_t[:, h : h + 1], (CHUNK, CHUNK)) - cum[h : h + 1, :]
        fading = jnp.exp(jnp.minimum(spread, 0.0))
        return (scores * fading * steps[h : h + 1, :]).astype(BF16)

    for j in range(pairs):
        lanes = slice(j * LANES, (j + 1) * LANES)
        left = jnp.concatenate([mixing(2 * j), mixing(2 * j + 1)], axis=1)
        y_ref[0, :, lanes] = mm(left, pair_rhs(xbc[:, lanes])).astype(BF16)


def local_response(xbc, cum, steps, inner):
    users, events, conv_dim = xbc.shape
    heads = cum.shape[1]
    head_block = pl.BlockSpec((1, heads, CHUNK), lambda u, c: (u, 0, c))
    return pl.pallas_call(
        local_kernel,
        out_shape=jax.ShapeDtypeStruct((users, events, inner), BF16),
        grid=(users, events // CHUNK),
        in_specs=[
            pl.BlockSpec((1, CHUNK, conv_dim), lambda u, c: (u, c, 0)),
            head_block,
            head_block,
        ],
        out_specs=pl.BlockSpec((1, CHUNK, inner), lambda u, c: (u, c, 0)),
        compiler_params=params(2),
        name="local_response",
    )(xbc, cum, steps)


def finish_kernel(
    len_ref,
    pos_ref,
    y_ref,
    coef_ref,
    gate_ref,
    x_ref,
    cum_ref,
    hold_ref,
    decay_ref,
    hin_ref,
    gain_ref,
    w_ref,
    out_ref,
    incoming,
    gated_ref,
    normed_ref,
):
    u = pl.program_id(0)
    c = pl.program_id(1)
    heads = cum_ref.shape[1]
    pairs = heads // 2
    half = LANES // 2

    def take(user):
        for j in range(pairs):
            a = hin_ref[2 * j].astype(F32)
            b = hin_ref[2 * j + 1].astype(F32)
            if user:
                a = pltpu.roll(a, half, 1)
            else:
                b = pltpu.roll(b, half, 1)
            incoming[:, j * LANES : (j + 1) * LANES] = lane_halves(a, b)

    for user in range(2):
        pl.when((c == 0) & (u == user))(functools.partial(take, user))

    held = (hold_ref[0, 0].astype(F32) + decay_ref[0, 0] * incoming[...]).astype(BF16)
    carried = mm(coef_ref[0][:, half:], held)
    cum = cum_ref[0]
    cum_t = jnp.concatenate([cum, jnp.zeros((LANES - heads, CHUNK), F32)], axis=0).T
    size = 2 * LANES
    same = jnp.where(
        iota((size, size), 0) // half == iota((size, size), 1) // half, 1.0 / half, 0.0
    ).astype(BF16)
    for j in range(pairs):
        lanes = slice(j * LANES, (j + 1) * LANES)
        fade = jnp.exp(
            lane_halves(
                jnp.broadcast_to(cum_t[:, 2 * j : 2 * j + 1], (CHUNK, LANES)),
                jnp.broadcast_to(cum_t[:, 2 * j + 1 : 2 * j + 2], (CHUNK, LANES)),
            )
        )
        response = y_ref[0, :, lanes].astype(F32) + fade * carried[:, lanes]
        gated_ref[:, lanes] = response * silu(gate_ref[0, :, lanes].astype(F32))
    for j in range(pairs // 2):
        lanes = slice(j * size, (j + 1) * size)
        gated = gated_ref[:, lanes]
        mean = mm((gated * gated).astype(BF16), same)
        normed_ref[:, lanes] = (gated * lax.rsqrt(mean + EPS) * gain_ref[:, lanes]).astype(BF16)
    mixed = mm(normed_ref[...], w_ref[...])
    position = pos_ref[0] + c * CHUNK + iota((CHUNK, 1), 0)
    alive = jnp.where(position < len_ref[u], 1.0, 0.0)
    out_ref[0] = (alive * (x_ref[0].astype(F32) + mixed)).astype(BF16)


def finish(lens, pos, y, xbc, gate, x, cum, hold, decay, hin, gain, weight):
    users, events, inner = y.shape
    heads = cum.shape[1]
    n_state = hold.shape[2]
    dim = x.shape[2]
    smem = pl.BlockSpec(memory_space=pltpu.SMEM)
    block = lambda width: pl.BlockSpec((1, CHUNK, width), lambda u, c: (u, c, 0))
    return pl.pallas_call(
        finish_kernel,
        out_shape=jax.ShapeDtypeStruct((users, events, dim), BF16),
        grid=(users, events // CHUNK),
        in_specs=[
            smem,
            smem,
            block(inner),
            pl.BlockSpec((1, CHUNK, LANES), lambda u, c: (u, c, inner // LANES)),
            block(inner),
            block(dim),
            pl.BlockSpec((1, heads, CHUNK), lambda u, c: (u, 0, c)),
            pl.BlockSpec((1, 1, n_state, inner), lambda u, c: (u, c, 0, 0)),
            pl.BlockSpec((1, 1, 1, inner), lambda u, c: (u, c, 0, 0)),
            full(hin.shape),
            full(gain.shape),
            full(weight.shape),
        ],
        out_specs=block(dim),
        scratch_shapes=[
            pltpu.VMEM((n_state, inner), F32),
            pltpu.VMEM((CHUNK, inner), F32),
            pltpu.VMEM((CHUNK, inner), BF16),
        ],
        compiler_params=params(2),
        name="finish",
    )(lens, pos, y, xbc, gate, x, cum, hold, decay, hin, gain, weight)


def exchange(values, axes):
    return lax.all_to_all(values, axes, split_axis=0, concat_axis=0, tiled=True)


def per_device(
    item_owner,
    item_row,
    history_len,
    event_gap,
    item_table,
    norm_gain,
    in_weight,
    conv_weight,
    conv_bias,
    dt_bias,
    decay_rate,
    out_gain,
    emitted_projection,
):
    users, events = item_row.shape
    dim = item_table.shape[1]
    heads = dt_bias.shape[0]
    inner = emitted_projection.shape[0]
    conv_dim = conv_weight.shape[1]
    n_state = (conv_dim - inner) // 2
    times = lax.axis_size("tm")
    devices = times * lax.axis_size("table")
    cap = 2 * events // devices
    slots = users * cap
    everyone = ("tm", "table")
    pos = (lax.axis_index("tm") * events).reshape(1).astype(jnp.int32)

    requests, place = route(item_owner[..., 0], item_row, devices, cap, 32)
    asked = exchange(requests, everyone)
    rows = fetch(asked, item_table, slots)
    got = exchange(rows.reshape(devices, slots, dim), everyone)
    x, gate, conv, step, tail = project(
        got, place, norm_gain[None, :], in_weight, inner, conv_dim, heads
    )
    edge = lax.ppermute(tail, "tm", [(i, i + 1) for i in range(times - 1)])
    xbc, cum, steps, hold, decay, ends = chunk_states(
        history_len,
        pos,
        conv,
        edge,
        step,
        event_gap[:, None, :],
        conv_weight,
        conv_bias[None, :],
        dt_bias[:, None],
        decay_rate[:, None],
        n_state,
    )
    by_head = exchange(ends, "tm")
    y = local_response(xbc, cum, steps, inner)
    hin = exchange(scan_spans(by_head), "tm")
    return finish(
        history_len,
        pos,
        y,
        xbc,
        gate,
        x,
        cum,
        hold,
        decay,
        hin,
        out_gain[None, :],
        emitted_projection,
    )


def solution(mesh):
    in_specs = (
        P("table", "tm", None),
        P("table", "tm"),
        P("table"),
        P("table", "tm"),
        P(("tm", "table"), None),
        P(),
        P(),
        P(),
        P(),
        P(),
        P(),
        P(),
        P(),
    )
    out_specs = P("table", "tm", None)
    return jax.shard_map(
        per_device, mesh=mesh, in_specs=in_specs, out_specs=out_specs, check_vma=False
    )
```

profile of v0, /device:TPU:0, one launch (start us, length us, event | category | flops | bytes accessed | tf_op | source)
XLA Modules:
  0.0 172.2 jit_solution(8304567006986326918)
XLA Ops:
  0.0 1.3 copy.19
  1.3 2.6 %route.1 = (s32[128,1,32]{2,1,0:T(1,128)}, s32[2,768,128]{2,1,0:T(8,128)}) custom-call(s32[2,768]{1,0:T(2,128)} %bitcast.10, s32[2,768]{1,0:T(2,128)} %row_ref.1), custom_call_target="tpu_custom_call" | custom-call | tf_op jit(solution)/shard_map/route/pallas_call | solution.py:82
  3.9 20.8 %all_to_all.20.idx_ref = s32[128,1,32]{2,1,0:T(1,128)} all-to-all(s32[128,1,32]{2,1,0:T(1,128)} %get-tuple-element.18), channel_id=1, replica_groups=mesh['tm'=16,'table'=8] {'tm','table'}, dimensions={0} | all-to-all | bytes 32768 | tf_op jit(solution)/shard_map/all_to_all | solution.py:546
  24.7 12.3 %fetch.1 = bf16[3072,512]{1,0:T(8,128)(2,1)} custom-call(s32[128,1,32]{2,1,0:T(1,128)} %all_to_all.20.idx_ref, bf16[4096,512]{1,0:T(8,128)(2,1)} %tab_ref.1), custom_call_target="tpu_custom_call" | custom-call | tf_op jit(solution)/shard_map/fetch/pallas_call | solution.py:134
  36.9 4.9 %all-to-all-start.1 = ((bf16[128,24,512]{2,1,0:T(8,128)(2,1)}), bf16[128,24,512]{2,1,0:T(8,128)(2,1)S(1)}, u32[]{:S(2)}, u32[]{:S(2)}) async-start(bf16[128,24,512]{2,1,0:T(8,128)(2,1)} %bitcast.9), calls=%async_computation.1 | async-start | bytes 6291456 | tf_op jit(solution)/shard_map/all_to_all | solution.py:546
  41.8 4.2 %copy.14.w_ref = bf16[512,2192]{1,0:T(8,128)(2,1)} copy(bf16[512,2192]{0,1:T(8,128)(2,1)} %param.19) | data formatting | bytes 4489216 | tf_op args[6]
  46.0 37.4 %all-to-all-done.1.got_ref = bf16[128,24,512]{2,1,0:T(8,128)(2,1)S(1)} async-done(((bf16[128,24,512]{2,1,0:T(8,128)(2,1)}), bf16[128,24,512]{2,1,0:T(8,128)(2,1)S(1)}, u32[]{:S(2)}, u32[]{:S(2)}) %all-to-all-start.1) | async-done | bytes 3145760 | tf_op jit(solution)/shard_map/all_to_all | solution.py:546
  83.4 0.0 copy-start
  83.4 1.6 copy-done
  85.1 0.0 copy-start.3
  85.1 0.0 copy-start.4
  85.1 0.0 copy-start.5
  85.1 0.0 copy-start.6
  85.1 13.3 %project.1 = (bf16[2,768,512]{2,1,0:T(8,128)(2,1)}, bf16[2,768,1024]{2,1,0:T(8,128)(2,1)}, bf16[2,768,1152]{2,1,0:T(8,128)(2,1)}, f32[2,16,768]{2,1,0:T(8,128)}, bf16[2,8,1152]{2,1,0:T(8,128)(2,1)}) custom-call(bf16[128,24,512]{2,1,0:T(8,128)(2,1)} %copy-done, s32[2,768,128]{2,1,0:T(8,128)} %get-tuple-element.19.place_ref, f32[1,512]{1,0:T(1,128)} %bitcast.12, ...), custom_call_target="tpu_custom_call" | custom-call | tf_op jit(solution)/shard_map/project/pallas_call | solution.py:185
  98.4 2.2 %collective-permute-start = (bf16[2,8,1152]{2,1,0:T(8,128)(2,1)}, bf16[2,8,1152]{2,1,0:T(8,128)(2,1)S(1)}, u32[]{:S(2)}, u32[]{:S(2)}) collective-permute-start(bf16[2,8,1152]{2,1,0:T(8,128)(2,1)} %get-tuple-element.21), channel_id=1, source_target_pairs={{0,8},{8,16},{16,24},{24,32},{32,40},{40,48},{48,56},{56,64},{64,7... | collective-permute-start | bytes 110600 | tf_op jit(solution)/shard_map/ppermute | solution.py:584
  100.6 0.0 copy-done.3
  100.6 0.6 broadcast_in_dim.20.cb_ref
  101.2 0.0 copy-done.4
  101.2 0.6 broadcast_in_dim.19.gap_ref
  101.8 0.0 copy-done.5
  101.8 0.7 copy.15.dt_ref
  102.5 0.0 copy-done.6
  102.5 0.7 copy.16.rate_ref
  103.1 0.0 collective-permute-done.edge_ref
  103.1 0.0 copy-start.2
  103.1 0.6 copy-done.2
  103.8 20.3 %chunk_states.1 = (bf16[2,768,1152]{2,1,0:T(8,128)(2,1)}, f32[2,16,768]{2,1,0:T(8,128)}, f32[2,16,768]{2,1,0:T(8,128)}, bf16[2,6,64,1024]{3,2,1,0:T(8,128)(2,1)}...) custom-call(s32[2]{0:T(128)} %len_ref.3, s32[1]{0:T(128)} %bitcast.pos_ref, ...), custom_call_target="tpu_custom_call" | custom-call | tf_op jit(solution)/shard_map/chunk_states/pallas_call | solution.py:336
  124.1 14.4 %all_to_all.21.in_ref = bf16[16,72,128]{2,1,0:T(8,128)(2,1)} all-to-all(bf16[16,72,128]{2,1,0:T(8,128)(2,1)} %get-tuple-element.30), channel_id=1, replica_groups=mesh['tm'=16,'table'=8] {'tm'}, dimensions={0} | all-to-all | bytes 589824 | tf_op jit(solution)/shard_map/all_to_all | solution.py:546
  138.5 1.7 %scan_spans.1 = bf16[16,64,128]{2,1,0:T(8,128)(2,1)} custom-call(bf16[16,72,128]{2,1,0:T(8,128)(2,1)} %all_to_all.21.in_ref), custom_call_target="tpu_custom_call" | custom-call | tf_op jit(solution)/shard_map/scan_spans/pallas_call | solution.py:390
  140.3 3.6 %all-to-all-start.3 = ((bf16[16,64,128]{2,1,0:T(8,128)(2,1)}), bf16[16,64,128]{2,1,0:T(8,128)(2,1)S(1)}, u32[]{:S(2)}, u32[]{:S(2)}) async-start(bf16[16,64,128]{2,1,0:T(8,128)(2,1)} %scan_spans.1), calls=%async_computation.3 | async-start | bytes 524288 | tf_op jit(solution)/shard_map/all_to_all | solution.py:546
  143.9 12.2 %local_response.1.y_ref = bf16[2,768,1024]{2,1,0:T(8,128)(2,1)} custom-call(bf16[2,768,1152]{2,1,0:T(8,128)(2,1)} %get-tuple-element.23.xbc_ref.coef_ref, f32[2,16,768]{2,1,0:T(8,128)} %get-tuple-element.24.cum_ref, f32[2,16,768]{2,1,0:T(8,128)} %get-tuple-element.25.steps_ref), custom_call_target="tpu_custom_call" | custom-call | tf_op jit(solution)/shard_map/local_response/pallas_call | solution.py:428
  156.1 0.0 all-to-all-done.3.hin_ref
  156.1 0.0 copy-start.1
  156.1 0.7 copy-done.1
  156.8 15.4 %finish.1 = bf16[2,768,512]{2,1,0:T(8,128)(2,1)} custom-call(s32[2]{0:T(128)} %len_ref.3, s32[1]{0:T(128)} %bitcast.pos_ref, bf16[2,768,1024]{2,1,0:T(8,128)(2,1)} %local_response.1.y_ref, bf16[2,768,1152]{2,1,0:T(8,128)(2,1)} %get-tuple-element.23.xbc_ref.coef_ref, bf16[2,768,1024]{2,1,0:T(8,128)(2,1)} %get-tuple-element.26.gate_ref, ...), custom_call_target="tpu_custom_call" | custom-call | tf_op jit(solution)/shard_map/finish/pallas_call | solution.py:516
Async XLA Ops:
  36.9 46.5 %all-to-all-start.1 = ((bf16[128,24,512]{2,1,0:T(8,128)(2,1)}), bf16[128,24,512]{2,1,0:T(8,128)(2,1)S(1)}, u32[]{:S(2)}, u32[]{:S(2)}) async-start(bf16[128,24,512]{2,1,0:T(8,128)(2,1)} %bitcast.9), calls=%async_computation.1 | async-start | bytes 6291456 | tf_op jit(solution)/shard_map/all_to_all | solution.py:546
  83.4 1.6 copy-start
  85.1 15.5 %copy-start.3 = (f32[1152]{0:T(1024)S(1)}, f32[1152]{0:T(1024)}, u32[]{:S(2)}) copy-start(f32[1152]{0:T(1024)} %param.21) | copy-start | bytes 13828
  85.1 16.1 %copy-start.4 = (f32[2,768]{1,0:T(2,128)S(1)}, f32[2,768]{1,0:T(2,128)}, u32[]{:S(2)}) copy-start(f32[2,768]{1,0:T(2,128)} %param.16) | copy-start | bytes 18436
  85.1 16.7 %copy-start.5 = (f32[16]{0:T(128)S(1)}, f32[16]{0:T(128)}, u32[]{:S(2)}) copy-start(f32[16]{0:T(128)} %param.22) | copy-start | bytes 196
  85.1 17.4 %copy-start.6 = (f32[16]{0:T(128)S(1)}, f32[16]{0:T(128)}, u32[]{:S(2)}) copy-start(f32[16]{0:T(128)} %param.23) | copy-start | bytes 196
  98.4 4.7 %collective-permute-start = (bf16[2,8,1152]{2,1,0:T(8,128)(2,1)}, bf16[2,8,1152]{2,1,0:T(8,128)(2,1)S(1)}, u32[]{:S(2)}, u32[]{:S(2)}) collective-permute-start(bf16[2,8,1152]{2,1,0:T(8,128)(2,1)} %get-tuple-element.21), channel_id=1, source_target_pairs={{0,8},{8,16},{16,24},{24,32},{32,40},{40,48},{48,56},{56,64},{64,7... | collective-permute-start | bytes 110600 | tf_op jit(solution)/shard_map/ppermute | solution.py:584
  103.1 0.6 copy-start.2
  140.3 15.9 %all-to-all-start.3 = ((bf16[16,64,128]{2,1,0:T(8,128)(2,1)}), bf16[16,64,128]{2,1,0:T(8,128)(2,1)S(1)}, u32[]{:S(2)}, u32[]{:S(2)}) async-start(bf16[16,64,128]{2,1,0:T(8,128)(2,1)} %scan_spans.1), calls=%async_computation.3 | async-start | bytes 524288 | tf_op jit(solution)/shard_map/all_to_all | solution.py:546
  156.1 0.7 copy-start.1
where the time goes:
time: 174 us; the launch traced here: 172 us
  Pallas kernels  77.8 us (45%)
  waiting for transfers between devices  37.4 us (21%)
  blocking collectives  35.3 us (20%)
  local copies, waits for them, and re-layouts  11 us (6%)
  starting transfers between devices  10.7 us (6%)
    all_to_all x2, waiting for transfers between devices, exchange(): return lax.all_to_all(values, axes, split_axis=0, concat_axis=0, tiled=True)  37.4 us
    all_to_all x2, blocking collectives, exchange(): return lax.all_to_all(values, axes, split_axis=0, concat_axis=0, tiled=True)  35.3 us
    pallas_call x1, Pallas kernels, chunk_states(): pl.pallas_call(states_kernel, out_shape=(jax.ShapeDtypeStruct((users, eve...  20.3 us
    pallas_call x1, Pallas kernels, finish(): pl.pallas_call(finish_kernel, out_shape=jax.ShapeDtypeStruct((users, even...  15.4 us
    pallas_call x1, Pallas kernels, project(): pl.pallas_call(functools.partial(project_kernel, inner=inner), out_shape=...  13.3 us
    pallas_call x1, Pallas kernels, fetch(): pl.pallas_call(functools.partial(fetch_kernel, slots=slots), out_shape=ja...  12.3 us
    pallas_call x1, Pallas kernels, local_response(): pl.pallas_call(local_kernel, out_shape=jax.ShapeDtypeStruct((users, event...  12.2 us
    all_to_all x2, starting transfers between devices, exchange(): return lax.all_to_all(values, axes, split_axis=0, concat_axis=0, tiled=True)  8.52 us
  transfers between devices with their start and end apart: 3, of which 1 were waited for; matrix products, arithmetic and copies ran while one was open for 4% of the time, Pallas kernels for 7%

commit v1 on v0

v1 whole, which is shorter than its diff:
```python
import functools

import jax
import jax.numpy as jnp
from jax import lax
from jax.experimental import pallas as pl
from jax.experimental.pallas import tpu as pltpu
from jax.sharding import PartitionSpec as P

F32 = jnp.float32
BF16 = jnp.bfloat16
EPS = 1e-05
LANES = 128
CHUNK = 128
TABLE_STEP = 512
FINISH_ROWS = 256
VMEM_LIMIT = 16 * 1024 * 1024


def params(axes):
    return pltpu.CompilerParams(
        dimension_semantics=("arbitrary",) * axes, vmem_limit_bytes=VMEM_LIMIT
    )


ON_CHIP = pl.BlockSpec(memory_space=pltpu.VMEM)
SCALARS = pl.BlockSpec(memory_space=pltpu.SMEM)


def near(array):
    return pltpu.with_memory_space_constraint(array, pltpu.VMEM)


def iota(shape, axis):
    return lax.broadcasted_iota(jnp.int32, shape, axis)


def nt(a, b):
    return lax.dot_general(a, b, (((1,), (1,)), ((), ())), preferred_element_type=F32)


def mm(a, b):
    return jnp.dot(a, b, preferred_element_type=F32)


def silu(v):
    half = 0.5 * v
    return half + half * jnp.tanh(half)


def route_kernel(owner_ref, row_ref, req_ref, place_ref, *, devices, cap, width):
    users, events = row_ref.shape
    tri = jnp.where(
        (iota((LANES, 2 * LANES), 0) < iota((LANES, 2 * LANES), 1))
        | (iota((LANES, 2 * LANES), 1) >= LANES),
        1.0,
        0.0,
    ).astype(BF16)
    slots = users * cap
    req = jnp.zeros((devices, width), F32)
    for u in range(users):
        running = jnp.zeros((devices, LANES), F32)
        for c in range(events // LANES):
            own = owner_ref[u, :, c * LANES : (c + 1) * LANES]
            row = row_ref[u : u + 1, c * LANES : (c + 1) * LANES]
            hot = iota((devices, LANES), 0) == own
            hot_b = jnp.where(hot, 1.0, 0.0).astype(BF16)
            counts = mm(hot_b, tri)
            rank = counts[:, :LANES] + running
            running = running + counts[:, LANES:]
            slot = jnp.sum(jnp.where(hot, rank, 0.0), axis=0, keepdims=True).astype(jnp.int32)
            slot = slot + u * cap
            match = iota((width, LANES), 0) == slot
            high = jnp.where(match, (row >> 6).astype(F32), 0.0).astype(BF16)
            low = jnp.where(match, (row & 63).astype(F32), 0.0).astype(BF16)
            req = req + 64.0 * nt(hot_b, high) + nt(hot_b, low)
            place = (own * (slots * 2 // 3) + slot - u * (slots // 3)).astype(F32)
            place_ref[u, c * LANES : (c + 1) * LANES, :] = jnp.broadcast_to(
                place, (LANES, LANES)
            ).T.astype(jnp.int32)
    req_ref[:, 0, :] = req.astype(jnp.int32)


def route(owners, rows, devices, cap, width):
    users, events = rows.shape
    return pl.pallas_call(
        functools.partial(route_kernel, devices=devices, cap=cap, width=width),
        out_shape=(
            jax.ShapeDtypeStruct((devices, 1, width), jnp.int32),
            pltpu.VMEM((users, events, LANES), jnp.int32),
        ),
        out_specs=(ON_CHIP, ON_CHIP),
        compiler_params=params(0),
        name="route",
    )(owners, rows)


def spread_kernel(tab_ref, out_ref):
    i = pl.program_id(0)
    step, dim = tab_ref.shape
    tiles = dim // LANES
    for cb in range(tiles):
        out_ref[pl.ds(i * step * tiles + cb, step, stride=tiles), :] = tab_ref[
            :, cb * LANES : (cb + 1) * LANES
        ].astype(F32)


def spread(table):
    items, dim = table.shape
    return pl.pallas_call(
        spread_kernel,
        out_shape=pltpu.VMEM((items * (dim // LANES), LANES), F32),
        grid=(items // TABLE_STEP,),
        in_specs=[pl.BlockSpec((TABLE_STEP, dim), lambda i: (i, 0))],
        out_specs=ON_CHIP,
        compiler_params=params(1),
        name="spread",
    )(table)


def fetch_kernel(idx_ref, tab_ref, out_ref, rows_ref, *, slots):
    owners = idx_ref.shape[0]
    tiles = out_ref.shape[1] // LANES

    def body(o, carry):
        base = pl.multiple_of(o * slots * tiles, 8)
        for s in range(slots):
            r = idx_ref[o, 0, s]
            rows_ref[pl.ds(base + tiles * s, tiles), :] = tab_ref[
                pl.ds(pl.multiple_of(r * tiles, tiles), tiles), :
            ]
        return carry

    lax.fori_loop(0, owners, body, 0)

    def pack(g, carry):
        for part in range(4):
            for cb in range(tiles):
                start = (g * 4 + part) * 16 * tiles + cb
                out_ref[
                    pl.ds(pl.multiple_of((g * 4 + part) * 16, 16), 16),
                    cb * LANES : (cb + 1) * LANES,
                ] = rows_ref[pl.ds(start, 16, stride=tiles), :].astype(BF16)
        return carry

    lax.fori_loop(0, owners * slots // 64, pack, 0)


def fetch(idx, table, slots, dim):
    owners = idx.shape[0]
    return pl.pallas_call(
        functools.partial(fetch_kernel, slots=slots),
        out_shape=jax.ShapeDtypeStruct((owners * slots, dim), BF16),
        in_specs=[SCALARS, ON_CHIP],
        scratch_shapes=[pltpu.VMEM((owners * slots * (dim // LANES), LANES), F32)],
        compiler_params=params(0),
        name="fetch",
    )(idx, near(table))


def choose_kernel(place_ref, out_ref):
    users, events, _ = place_ref.shape
    width = out_ref.shape[1]
    rows = LANES

    def body(i, carry):
        at = pl.ds(pl.multiple_of(i * rows, rows), rows)
        for u in range(users):
            place = place_ref[u, at, :]
            to = pl.ds(pl.multiple_of(u * events + i * rows, rows), rows)
            for k in range(width // LANES):
                out_ref[to, k * LANES : (k + 1) * LANES] = jnp.where(
                    place == iota((rows, LANES), 1) + k * LANES, 1.0, 0.0
                ).astype(BF16)
        return carry

    lax.fori_loop(0, events // rows, body, 0)


def choose(place, width):
    users, events, _ = place.shape
    return pl.pallas_call(
        choose_kernel,
        out_shape=pltpu.VMEM((users * events, width), BF16),
        in_specs=[ON_CHIP],
        out_specs=ON_CHIP,
        compiler_params=params(0),
        name="choose",
    )(near(place))


def project_kernel(
    got_ref, hot_ref, gain_ref, w_ref, x_ref, normed_ref, conv_ref, step_ref, tail_ref, *, inner
):
    owners, slots, dim = got_ref.shape
    users, events, conv_dim = conv_ref.shape
    heads = step_ref.shape[1]
    window = slots * 2 // 3
    for u in range(users):
        shift = u * (slots // 3)
        got = got_ref[:, shift : shift + window, :].reshape(owners * window, dim)
        x = mm(hot_ref[u * events : (u + 1) * events, :], got)
        x_ref[u] = x.astype(BF16)
        normed = x * lax.rsqrt(jnp.mean(x * x, axis=-1, keepdims=True) + EPS) * gain_ref[...]
        normed = normed.astype(BF16)
        normed_ref[u] = normed
        conv = mm(normed, w_ref[:, inner : inner + conv_dim]).astype(BF16)
        conv_ref[u] = conv
        tail_ref[u] = conv[events - 8 :, :]
        raw = mm(normed, w_ref[:, inner + conv_dim : inner + conv_dim + heads])
        step_ref[u] = raw.astype(BF16).astype(F32).T


def project(got, hot, gain, weight, inner, conv_dim, heads, users):
    events = hot.shape[0] // users
    dim = got.shape[2]
    return pl.pallas_call(
        functools.partial(project_kernel, inner=inner),
        out_shape=(
            pltpu.VMEM((users, events, dim), BF16),
            pltpu.VMEM((users, events, dim), BF16),
            pltpu.VMEM((users, events, conv_dim), BF16),
            pltpu.VMEM((users, heads, events), F32),
            jax.ShapeDtypeStruct((users, 8, conv_dim), BF16),
        ),
        in_specs=[ON_CHIP] * 4,
        out_specs=(ON_CHIP,) * 5,
        compiler_params=params(0),
        name="project",
    )(near(got), near(hot), gain, near(weight))


def lane_halves(rows_a, rows_b):
    return jnp.where(iota(rows_a.shape, rows_a.ndim - 1) < LANES // 2, rows_a, rows_b)


def running_sums(values):
    lane = iota(values.shape, 1)
    size = values.shape[1]
    ahead, back = values, values
    k = 1
    while k < size:
        ahead = ahead + jnp.where(lane >= k, pltpu.roll(ahead, k, 1), 0.0)
        back = back + jnp.where(lane < size - k, pltpu.roll(back, size - k, 1), 0.0)
        k *= 2
    return ahead, back


def pair_rhs(pair):
    low = iota(pair.shape, 1) < LANES // 2
    zero = jnp.zeros_like(pair)
    return jnp.concatenate([jnp.where(low, pair, zero), jnp.where(low, zero, pair)], axis=0)


def column(row):
    size = row.shape[1]
    return jnp.sum(
        jnp.where(iota((size, size), 0) == iota((size, size), 1), row, 0.0), axis=1, keepdims=True
    )


def states_kernel(
    len_ref,
    pos_ref,
    conv_ref,
    edge_ref,
    step_ref,
    gap_ref,
    cw_ref,
    cb_ref,
    dt_ref,
    rate_ref,
    xbc_ref,
    cum_ref,
    steps_ref,
    hold_ref,
    decay_ref,
    end_ref,
    prev,
    moves,
    weights,
    totals,
    state,
    pref,
):
    users, events, conv_dim = conv_ref.shape
    heads = step_ref.shape[1]
    chunks = events // CHUNK
    pairs = heads // 2
    inner = pairs * LANES
    n_state = state.shape[1]
    half = LANES // 2

    dt = column(dt_ref[...])
    rate = column(rate_ref[...])
    steps_all, decay_all = [], []
    for c in range(chunks):
        lanes = slice(c * CHUNK, (c + 1) * CHUNK)
        for u in range(users):
            position = pos_ref[0] + c * CHUNK + iota((heads, CHUNK), 1)
            alive = jnp.where(position < len_ref[u], 1.0, 0.0)
            raw = step_ref[u, :, lanes] + dt
            steps = alive * (jnp.maximum(raw, 0.0) + jnp.log1p(jnp.exp(-jnp.abs(raw))))
            steps_all.append(steps)
            decay_all.append(-rate * gap_ref[u : u + 1, lanes] * steps)
    steps = jnp.concatenate(steps_all, axis=0)
    ahead, back = running_sums(jnp.concatenate(decay_all, axis=0))
    after = jnp.where(iota(back.shape, 1) < CHUNK - 1, pltpu.roll(back, CHUNK - 1, 1), 0.0)
    cum_ref[...] = ahead
    steps_ref[...] = steps
    weights[...] = jnp.exp(after) * steps
    totals[...] = jnp.broadcast_to(back[:, 0:1], totals.shape)

    state[...] = jnp.zeros_like(state)
    pref[...] = jnp.zeros_like(pref)
    prev[:, 0:8, :] = jnp.zeros((users, 8, conv_dim), BF16)
    prev[:, 8:16, :] = edge_ref[...]
    for k in range(3):
        source = iota((CHUNK, CHUNK + 16), 0) - (3 - k)
        source = jnp.where(source < 0, source + CHUNK + 16, source)
        moves[k] = jnp.where(source == iota((CHUNK, CHUNK + 16), 1), 1.0, 0.0).astype(BF16)

    def chunk(c, carry):
        for u in range(users):
            time = pl.ds(pl.multiple_of(c * CHUNK, CHUNK), CHUNK)
            at = 0
            while at < conv_dim:
                width = min(2 * LANES, conv_dim - at)
                cols = slice(at, at + width)
                here = conv_ref[u, time, cols]
                both = jnp.concatenate([here, prev[u, :, cols]], axis=0)
                prev[u, :, cols] = here[CHUNK - 16 :, :]
                total = cb_ref[:, cols] + cw_ref[3:4, cols] * here.astype(F32)
                for k in range(3):
                    total = total + cw_ref[k : k + 1, cols] * mm(moves[k], both)
                xbc_ref[u, time, cols] = silu(total).astype(BF16)
                at += width
            decay_ref[u, c] = jnp.exp(pref[u])
            hold_ref[u, c] = state[u].astype(BF16)
            coef_t = xbc_ref[u, time, inner : inner + LANES].astype(F32).T[:n_state, :]
            first = pl.multiple_of((c * users + u) * heads, heads)
            weight = weights[pl.ds(first, heads), :]
            total = totals[pl.ds(first, heads), :]
            for j in range(pairs):
                lanes = slice(j * LANES, (j + 1) * LANES)
                a, b = 2 * j, 2 * j + 1
                left = jnp.concatenate(
                    [coef_t * weight[a : a + 1, :], coef_t * weight[b : b + 1, :]], axis=1
                ).astype(BF16)
                add = mm(left, pair_rhs(xbc_ref[u, time, lanes]))
                tot = lane_halves(total[a : a + 1, :], total[b : b + 1, :])
                state[u, :, lanes] = jnp.exp(tot) * state[u, :, lanes] + add
                pref[u, :, lanes] = pref[u, :, lanes] + tot
        return carry

    lax.fori_loop(0, chunks, chunk, 0)

    for h in range(heads):
        lanes = slice((h // 2) * LANES, (h // 2 + 1) * LANES)
        parts = []
        for u in range(users):
            value = state[u, :, lanes]
            low = jnp.broadcast_to(pref[u, :, lanes], (8, LANES))
            if h % 2 != u:
                value = pltpu.roll(value, half, 1)
                low = pltpu.roll(low, half, 1)
            high = low.astype(BF16).astype(F32)
            row = iota((8, LANES), 0)
            extra = jnp.where(row == 0, high, jnp.where(row == 1, low - high, 0.0))
            parts.append(jnp.concatenate([value, extra], axis=0))
        end_ref[h] = lane_halves(*parts).astype(BF16)


def chunk_states(lens, pos, conv, edge, step, gap, cw, cb, dt, rate, n_state):
    users, events, conv_dim = conv.shape
    heads = step.shape[1]
    inner = conv_dim - 2 * n_state
    chunks = events // CHUNK
    lines = chunks * users * heads
    return pl.pallas_call(
        states_kernel,
        out_shape=(
            pltpu.VMEM((users, events, conv_dim), BF16),
            pltpu.VMEM((lines, CHUNK), F32),
            pltpu.VMEM((lines, CHUNK), F32),
            pltpu.VMEM((users, chunks, n_state, inner), BF16),
            pltpu.VMEM((users, chunks, 1, inner), F32),
            jax.ShapeDtypeStruct((heads, n_state + 8, LANES), BF16),
        ),
        in_specs=[SCALARS] * 2 + [ON_CHIP] * 8,
        out_specs=(ON_CHIP,) * 6,
        scratch_shapes=[
            pltpu.VMEM((users, 16, conv_dim), BF16),
            pltpu.VMEM((3, CHUNK, CHUNK + 16), BF16),
            pltpu.VMEM((lines, CHUNK), F32),
            pltpu.VMEM((lines, LANES), F32),
            pltpu.VMEM((users, n_state, inner), F32),
            pltpu.VMEM((users, 1, inner), F32),
        ],
        compiler_params=params(0),
        name="chunk_states",
    )(lens, pos, near(conv), near(edge), near(step), gap, cw, cb, dt, rate)


def scan_kernel(in_ref, out_ref):
    spans, rows, lanes = in_ref.shape
    n_state = rows - 8
    running = jnp.zeros((n_state, lanes), F32)
    for k in range(spans):
        out_ref[k] = running.astype(BF16)
        block = in_ref[k].astype(F32)
        log_decay = block[n_state : n_state + 1, :] + block[n_state + 1 : n_state + 2, :]
        running = jnp.exp(log_decay) * running + block[:n_state, :]


def scan_spans(ends):
    spans, rows, lanes = ends.shape
    return pl.pallas_call(
        scan_kernel,
        out_shape=jax.ShapeDtypeStruct((spans, rows - 8, lanes), BF16),
        in_specs=[ON_CHIP],
        out_specs=ON_CHIP,
        compiler_params=params(0),
        name="scan_spans",
    )(near(ends))


def local_kernel(normed_ref, w_ref, xbc_ref, cum_ref, steps_ref, y_ref, fade_ref, gates, *, user):
    events, inner = y_ref.shape
    users = xbc_ref.shape[0]
    chunks = events // CHUNK
    heads = cum_ref.shape[0] // (users * chunks)
    pairs = heads // 2
    half = LANES // 2

    def chunk(c, carry):
        time = pl.ds(pl.multiple_of(c * CHUNK, CHUNK), CHUNK)
        gates[...] = silu(mm(normed_ref[user, time, :], w_ref[:, :inner]).astype(BF16).astype(F32))
        coef = xbc_ref[user, time, inner : inner + LANES]
        scores = nt(coef[:, half:], coef[:, :half])
        causal = iota((CHUNK, CHUNK), 0) >= iota((CHUNK, CHUNK), 1)
        scores = jnp.where(causal, scores, 0.0)
        first = pl.multiple_of((c * users + user) * heads, heads)
        cum = cum_ref[pl.ds(first, heads), :]
        steps = steps_ref[pl.ds(first, heads), :]
        cum_t = jnp.concatenate([cum, jnp.zeros((LANES - heads, CHUNK), F32)], axis=0).T

        def mixing(h):
            own = jnp.broadcast_to(cum_t[:, h : h + 1], (CHUNK, CHUNK))
            fading = jnp.exp(jnp.minimum(own - cum[h : h + 1, :], 0.0))
            return own, (scores * fading * steps[h : h + 1, :]).astype(BF16)

        for j in range(pairs):
            lanes = slice(j * LANES, (j + 1) * LANES)
            own_a, mix_a = mixing(2 * j)
            own_b, mix_b = mixing(2 * j + 1)
            left = jnp.concatenate([mix_a, mix_b], axis=1)
            gate = gates[:, lanes]
            y_ref[time, lanes] = gate * mm(left, pair_rhs(xbc_ref[user, time, lanes]))
            fade_ref[time, lanes] = gate * jnp.exp(lane_halves(own_a, own_b))
        return carry

    lax.fori_loop(0, chunks, chunk, 0)


def local_response(normed, weight, xbc, cum, steps, inner, user):
    events = xbc.shape[1]
    return pl.pallas_call(
        functools.partial(local_kernel, user=user),
        out_shape=(pltpu.VMEM((events, inner), F32), pltpu.VMEM((events, inner), F32)),
        in_specs=[ON_CHIP] * 5,
        out_specs=(ON_CHIP, ON_CHIP),
        scratch_shapes=[pltpu.VMEM((CHUNK, inner), F32)],
        compiler_params=params(0),
        name="local_response",
    )(near(normed), near(weight), near(xbc), near(cum), near(steps))


def finish_kernel(
    len_ref,
    pos_ref,
    y0_ref,
    y1_ref,
    fade0_ref,
    fade1_ref,
    xbc_ref,
    x_ref,
    hold_ref,
    decay_ref,
    hin_ref,
    gain_ref,
    w_ref,
    out_ref,
    incoming,
    same,
    normed,
):
    u = pl.program_id(0)
    b = pl.program_id(1)
    heads = hin_ref.shape[0]
    pairs = heads // 2
    inner = pairs * LANES
    half = LANES // 2
    size = 2 * LANES
    rows = out_ref.shape[1]

    @pl.when((u == 0) & (b == 0))
    def _():
        same[...] = jnp.where(
            iota((size, size), 0) // half == iota((size, size), 1) // half, 1.0 / half, 0.0
        ).astype(BF16)
        for j in range(pairs):
            a = hin_ref[2 * j].astype(F32)
            b = hin_ref[2 * j + 1].astype(F32)
            lanes = slice(j * LANES, (j + 1) * LANES)
            incoming[0, :, lanes] = lane_halves(a, pltpu.roll(b, half, 1))
            incoming[1, :, lanes] = lane_halves(pltpu.roll(a, half, 1), b)

    def work(y_ref, fade_ref):
        for part in range(rows // CHUNK):
            c = b * (rows // CHUNK) + part
            time = pl.ds(pl.multiple_of(c * CHUNK, CHUNK), CHUNK)
            here = slice(part * CHUNK, (part + 1) * CHUNK)
            held = (hold_ref[u, c].astype(F32) + decay_ref[u, c] * incoming[u]).astype(BF16)
            coef = xbc_ref[u, time, inner : inner + LANES][:, half:]
            for j in range(pairs // 2):
                lanes = slice(j * size, (j + 1) * size)
                carried = mm(coef, held[:, lanes])
                gated = y_ref[time, lanes] + fade_ref[time, lanes] * carried
                mean = mm((gated * gated).astype(BF16), same[...])
                normed[here, lanes] = (
                    gated * lax.rsqrt(mean + EPS) * gain_ref[:, lanes]
                ).astype(BF16)
        mixed = mm(normed[...], w_ref[...])
        position = pos_ref[0] + b * rows + iota((rows, 1), 0)
        alive = jnp.where(position < len_ref[u], 1.0, 0.0)
        span = pl.ds(pl.multiple_of(b * rows, rows), rows)
        out_ref[0] = (alive * (x_ref[u, span, :].astype(F32) + mixed)).astype(BF16)

    pl.when(u == 0)(functools.partial(work, y0_ref, fade0_ref))
    pl.when(u == 1)(functools.partial(work, y1_ref, fade1_ref))


def finish(lens, pos, ys, fades, xbc, x, hold, decay, hin, gain, weight):
    events, inner = ys[0].shape
    n_state = hold.shape[2]
    users, _, dim = x.shape
    size = 2 * LANES
    return pl.pallas_call(
        finish_kernel,
        out_shape=jax.ShapeDtypeStruct((users, events, dim), BF16),
        grid=(users, events // FINISH_ROWS),
        in_specs=[SCALARS] * 2 + [ON_CHIP] * 11,
        out_specs=pl.BlockSpec((1, FINISH_ROWS, dim), lambda u, b: (u, b, 0)),
        scratch_shapes=[
            pltpu.VMEM((users, n_state, inner), F32),
            pltpu.VMEM((size, size), BF16),
            pltpu.VMEM((FINISH_ROWS, inner), BF16),
        ],
        compiler_params=params(2),
        name="finish",
    )(
        lens,
        pos,
        *[near(v) for v in (*ys, *fades, xbc, x, hold, decay, hin, gain, weight)],
    )


def exchange(values, axes):
    return lax.all_to_all(values, axes, split_axis=0, concat_axis=0, tiled=True)


def per_device(
    item_owner,
    item_row,
    history_len,
    event_gap,
    item_table,
    norm_gain,
    in_weight,
    conv_weight,
    conv_bias,
    dt_bias,
    decay_rate,
    out_gain,
    emitted_projection,
):
    users, events = item_row.shape
    dim = item_table.shape[1]
    heads = dt_bias.shape[0]
    inner = emitted_projection.shape[0]
    conv_dim = conv_weight.shape[1]
    n_state = (conv_dim - inner) // 2
    times = lax.axis_size("tm")
    devices = times * lax.axis_size("table")
    cap = 2 * events // devices
    slots = users * cap
    everyone = ("tm", "table")
    pos = (lax.axis_index("tm") * events).reshape(1).astype(jnp.int32)

    requests, place = route(jnp.swapaxes(item_owner, 1, 2), item_row, devices, cap, 32)
    asked = exchange(requests, everyone)
    rows = fetch(asked, spread(item_table), slots, dim)
    got = exchange(rows.reshape(devices, slots, dim), everyone)
    hot = choose(place, devices * (slots * 2 // 3))
    x, normed, conv, step, tail = project(
        got, hot, norm_gain[None, :], in_weight, inner, conv_dim, heads, users
    )
    edge = lax.ppermute(tail, "tm", [(i, i + 1) for i in range(times - 1)])
    xbc, cum, steps, hold, decay, ends = chunk_states(
        history_len,
        pos,
        conv,
        edge,
        step,
        event_gap,
        conv_weight,
        conv_bias[None, :],
        dt_bias[None, :],
        decay_rate[None, :],
        n_state,
    )
    by_head = exchange(ends, "tm")
    ys, fades = zip(
        *[local_response(normed, in_weight, xbc, cum, steps, inner, u) for u in range(users)]
    )
    hin = exchange(scan_spans(by_head), "tm")
    return finish(
        history_len,
        pos,
        ys,
        fades,
        xbc,
        x,
        hold,
        decay,
        hin,
        out_gain[None, :],
        emitted_projection,
    )


def solution(mesh):
    in_specs = (
        P("table", "tm", None),
        P("table", "tm"),
        P("table"),
        P("table", "tm"),
        P(("tm", "table"), None),
        P(),
        P(),
        P(),
        P(),
        P(),
        P(),
        P(),
        P(),
    )
    out_specs = P("table", "tm", None)
    return jax.shard_map(
        per_device, mesh=mesh, in_specs=in_specs, out_specs=out_specs, check_vma=False
    )
```

time: 174 us -> 178 us (1.023)
  local copies, waits for them, and re-layouts: 11 us -> 51.2 us
  Pallas kernels: 77.8 us -> 47.9 us
  blocking collectives: 35.3 us -> 14.9 us
  starting transfers between devices: 10.7 us -> 24.6 us
    unnamed x16 -> x71, local copies, waits for them, and re-layouts: 8.47 us -> 51.2 us
    all_to_all x2 -> x1, blocking collectives: 35.3 us -> 14.9 us  [exchange(): return lax.all_to_all(values, axes, split_axis=0, concat_axis=0, tiled=True)]
    all_to_all x2 -> x3, starting transfers between devices: 8.52 us -> 22.5 us  [exchange(): return lax.all_to_all(values, axes, split_axis=0, concat_axis=0, tiled=True)]
    pallas_call x2 -> x5, Pallas kernels: 32.5 us -> 22.1 us  [the longest x2 10 us: local_response(): pl.pallas_call(functools.partial(local_kernel, user=user), out_shape=(plt...]
    pallas_call x1, Pallas kernels: 15.4 us -> 7.36 us  [finish(): pl.pallas_call(finish_kernel, out_shape=jax.ShapeDtypeStruct((users, even...]
    pallas_call x1, Pallas kernels: 13.3 us -> 7.97 us  [project(): pl.pallas_call(functools.partial(project_kernel, inner=inner), out_shape=...]
    pallas_call x1, Pallas kernels: 12.3 us -> 7.99 us  [fetch(): pl.pallas_call(functools.partial(fetch_kernel, slots=slots), out_shape=ja...]
    broadcast_in_dim x3 -> x0, local copies, waits for them, and re-layouts: 1.95 us -> none  [the longest x1 0.67 us: per_device(): dt_bias[:, None]]
  transfers between devices with their start and end apart: 3 -> 4, of which waited for: 1 -> 3; matrix products, arithmetic and copies ran while one was open for 4% -> 2% of each run, Pallas kernels for 7% -> 7%
where the time goes in v1:
time: 178 us; the launch traced here: 177 us
  local copies, waits for them, and re-layouts  51.2 us (29%)
  Pallas kernels  47.9 us (27%)
  waiting for transfers between devices  38.3 us (22%)
  starting transfers between devices  24.6 us (14%)
  blocking collectives  14.9 us (8%)
    unnamed x71, local copies, waits for them, and re-layouts  51.2 us
    all_to_all x3, waiting for transfers between devices, exchange(): return lax.all_to_all(values, axes, split_axis=0, concat_axis=0, tiled=True)  36.7 us
    all_to_all x3, starting transfers between devices, exchange(): return lax.all_to_all(values, axes, split_axis=0, concat_axis=0, tiled=True)  22.5 us
    all_to_all x1, blocking collectives, exchange(): return lax.all_to_all(values, axes, split_axis=0, concat_axis=0, tiled=True)  14.9 us
    pallas_call x2, Pallas kernels, local_response(): pl.pallas_call(functools.partial(local_kernel, user=user), out_shape=(plt...  10 us
    pallas_call x1, Pallas kernels, chunk_states(): pl.pallas_call(states_kernel, out_shape=(pltpu.VMEM((users, events, conv_...  9.38 us
    pallas_call x1, Pallas kernels, fetch(): pl.pallas_call(functools.partial(fetch_kernel, slots=slots), out_shape=ja...  7.99 us
    pallas_call x1, Pallas kernels, project(): pl.pallas_call(functools.partial(project_kernel, inner=inner), out_shape=...  7.97 us
  transfers between devices with their start and end apart: 4, of which 3 were waited for; matrix products, arithmetic and copies ran while one was open for 2% of the time, Pallas kernels for 7%

profile of v1, /device:TPU:0, one launch (start us, length us, event | category | flops | bytes accessed | tf_op | source)
XLA Modules:
  0.0 177.2 jit_solution(2323674411944122704)
XLA Ops:
  0.0 0.7 copy-done.27
  0.7 0.7 copy-done.28
  1.4 1.7 route.1
  3.1 11.1 %all-to-all-start = ((s32[128,1,32]{2,1,0:T(1,128)}), s32[128,1,32]{2,1,0:T(1,128)S(1)}, u32[]{:S(2)}, u32[]{:S(2)}) async-start(s32[128,1,32]{2,1,0:T(1,128)} %get-tuple-element.22), calls=%async_computation | async-start | bytes 131072 | tf_op jit(solution)/shard_map/all_to_all | solution.py:570
  14.2 0.0 copy-start.9
  14.2 2.2 %copy-done.9 = bf16[4096,512]{1,0:T(8,128)(2,1)S(1)} copy-done((bf16[4096,512]{1,0:T(8,128)(2,1)S(1)}, bf16[4096,512]{1,0:T(8,128)(2,1)}, u32[]{:S(2)}) %copy-start.9) | copy-done | bytes 4194328
  16.4 1.1 spread.1.tab_ref
  17.5 0.0 copy-start
  17.5 3.3 %copy-done = f32[16384,128]{1,0:T(8,128)} copy-done((f32[16384,128]{1,0:T(8,128)}, f32[16384,128]{1,0:T(8,128)S(1)}, u32[]{:S(2)}) %copy-start) | copy-done | bytes 8388632
  20.8 2.6 %all-to-all-done.idx_ref = s32[128,1,32]{2,1,0:T(1,128)S(1)} async-done(((s32[128,1,32]{2,1,0:T(1,128)}), s32[128,1,32]{2,1,0:T(1,128)S(1)}, u32[]{:S(2)}, u32[]{:S(2)}) %all-to-all-start) | async-done | bytes 16416 | tf_op jit(solution)/shard_map/all_to_all | solution.py:570
  23.4 3.4 %copy-done.1 = f32[16384,128]{1,0:T(8,128)S(1)} copy-done((f32[16384,128]{1,0:T(8,128)S(1)}, f32[16384,128]{1,0:T(8,128)}, u32[]{:S(2)}) %copy-start.1) | copy-done | bytes 8388632
  26.8 8.0 %fetch.1 = bf16[3072,512]{1,0:T(8,128)(2,1)} custom-call(s32[128,1,32]{2,1,0:T(1,128)S(1)} %all-to-all-done.idx_ref, f32[16384,128]{1,0:T(8,128)S(1)} %copy-done.1), custom_call_target="tpu_custom_call" | custom-call | tf_op jit(solution)/shard_map/fetch/pallas_call | solution.py:151
  34.8 7.6 %all-to-all-start.1 = ((bf16[128,24,512]{2,1,0:T(8,128)(2,1)}), bf16[128,24,512]{2,1,0:T(8,128)(2,1)}, u32[]{:S(2)}, u32[]{:S(2)}) async-start(bf16[128,24,512]{2,1,0:T(8,128)(2,1)} %bitcast.2), calls=%async_computation.1 | async-start | bytes 6291456 | tf_op jit(solution)/shard_map/all_to_all | solution.py:570
  42.4 2.8 %copy.14.w_ref = bf16[512,2192]{1,0:T(8,128)(2,1)S(1)} copy(bf16[512,2192]{0,1:T(8,128)(2,1)} %param.19) | data formatting | bytes 4489216 | tf_op args[6]
  45.2 0.0 copy-start.30
  45.3 1.6 choose.1.hot_ref
  46.9 0.0 copy-start.5
  46.9 2.7 %copy-done.5 = bf16[1536,2048]{1,0:T(8,128)(2,1)} copy-done((bf16[1536,2048]{1,0:T(8,128)(2,1)}, bf16[1536,2048]{1,0:T(8,128)(2,1)S(1)}, u32[]{:S(2)}) %copy-start.5) | copy-done | bytes 6291480
  49.6 34.1 %all-to-all-done.1.got_ref = bf16[128,24,512]{2,1,0:T(8,128)(2,1)} async-done(((bf16[128,24,512]{2,1,0:T(8,128)(2,1)}), bf16[128,24,512]{2,1,0:T(8,128)(2,1)}, u32[]{:S(2)}, u32[]{:S(2)}) %all-to-all-start.1) | async-done | bytes 3145760 | tf_op jit(solution)/shard_map/all_to_all | solution.py:570
  83.7 0.0 copy-done.30
  83.7 2.8 %copy-done.6 = bf16[1536,2048]{1,0:T(8,128)(2,1)S(1)} copy-done((bf16[1536,2048]{1,0:T(8,128)(2,1)S(1)}, bf16[1536,2048]{1,0:T(8,128)(2,1)}, u32[]{:S(2)}) %copy-start.6) | copy-done | bytes 6291480
  86.5 0.0 copy-start.32
  86.5 0.0 copy-start.33
  86.5 8.0 %project.1 = (bf16[2,768,512]{2,1,0:T(8,128)(2,1)S(1)}, bf16[2,768,512]{2,1,0:T(8,128)(2,1)S(1)}, bf16[2,768,1152]{2,1,0:T(8,128)(2,1)S(1)}, f32[2,16,768]{2,1,0:T(8,128)S(1)}, bf16[2,8,1152]{2,1,0:T(8,128)(2,1)S(1)}) custom-call(bf16[128,24,512]{2,1,0:T(8,128)(2,1)} %all-to-all-done.1.got_ref, bf16[1536,2048]{1,0:T(8,128)(2,1)S(1)} %copy-done.6, ...), custom_call_target="tpu_custom_call" | custom-call | tf_op jit(solution)/shard_map/project/pallas_call | solution.py:217
  94.5 1.1 copy-done.7
  95.6 1.7 copy-done.10
  97.4 1.2 copy-done.20
  98.5 2.1 %collective-permute-start = (bf16[2,8,1152]{2,1,0:T(8,128)(2,1)S(1)}, bf16[2,8,1152]{2,1,0:T(8,128)(2,1)S(1)}, u32[]{:S(2)}, u32[]{:S(2)}) collective-permute-start(bf16[2,8,1152]{2,1,0:T(8,128)(2,1)S(1)} %get-tuple-element.26), channel_id=1, source_target_pairs={{0,8},{8,16},{16,24},{24,32},{32,40},{40,48},{48,56},{56,64},{64,7... | collective-permute-start | bytes 110600 | tf_op jit(solution)/shard_map/ppermute | solution.py:609
  100.7 0.0 copy-done.34
  100.7 1.6 collective-permute-done.edge_ref
  102.3 0.0 copy-done.25
  102.3 0.0 copy-done.26
  102.3 0.0 copy-done.31
  102.3 0.0 copy-done.32
  102.3 0.0 copy-done.33
  102.3 0.0 copy-start.11
  102.4 2.0 %copy-done.11 = bf16[2,768,1152]{2,1,0:T(8,128)(2,1)S(1)} copy-done((bf16[2,768,1152]{2,1,0:T(8,128)(2,1)S(1)}, bf16[2,768,1152]{2,1,0:T(8,128)(2,1)}, u32[]{:S(2)}) %copy-start.11) | copy-done | bytes 3538968
  104.3 9.4 %chunk_states.1 = (bf16[2,768,1152]{2,1,0:T(8,128)(2,1)S(1)}, f32[192,128]{1,0:T(8,128)S(1)}, f32[192,128]{1,0:T(8,128)S(1)}, bf16[2,6,64,1024]{3,2,1,0:T(8,128)...) custom-call(s32[2]{0:T(128)S(1)} %copy-done.31, s32[1]{0:T(128)} %bitcast.pos_ref, ...), custom_call_target="tpu_custom_call" | custom-call | tf_op jit(solution)/shard_map/chunk_states/pallas_call | solution.py:380
  113.7 0.0 copy-start.2
  113.8 1.7 copy-done.2
  115.5 1.2 copy-done.22
  116.7 14.9 %all_to_all.20.in_ref = bf16[16,72,128]{2,1,0:T(8,128)(2,1)S(1)} all-to-all(bf16[16,72,128]{2,1,0:T(8,128)(2,1)S(1)} %get-tuple-element.38), channel_id=1, replica_groups=mesh['tm'=16,'table'=8] {'tm'}, dimensions={0} | all-to-all | bytes 589824 | tf_op jit(solution)/shard_map/all_to_all | solution.py:570
  131.5 0.8 scan_spans.1
  132.3 3.7 %all-to-all-start.3 = ((bf16[16,64,128]{2,1,0:T(8,128)(2,1)}), bf16[16,64,128]{2,1,0:T(8,128)(2,1)S(1)}, u32[]{:S(2)}, u32[]{:S(2)}) async-start(bf16[16,64,128]{2,1,0:T(8,128)(2,1)} %scan_spans.1), calls=%async_computation.3 | async-start | bytes 524288 | tf_op jit(solution)/shard_map/all_to_all | solution.py:570
  136.0 0.0 copy-start.3
  136.0 2.0 %copy-done.3 = bf16[2,768,1152]{2,1,0:T(8,128)(2,1)S(1)} copy-done((bf16[2,768,1152]{2,1,0:T(8,128)(2,1)S(1)}, bf16[2,768,1152]{2,1,0:T(8,128)(2,1)}, u32[]{:S(2)}) %copy-start.3) | copy-done | bytes 3538968
  138.0 1.4 copy-done.8
  139.4 5.0 %local_response.3 = (f32[768,1024]{1,0:T(8,128)S(1)}, f32[768,1024]{1,0:T(8,128)S(1)}) custom-call(bf16[2,768,512]{2,1,0:T(8,128)(2,1)S(1)} %copy-done.8, bf16[512,2192]{1,0:T(8,128)(2,1)S(1)} %copy.14.w_ref, bf16[2,768,1152]{2,1,0:T(8,128)(2,1)S(1)} %copy-done.3, f32[192,128]{1,0:T(8,128)S(1)} %get-tuple-element.29.cum_ref, ...), custom_call_target="tpu_custom_call" | custom-call | tf_op jit(solution)/shard_map/local_response/pallas_call | solution.py:468
  144.5 1.7 copy-done.12
  146.2 1.6 copy-done.14
  147.8 5.0 %local_response.2 = (f32[768,1024]{1,0:T(8,128)S(1)}, f32[768,1024]{1,0:T(8,128)S(1)}) custom-call(bf16[2,768,512]{2,1,0:T(8,128)(2,1)S(1)} %copy-done.8, bf16[512,2192]{1,0:T(8,128)(2,1)S(1)} %copy.14.w_ref, bf16[2,768,1152]{2,1,0:T(8,128)(2,1)S(1)} %copy-done.3, f32[192,128]{1,0:T(8,128)S(1)} %get-tuple-element.29.cum_ref, ...), custom_call_target="tpu_custom_call" | custom-call | tf_op jit(solution)/shard_map/local_response/pallas_call | solution.py:468
  152.8 1.7 copy-done.16
  154.5 1.7 copy-done.18
  156.2 0.0 all-to-all-done.3.hin_ref
  156.2 0.0 copy-done.29
  156.2 2.0 %copy-done.4 = bf16[2,768,1152]{2,1,0:T(8,128)(2,1)S(1)} copy-done((bf16[2,768,1152]{2,1,0:T(8,128)(2,1)S(1)}, bf16[2,768,1152]{2,1,0:T(8,128)(2,1)}, u32[]{:S(2)}) %copy-start.4) | copy-done | bytes 3538968
  158.2 1.9 %copy-done.13 = f32[768,1024]{1,0:T(8,128)S(1)} copy-done((f32[768,1024]{1,0:T(8,128)S(1)}, f32[768,1024]{1,0:T(8,128)}, u32[]{:S(2)}) %copy-start.13) | copy-done | bytes 3145752
  160.1 1.9 %copy-done.15 = f32[768,1024]{1,0:T(8,128)S(1)} copy-done((f32[768,1024]{1,0:T(8,128)S(1)}, f32[768,1024]{1,0:T(8,128)}, u32[]{:S(2)}) %copy-start.15) | copy-done | bytes 3145752
  162.0 1.9 %copy-done.17 = f32[768,1024]{1,0:T(8,128)S(1)} copy-done((f32[768,1024]{1,0:T(8,128)S(1)}, f32[768,1024]{1,0:T(8,128)}, u32[]{:S(2)}) %copy-start.17) | copy-done | bytes 3145752
  163.9 1.9 %copy-done.19 = f32[768,1024]{1,0:T(8,128)S(1)} copy-done((f32[768,1024]{1,0:T(8,128)S(1)}, f32[768,1024]{1,0:T(8,128)}, u32[]{:S(2)}) %copy-start.19) | copy-done | bytes 3145752
  165.8 1.4 copy-done.21
  167.2 1.4 copy-done.23
  168.6 1.2 copy-done.24
  169.8 7.4 %finish.1 = bf16[2,768,512]{2,1,0:T(8,128)(2,1)} custom-call(s32[2]{0:T(128)S(1)} %copy-done.31, s32[1]{0:T(128)} %bitcast.pos_ref, f32[768,1024]{1,0:T(8,128)S(1)} %copy-done.17, f32[768,1024]{1,0:T(8,128)S(1)} %copy-done.13, f32[768,1024]{1,0:T(8,128)S(1)} %copy-done.19, f32[768,1024]{1,0:T(8,128)S(1)} %copy-done.15, bf16[2,768,1152]{2,1,0:T(8,128)(2,1)S(1)} %copy-done.4, ...), custom_call_target="tpu_custom_call" | custom-call | tf_op jit(solution)/shard_map/finish/pallas_call | solution.py:549
  (27 shorter events, 0.0 us)
Async XLA Ops:
  0.0 0.7 copy-start.27
  0.7 0.7 copy-start.28
  3.1 20.4 %all-to-all-start = ((s32[128,1,32]{2,1,0:T(1,128)}), s32[128,1,32]{2,1,0:T(1,128)S(1)}, u32[]{:S(2)}, u32[]{:S(2)}) async-start(s32[128,1,32]{2,1,0:T(1,128)} %get-tuple-element.22), calls=%async_computation | async-start | bytes 131072 | tf_op jit(solution)/shard_map/all_to_all | solution.py:570
  14.2 2.2 %copy-start.9 = (bf16[4096,512]{1,0:T(8,128)(2,1)S(1)}, bf16[4096,512]{1,0:T(8,128)(2,1)}, u32[]{:S(2)}) copy-start(bf16[4096,512]{1,0:T(8,128)(2,1)} %tab_ref.1) | copy-start | bytes 12582916
  17.5 3.3 %copy-start = (f32[16384,128]{1,0:T(8,128)}, f32[16384,128]{1,0:T(8,128)S(1)}, u32[]{:S(2)}) copy-start(f32[16384,128]{1,0:T(8,128)S(1)} %spread.1.tab_ref) | copy-start | bytes 25165828
  23.4 3.4 %copy-start.1 = (f32[16384,128]{1,0:T(8,128)S(1)}, f32[16384,128]{1,0:T(8,128)}, u32[]{:S(2)}) copy-start(f32[16384,128]{1,0:T(8,128)} %copy-done) | copy-start | bytes 25165828
  34.8 48.9 %all-to-all-start.1 = ((bf16[128,24,512]{2,1,0:T(8,128)(2,1)}), bf16[128,24,512]{2,1,0:T(8,128)(2,1)}, u32[]{:S(2)}, u32[]{:S(2)}) async-start(bf16[128,24,512]{2,1,0:T(8,128)(2,1)} %bitcast.2), calls=%async_computation.1 | async-start | bytes 6291456 | tf_op jit(solution)/shard_map/all_to_all | solution.py:570
  45.2 38.4 %copy-start.30 = (f32[512]{0:T(512)S(1)}, f32[512]{0:T(512)}, u32[]{:S(2)}) copy-start(f32[512]{0:T(512)} %param.18) | copy-start | bytes 6148
  46.9 2.7 %copy-start.5 = (bf16[1536,2048]{1,0:T(8,128)(2,1)}, bf16[1536,2048]{1,0:T(8,128)(2,1)S(1)}, u32[]{:S(2)}) copy-start(bf16[1536,2048]{1,0:T(8,128)(2,1)S(1)} %choose.1.hot_ref) | copy-start | bytes 18874372
  83.7 2.8 %copy-start.6 = (bf16[1536,2048]{1,0:T(8,128)(2,1)S(1)}, bf16[1536,2048]{1,0:T(8,128)(2,1)}, u32[]{:S(2)}) copy-start(bf16[1536,2048]{1,0:T(8,128)(2,1)} %copy-done.5) | copy-start | bytes 18874372
  86.5 14.2 %copy-start.34 = (f32[1152]{0:T(1024)S(1)}, f32[1152]{0:T(1024)}, u32[]{:S(2)}) copy-start(f32[1152]{0:T(1024)} %param.21) | copy-start | bytes 13828
  86.5 15.8 %copy-start.25 = (f32[4,1152]{1,0:T(4,128)S(1)}, f32[4,1152]{1,0:T(4,128)}, u32[]{:S(2)}) copy-start(f32[4,1152]{1,0:T(4,128)} %cw_ref.1) | copy-start | bytes 55300
  86.5 15.8 %copy-start.26 = (f32[2,768]{1,0:T(2,128)S(1)}, f32[2,768]{1,0:T(2,128)}, u32[]{:S(2)}) copy-start(f32[2,768]{1,0:T(2,128)} %gap_ref.1) | copy-start | bytes 18436
  86.5 15.8 %copy-start.31 = (s32[2]{0:T(128)S(1)}, s32[2]{0:T(128)}, u32[]{:S(2)}) copy-start(s32[2]{0:T(128)} %len_ref.3) | copy-start | bytes 28
  86.5 15.8 %copy-start.32 = (f32[16]{0:T(128)S(1)}, f32[16]{0:T(128)}, u32[]{:S(2)}) copy-start(f32[16]{0:T(128)} %param.22) | copy-start | bytes 196
  86.5 15.8 %copy-start.33 = (f32[16]{0:T(128)S(1)}, f32[16]{0:T(128)}, u32[]{:S(2)}) copy-start(f32[16]{0:T(128)} %param.23) | copy-start | bytes 196
  94.5 1.2 copy-start.7
  95.6 1.7 copy-start.10
  97.4 1.2 copy-start.20
  98.5 3.8 %collective-permute-start = (bf16[2,8,1152]{2,1,0:T(8,128)(2,1)S(1)}, bf16[2,8,1152]{2,1,0:T(8,128)(2,1)S(1)}, u32[]{:S(2)}, u32[]{:S(2)}) collective-permute-start(bf16[2,8,1152]{2,1,0:T(8,128)(2,1)S(1)} %get-tuple-element.26), channel_id=1, source_target_pairs={{0,8},{8,16},{16,24},{24,32},{32,40},{40,48},{48,56},{56,64},{64,7... | collective-permute-start | bytes 110600 | tf_op jit(solution)/shard_map/ppermute | solution.py:609
  102.3 2.0 %copy-start.11 = (bf16[2,768,1152]{2,1,0:T(8,128)(2,1)S(1)}, bf16[2,768,1152]{2,1,0:T(8,128)(2,1)}, u32[]{:S(2)}) copy-start(bf16[2,768,1152]{2,1,0:T(8,128)(2,1)} %copy-done.10) | copy-start | bytes 10616836
  113.7 1.7 copy-start.2
  115.5 1.2 copy-start.22
  132.3 23.9 %all-to-all-start.3 = ((bf16[16,64,128]{2,1,0:T(8,128)(2,1)}), bf16[16,64,128]{2,1,0:T(8,128)(2,1)S(1)}, u32[]{:S(2)}, u32[]{:S(2)}) async-start(bf16[16,64,128]{2,1,0:T(8,128)(2,1)} %scan_spans.1), calls=%async_computation.3 | async-start | bytes 524288 | tf_op jit(solution)/shard_map/all_to_all | solution.py:570
  136.0 2.0 %copy-start.3 = (bf16[2,768,1152]{2,1,0:T(8,128)(2,1)S(1)}, bf16[2,768,1152]{2,1,0:T(8,128)(2,1)}, u32[]{:S(2)}) copy-start(bf16[2,768,1152]{2,1,0:T(8,128)(2,1)} %copy-done.2) | copy-start | bytes 10616836
  138.0 1.4 copy-start.8
  144.5 1.7 copy-start.12
  146.2 1.6 copy-start.14
  147.8 8.4 %copy-start.29 = (f32[1024]{0:T(1024)S(1)}, f32[1024]{0:T(1024)}, u32[]{:S(2)}) copy-start(f32[1024]{0:T(1024)} %param.24) | copy-start | bytes 12292
  152.8 1.7 copy-start.16
  154.5 1.7 copy-start.18
  156.2 2.0 %copy-start.4 = (bf16[2,768,1152]{2,1,0:T(8,128)(2,1)S(1)}, bf16[2,768,1152]{2,1,0:T(8,128)(2,1)}, u32[]{:S(2)}) copy-start(bf16[2,768,1152]{2,1,0:T(8,128)(2,1)} %copy-done.2) | copy-start | bytes 10616836
  158.2 1.9 %copy-start.13 = (f32[768,1024]{1,0:T(8,128)S(1)}, f32[768,1024]{1,0:T(8,128)}, u32[]{:S(2)}) copy-start(f32[768,1024]{1,0:T(8,128)} %copy-done.12) | copy-start | bytes 9437188
  160.1 1.9 %copy-start.15 = (f32[768,1024]{1,0:T(8,128)S(1)}, f32[768,1024]{1,0:T(8,128)}, u32[]{:S(2)}) copy-start(f32[768,1024]{1,0:T(8,128)} %copy-done.14) | copy-start | bytes 9437188
  162.0 1.9 %copy-start.17 = (f32[768,1024]{1,0:T(8,128)S(1)}, f32[768,1024]{1,0:T(8,128)}, u32[]{:S(2)}) copy-start(f32[768,1024]{1,0:T(8,128)} %copy-done.16) | copy-start | bytes 9437188
  163.9 1.9 %copy-start.19 = (f32[768,1024]{1,0:T(8,128)S(1)}, f32[768,1024]{1,0:T(8,128)}, u32[]{:S(2)}) copy-start(f32[768,1024]{1,0:T(8,128)} %copy-done.18) | copy-start | bytes 9437188
  165.8 1.4 copy-start.21
  167.2 1.4 copy-start.23
  168.6 1.2 copy-start.24

commit v2 on v1

v2 whole, which is shorter than its diff:
```python
import functools

import jax
import jax.numpy as jnp
from jax import lax
from jax.experimental import pallas as pl
from jax.experimental.pallas import tpu as pltpu
from jax.sharding import PartitionSpec as P

F32 = jnp.float32
BF16 = jnp.bfloat16
EPS = 1e-05
LANES = 128
CHUNK = 128
TABLE_STEP = 512
FINISH_ROWS = 256
MEBI = 1024 * 1024


def params(axes, mebi=16):
    return pltpu.CompilerParams(
        dimension_semantics=("arbitrary",) * axes, vmem_limit_bytes=mebi * MEBI
    )


def full(shape):
    return pl.BlockSpec(shape, lambda *_: (0,) * len(shape))


def first_position(events):
    return lax.axis_index("tm") * events


ON_CHIP = pl.BlockSpec(memory_space=pltpu.VMEM)
SCALARS = pl.BlockSpec(memory_space=pltpu.SMEM)


def near(array):
    return pltpu.with_memory_space_constraint(array, pltpu.VMEM)


def far(array):
    return pltpu.with_memory_space_constraint(array, pltpu.HBM)


def iota(shape, axis):
    return lax.broadcasted_iota(jnp.int32, shape, axis)


def nt(a, b):
    return lax.dot_general(a, b, (((1,), (1,)), ((), ())), preferred_element_type=F32)


def mm(a, b):
    return jnp.dot(a, b, preferred_element_type=F32)


def silu(v):
    half = 0.5 * v
    return half + half * jnp.tanh(half)


def route_kernel(owner_ref, row_ref, req_ref, place_ref, *, devices, cap, width):
    users, events = row_ref.shape
    tri = jnp.where(
        (iota((LANES, 2 * LANES), 0) < iota((LANES, 2 * LANES), 1))
        | (iota((LANES, 2 * LANES), 1) >= LANES),
        1.0,
        0.0,
    ).astype(BF16)
    slots = users * cap
    req = jnp.zeros((devices, width), F32)
    for u in range(users):
        running = jnp.zeros((devices, LANES), F32)
        for c in range(events // LANES):
            own = owner_ref[u, :, c * LANES : (c + 1) * LANES]
            row = row_ref[u : u + 1, c * LANES : (c + 1) * LANES]
            hot = iota((devices, LANES), 0) == own
            hot_b = jnp.where(hot, 1.0, 0.0).astype(BF16)
            counts = mm(hot_b, tri)
            rank = counts[:, :LANES] + running
            running = running + counts[:, LANES:]
            slot = jnp.sum(jnp.where(hot, rank, 0.0), axis=0, keepdims=True).astype(jnp.int32)
            slot = slot + u * cap
            match = iota((width, LANES), 0) == slot
            high = jnp.where(match, (row >> 6).astype(F32), 0.0).astype(BF16)
            low = jnp.where(match, (row & 63).astype(F32), 0.0).astype(BF16)
            req = req + 64.0 * nt(hot_b, high) + nt(hot_b, low)
            place = (own * (slots * 2 // 3) + slot - u * (slots // 3)).astype(F32)
            place_ref[u, c * LANES : (c + 1) * LANES, :] = jnp.broadcast_to(
                place, (LANES, LANES)
            ).T.astype(jnp.int32)
    req_ref[:, 0, :] = req.astype(jnp.int32)


def route(owners, rows, devices, cap, width):
    users, events = rows.shape
    return pl.pallas_call(
        functools.partial(route_kernel, devices=devices, cap=cap, width=width),
        out_shape=(
            jax.ShapeDtypeStruct((devices, 1, width), jnp.int32),
            pltpu.HBM((users, events, LANES), jnp.int32),
        ),
        out_specs=(ON_CHIP, ON_CHIP),
        compiler_params=params(0),
        name="route",
    )(owners, rows)


def fetch_kernel(idx_ref, tab_ref, out_ref, wide_ref, rows_ref, *, slots):
    i = pl.program_id(0)
    step, dim = tab_ref.shape
    owners = idx_ref.shape[0]
    tiles = dim // LANES
    for cb in range(tiles):
        wide_ref[pl.ds(i * step * tiles + cb, step, stride=tiles), :] = tab_ref[
            :, cb * LANES : (cb + 1) * LANES
        ].astype(F32)

    @pl.when(i == pl.num_programs(0) - 1)
    def _():
        def body(o, carry):
            base = pl.multiple_of(o * slots * tiles, 8)
            for s in range(slots):
                r = idx_ref[o, 0, s]
                rows_ref[pl.ds(base + tiles * s, tiles), :] = wide_ref[
                    pl.ds(pl.multiple_of(r * tiles, tiles), tiles), :
                ]
            return carry

        lax.fori_loop(0, owners, body, 0)

        def pack(g, carry):
            for part in range(4):
                for cb in range(tiles):
                    start = (g * 4 + part) * 16 * tiles + cb
                    out_ref[
                        pl.ds(pl.multiple_of((g * 4 + part) * 16, 16), 16),
                        cb * LANES : (cb + 1) * LANES,
                    ] = rows_ref[pl.ds(start, 16, stride=tiles), :].astype(BF16)
            return carry

        lax.fori_loop(0, owners * slots // 64, pack, 0)


def fetch(idx, table, slots):
    owners = idx.shape[0]
    items, dim = table.shape
    tiles = dim // LANES
    return pl.pallas_call(
        functools.partial(fetch_kernel, slots=slots),
        out_shape=jax.ShapeDtypeStruct((owners * slots, dim), BF16),
        grid=(items // TABLE_STEP,),
        in_specs=[SCALARS, pl.BlockSpec((TABLE_STEP, dim), lambda i: (i, 0))],
        out_specs=full((owners * slots, dim)),
        scratch_shapes=[
            pltpu.VMEM((items * tiles, LANES), F32),
            pltpu.VMEM((owners * slots * tiles, LANES), F32),
        ],
        compiler_params=params(1, 26),
        name="fetch",
    )(idx, far(table))


def project_kernel(
    got_ref, place_ref, gain_ref, w_ref, x_ref, normed_ref, conv_ref, step_ref, tail_ref, hot
):
    u = pl.program_id(0)
    owners, slots, dim = got_ref.shape
    events, width = hot.shape
    conv_dim = conv_ref.shape[2]
    heads = step_ref.shape[1]
    window = slots * 2 // 3
    rows = LANES
    for i in range(events // rows):
        at = slice(i * rows, (i + 1) * rows)
        place = place_ref[0, at, :]
        for k in range(width // LANES):
            hot[at, k * LANES : (k + 1) * LANES] = jnp.where(
                place == iota((rows, LANES), 1) + k * LANES, 1.0, 0.0
            ).astype(BF16)
    shift = pl.multiple_of(u * (slots // 3), 8)
    got = got_ref[:, pl.ds(shift, window), :].reshape(owners * window, dim)
    x = mm(hot[...], got)
    x_ref[0] = x.astype(BF16)
    normed = x * lax.rsqrt(jnp.mean(x * x, axis=-1, keepdims=True) + EPS) * gain_ref[...]
    normed = normed.astype(BF16)
    normed_ref[0] = normed
    conv = mm(normed, w_ref[:, :conv_dim]).astype(BF16)
    conv_ref[u] = conv
    tail_ref[u] = conv[events - 8 :, :]
    raw = mm(normed, w_ref[:, conv_dim : conv_dim + heads])
    step_ref[u] = raw.astype(BF16).astype(F32).T


def project(got, place, gain, weight, conv_dim, heads):
    users, events, _ = place.shape
    owners, slots, dim = got.shape
    block = lambda width: pl.BlockSpec((1, events, width), lambda u: (u, 0, 0))
    return pl.pallas_call(
        project_kernel,
        out_shape=(
            pltpu.HBM((users, events, dim), BF16),
            pltpu.HBM((users, events, dim), BF16),
            pltpu.VMEM((users, events, conv_dim), BF16),
            pltpu.VMEM((users, heads, events), F32),
            jax.ShapeDtypeStruct((users, 8, conv_dim), BF16),
        ),
        grid=(users,),
        in_specs=[ON_CHIP, block(LANES), full(gain.shape), ON_CHIP],
        out_specs=(block(dim), block(dim), ON_CHIP, ON_CHIP, full((users, 8, conv_dim))),
        scratch_shapes=[pltpu.VMEM((events, owners * (slots * 2 // 3)), BF16)],
        compiler_params=params(1, 24),
        name="project",
    )(near(got), far(place), gain, near(weight))


def lane_halves(rows_a, rows_b):
    return jnp.where(iota(rows_a.shape, rows_a.ndim - 1) < LANES // 2, rows_a, rows_b)


def running_sums(values):
    lane = iota(values.shape, 1)
    size = values.shape[1]
    ahead, back = values, values
    k = 1
    while k < size:
        ahead = ahead + jnp.where(lane >= k, pltpu.roll(ahead, k, 1), 0.0)
        back = back + jnp.where(lane < size - k, pltpu.roll(back, size - k, 1), 0.0)
        k *= 2
    return ahead, back


def pair_rhs(pair):
    low = iota(pair.shape, 1) < LANES // 2
    zero = jnp.zeros_like(pair)
    return jnp.concatenate([jnp.where(low, pair, zero), jnp.where(low, zero, pair)], axis=0)


def column(row):
    size = row.shape[1]
    return jnp.sum(
        jnp.where(iota((size, size), 0) == iota((size, size), 1), row, 0.0), axis=1, keepdims=True
    )


def states_kernel(
    len_ref,
    conv_ref,
    edge_ref,
    step_ref,
    gap_ref,
    cw_ref,
    cb_ref,
    dt_ref,
    rate_ref,
    xbc_ref,
    cum_ref,
    steps_ref,
    hold_ref,
    decay_ref,
    end_ref,
    prev,
    moves,
    weights,
    totals,
    state,
    pref,
):
    users, events, conv_dim = conv_ref.shape
    heads = step_ref.shape[1]
    chunks = events // CHUNK
    pairs = heads // 2
    inner = pairs * LANES
    n_state = state.shape[1]
    half = LANES // 2

    c = pl.program_id(0)

    @pl.when(c == 0)
    def _():
        dt = column(dt_ref[...])
        rate = column(rate_ref[...])
        start = first_position(events)
        steps_all, decay_all = [], []
        for k in range(chunks):
            lanes = slice(k * CHUNK, (k + 1) * CHUNK)
            for u in range(users):
                position = start + k * CHUNK + iota((heads, CHUNK), 1)
                alive = jnp.where(position < len_ref[u], 1.0, 0.0)
                raw = step_ref[u, :, lanes] + dt
                steps = alive * (jnp.maximum(raw, 0.0) + jnp.log1p(jnp.exp(-jnp.abs(raw))))
                steps_all.append(steps)
                decay_all.append(-rate * gap_ref[u : u + 1, lanes] * steps)
        steps = jnp.concatenate(steps_all, axis=0)
        ahead, back = running_sums(jnp.concatenate(decay_all, axis=0))
        after = jnp.where(iota(back.shape, 1) < CHUNK - 1, pltpu.roll(back, CHUNK - 1, 1), 0.0)
        cum_ref[...] = ahead
        steps_ref[...] = steps
        weights[...] = jnp.exp(after) * steps
        totals[...] = jnp.broadcast_to(back[:, 0:1], totals.shape)
        state[...] = jnp.zeros_like(state)
        pref[...] = jnp.zeros_like(pref)
        prev[:, 0:8, :] = jnp.zeros((users, 8, conv_dim), BF16)
        prev[:, 8:16, :] = edge_ref[...]
        for k in range(3):
            source = iota((CHUNK, CHUNK + 16), 0) - (3 - k)
            source = jnp.where(source < 0, source + CHUNK + 16, source)
            moves[k] = jnp.where(source == iota((CHUNK, CHUNK + 16), 1), 1.0, 0.0).astype(BF16)

    for u in range(users):
        time = pl.ds(pl.multiple_of(c * CHUNK, CHUNK), CHUNK)
        at = 0
        while at < conv_dim:
            width = min(2 * LANES, conv_dim - at)
            cols = slice(at, at + width)
            here = conv_ref[u, time, cols]
            both = jnp.concatenate([here, prev[u, :, cols]], axis=0)
            prev[u, :, cols] = here[CHUNK - 16 :, :]
            total = cb_ref[cols].reshape(1, width) + cw_ref[3:4, cols] * here.astype(F32)
            for k in range(3):
                total = total + cw_ref[k : k + 1, cols] * mm(moves[k], both)
            xbc_ref[u, :, cols] = silu(total).astype(BF16)
            at += width
        decay_ref[u, 0] = jnp.exp(pref[u])
        hold_ref[u, 0] = state[u].astype(BF16)
        coef_t = xbc_ref[u, :, inner : inner + LANES].astype(F32).T[:n_state, :]
        first = pl.multiple_of((c * users + u) * heads, heads)
        weight = weights[pl.ds(first, heads), :]
        total = totals[pl.ds(first, heads), :]
        for j in range(pairs):
            lanes = slice(j * LANES, (j + 1) * LANES)
            a, b = 2 * j, 2 * j + 1
            left = jnp.concatenate(
                [coef_t * weight[a : a + 1, :], coef_t * weight[b : b + 1, :]], axis=1
            ).astype(BF16)
            add = mm(left, pair_rhs(xbc_ref[u, :, lanes]))
            tot = lane_halves(total[a : a + 1, :], total[b : b + 1, :])
            state[u, :, lanes] = jnp.exp(tot) * state[u, :, lanes] + add
            pref[u, :, lanes] = pref[u, :, lanes] + tot

    @pl.when(c == chunks - 1)
    def _():
        for h in range(heads):
            lanes = slice((h // 2) * LANES, (h // 2 + 1) * LANES)
            parts = []
            for u in range(users):
                value = state[u, :, lanes]
                low = jnp.broadcast_to(pref[u, :, lanes], (8, LANES))
                if h % 2 != u:
                    value = pltpu.roll(value, half, 1)
                    low = pltpu.roll(low, half, 1)
                high = low.astype(BF16).astype(F32)
                row = iota((8, LANES), 0)
                extra = jnp.where(row == 0, high, jnp.where(row == 1, low - high, 0.0))
                parts.append(jnp.concatenate([value, extra], axis=0))
            end_ref[h] = lane_halves(*parts).astype(BF16)


def chunk_states(lens, conv, edge, step, gap, cw, cb, dt, rate, n_state):
    users, events, conv_dim = conv.shape
    heads = step.shape[1]
    inner = conv_dim - 2 * n_state
    chunks = events // CHUNK
    lines = chunks * users * heads
    return pl.pallas_call(
        states_kernel,
        out_shape=(
            pltpu.HBM((users, events, conv_dim), BF16),
            pltpu.HBM((lines, CHUNK), F32),
            pltpu.HBM((lines, CHUNK), F32),
            pltpu.HBM((users, chunks, n_state, inner), BF16),
            pltpu.HBM((users, chunks, 1, inner), F32),
            pltpu.HBM((heads, n_state + 8, LANES), BF16),
        ),
        grid=(chunks,),
        in_specs=[SCALARS, ON_CHIP, full(edge.shape), ON_CHIP]
        + [full(v.shape) for v in (gap, cw, cb, dt, rate)],
        out_specs=(
            pl.BlockSpec((users, CHUNK, conv_dim), lambda c: (0, c, 0)),
            full((lines, CHUNK)),
            full((lines, CHUNK)),
            pl.BlockSpec((users, 1, n_state, inner), lambda c: (0, c, 0, 0)),
            pl.BlockSpec((users, 1, 1, inner), lambda c: (0, c, 0, 0)),
            full((heads, n_state + 8, LANES)),
        ),
        scratch_shapes=[
            pltpu.VMEM((users, 16, conv_dim), BF16),
            pltpu.VMEM((3, CHUNK, CHUNK + 16), BF16),
            pltpu.VMEM((lines, CHUNK), F32),
            pltpu.VMEM((lines, LANES), F32),
            pltpu.VMEM((users, n_state, inner), F32),
            pltpu.VMEM((users, 1, inner), F32),
        ],
        compiler_params=params(1),
        name="chunk_states",
    )(lens, near(conv), edge, near(step), gap, cw, cb, dt, rate)


def scan_kernel(in_ref, out_ref):
    spans, rows, lanes = in_ref.shape
    n_state = rows - 8
    running = jnp.zeros((n_state, lanes), F32)
    for k in range(spans):
        out_ref[k] = running.astype(BF16)
        block = in_ref[k].astype(F32)
        log_decay = block[n_state : n_state + 1, :] + block[n_state + 1 : n_state + 2, :]
        running = jnp.exp(log_decay) * running + block[:n_state, :]


def scan_spans(ends):
    spans, rows, lanes = ends.shape
    return pl.pallas_call(
        scan_kernel,
        out_shape=jax.ShapeDtypeStruct((spans, rows - 8, lanes), BF16),
        in_specs=[ON_CHIP],
        out_specs=ON_CHIP,
        compiler_params=params(0),
        name="scan_spans",
    )(near(ends))


def local_kernel(normed_ref, w_ref, xbc_ref, cum_ref, steps_ref, y_ref, fade_ref, gates):
    _, inner = y_ref.shape
    heads = cum_ref.shape[0]
    pairs = heads // 2
    half = LANES // 2
    gates[...] = silu(mm(normed_ref[0], w_ref[...]).astype(BF16).astype(F32))
    coef = xbc_ref[0, :, inner : inner + LANES]
    scores = nt(coef[:, half:], coef[:, :half])
    causal = iota((CHUNK, CHUNK), 0) >= iota((CHUNK, CHUNK), 1)
    scores = jnp.where(causal, scores, 0.0)
    cum = cum_ref[...]
    steps = steps_ref[...]
    cum_t = jnp.concatenate([cum, jnp.zeros((LANES - heads, CHUNK), F32)], axis=0).T

    def mixing(h):
        own = jnp.broadcast_to(cum_t[:, h : h + 1], (CHUNK, CHUNK))
        fading = jnp.exp(jnp.minimum(own - cum[h : h + 1, :], 0.0))
        return own, (scores * fading * steps[h : h + 1, :]).astype(BF16)

    for j in range(pairs):
        lanes = slice(j * LANES, (j + 1) * LANES)
        own_a, mix_a = mixing(2 * j)
        own_b, mix_b = mixing(2 * j + 1)
        left = jnp.concatenate([mix_a, mix_b], axis=1)
        gate = gates[:, lanes]
        y_ref[:, lanes] = gate * mm(left, pair_rhs(xbc_ref[0, :, lanes]))
        fade_ref[:, lanes] = gate * jnp.exp(lane_halves(own_a, own_b))


def local_response(normed, weight, xbc, cum, steps, user):
    users, events, conv_dim = xbc.shape
    dim, inner = weight.shape
    heads = cum.shape[0] * CHUNK // (users * events)
    block = lambda width: pl.BlockSpec((1, CHUNK, width), lambda c: (user, c, 0))
    lines = pl.BlockSpec((heads, CHUNK), lambda c: (c * users + user, 0))
    result = pl.BlockSpec((CHUNK, inner), lambda c: (c, 0))
    return pl.pallas_call(
        local_kernel,
        out_shape=(pltpu.HBM((events, inner), F32),) * 2,
        grid=(events // CHUNK,),
        in_specs=[block(dim), full(weight.shape), block(conv_dim), lines, lines],
        out_specs=(result, result),
        scratch_shapes=[pltpu.VMEM((CHUNK, inner), F32)],
        compiler_params=params(1),
        name="local_response",
    )(*[far(v) for v in (normed, weight, xbc, cum, steps)])


def finish_kernel(
    len_ref,
    y0_ref,
    y1_ref,
    fade0_ref,
    fade1_ref,
    coef_ref,
    x_ref,
    hold_ref,
    decay_ref,
    hin_ref,
    gain_ref,
    w_ref,
    out_ref,
    incoming,
    same,
    normed,
    *,
    blocks,
):
    u = pl.program_id(0) // blocks
    b = pl.program_id(0) % blocks
    heads = hin_ref.shape[0]
    pairs = heads // 2
    half = LANES // 2
    size = 2 * LANES
    rows = out_ref.shape[1]

    @pl.when(pl.program_id(0) == 0)
    def _():
        same[...] = jnp.where(
            iota((size, size), 0) // half == iota((size, size), 1) // half, 1.0 / half, 0.0
        ).astype(BF16)
        for j in range(pairs):
            a = hin_ref[2 * j].astype(F32)
            b = hin_ref[2 * j + 1].astype(F32)
            lanes = slice(j * LANES, (j + 1) * LANES)
            incoming[0, :, lanes] = lane_halves(a, pltpu.roll(b, half, 1))
            incoming[1, :, lanes] = lane_halves(pltpu.roll(a, half, 1), b)

    def work(y_ref, fade_ref):
        for part in range(rows // CHUNK):
            here = slice(part * CHUNK, (part + 1) * CHUNK)
            held = hold_ref[0, part].astype(F32) + decay_ref[0, part] * incoming[u]
            held = held.astype(BF16)
            coef = coef_ref[0, here, half:]
            for j in range(pairs // 2):
                lanes = slice(j * size, (j + 1) * size)
                carried = mm(coef, held[:, lanes])
                gated = y_ref[here, lanes] + fade_ref[here, lanes] * carried
                mean = mm((gated * gated).astype(BF16), same[...])
                normed[here, lanes] = (
                    gated * lax.rsqrt(mean + EPS) * gain_ref[:, lanes]
                ).astype(BF16)
        mixed = mm(normed[...], w_ref[...])
        position = first_position(blocks * rows) + b * rows + iota((rows, 1), 0)
        alive = jnp.where(position < len_ref[u], 1.0, 0.0)
        out_ref[0] = (alive * (x_ref[0].astype(F32) + mixed)).astype(BF16)

    pl.when(u == 0)(functools.partial(work, y0_ref, fade0_ref))
    pl.when(u == 1)(functools.partial(work, y1_ref, fade1_ref))


def finish(lens, ys, fades, xbc, x, hold, decay, hin, gain, weight):
    events, inner = ys[0].shape
    n_state = hold.shape[2]
    users, _, dim = x.shape
    size = 2 * LANES
    rows = FINISH_ROWS
    blocks = events // rows
    parts = rows // CHUNK
    early = pl.BlockSpec((rows, inner), lambda i: (jnp.minimum(i, blocks - 1), 0))
    late = pl.BlockSpec((rows, inner), lambda i: (jnp.maximum(i - blocks, 0), 0))
    block = pl.BlockSpec((1, rows, dim), lambda i: (i // blocks, i % blocks, 0))
    per_chunk = lambda *shape: pl.BlockSpec(
        (1, parts) + shape, lambda i: (i // blocks, i % blocks, 0, 0)
    )
    return pl.pallas_call(
        functools.partial(finish_kernel, blocks=blocks),
        out_shape=jax.ShapeDtypeStruct((users, events, dim), BF16),
        grid=(users * blocks,),
        in_specs=[
            SCALARS,
            early,
            late,
            early,
            late,
            pl.BlockSpec((1, rows, LANES), lambda i: (i // blocks, i % blocks, inner // LANES)),
            block,
            per_chunk(n_state, inner),
            per_chunk(1, inner),
            full(hin.shape),
            full(gain.shape),
            full(weight.shape),
        ],
        out_specs=block,
        scratch_shapes=[
            pltpu.VMEM((users, n_state, inner), F32),
            pltpu.VMEM((size, size), BF16),
            pltpu.VMEM((rows, inner), BF16),
        ],
        compiler_params=params(1, 24),
        name="finish",
    )(lens, *[far(v) for v in (*ys, *fades, xbc, x, hold, decay)], hin, gain, weight)


def exchange(values, axes):
    return lax.all_to_all(values, axes, split_axis=0, concat_axis=0, tiled=True)


def per_device(
    item_owner,
    item_row,
    history_len,
    event_gap,
    item_table,
    norm_gain,
    in_weight,
    conv_weight,
    conv_bias,
    dt_bias,
    decay_rate,
    out_gain,
    emitted_projection,
):
    users, events = item_row.shape
    dim = item_table.shape[1]
    heads = dt_bias.shape[0]
    inner = emitted_projection.shape[0]
    conv_dim = conv_weight.shape[1]
    n_state = (conv_dim - inner) // 2
    times = lax.axis_size("tm")
    devices = times * lax.axis_size("table")
    cap = 2 * events // devices
    slots = users * cap
    everyone = ("tm", "table")

    requests, place = route(jnp.swapaxes(item_owner, 1, 2), item_row, devices, cap, 32)
    asked = exchange(requests, everyone)
    rows = fetch(asked, item_table, slots)
    got = exchange(rows.reshape(devices, slots, dim), everyone)
    got, gate_weight, conv_in_weight = lax.optimization_barrier(
        (got, in_weight[:, :inner], in_weight[:, inner:])
    )
    x, normed, conv, step, tail = project(
        got, place, norm_gain[None, :], conv_in_weight, conv_dim, heads
    )
    edge = lax.ppermute(tail, "tm", [(i, i + 1) for i in range(times - 1)])
    xbc, cum, steps, hold, decay, ends = chunk_states(
        history_len,
        conv,
        edge,
        step,
        event_gap,
        conv_weight,
        conv_bias,
        dt_bias[None, :],
        decay_rate[None, :],
        n_state,
    )
    by_head = exchange(ends, "tm")
    y0, fade0 = local_response(normed, gate_weight, xbc, cum, steps, 0)
    by_head, y0, fade0 = lax.optimization_barrier((by_head, y0, fade0))
    hin = exchange(scan_spans(by_head), "tm")
    y1, fade1 = local_response(normed, gate_weight, xbc, cum, steps, 1)
    return finish(
        history_len,
        (y0, y1),
        (fade0, fade1),
        xbc,
        x,
        hold,
        decay,
        hin,
        out_gain[None, :],
        emitted_projection,
    )


def solution(mesh):
    in_specs = (
        P("table", "tm", None),
        P("table", "tm"),
        P("table"),
        P("table", "tm"),
        P(("tm", "table"), None),
        P(),
        P(),
        P(),
        P(),
        P(),
        P(),
        P(),
        P(),
    )
    out_specs = P("table", "tm", None)
    return jax.shard_map(
        per_device, mesh=mesh, in_specs=in_specs, out_specs=out_specs, check_vma=False
    )
```

time: 178 us -> 149 us (0.84)
  local copies, waits for them, and re-layouts: 51.2 us -> 12.1 us
  Pallas kernels: 47.9 us -> 60.5 us
  blocking collectives: 14.9 us -> 20.2 us
  starting transfers between devices: 24.6 us -> 20.4 us
  waiting for transfers between devices: 38.3 us -> 34.1 us
    unnamed x71 -> x24, local copies, waits for them, and re-layouts: 51.2 us -> 2.74 us
    pallas_call x7 -> x5, Pallas kernels: 37.4 us -> 45.9 us  [the longest x2 17 us: local_response(): pl.pallas_call(local_kernel, out_shape=(pltpu.HBM((events, inner), F32),)...]
    all_to_all x1, blocking collectives: 14.9 us -> 20.2 us  [exchange(): return lax.all_to_all(values, axes, split_axis=0, concat_axis=0, tiled=True)]
    optimization_barrier x0 -> x2, local copies, waits for them, and re-layouts: none -> 4.71 us  [per_device(): lax.optimization_barrier((got, in_weight[:, :inner], in_weight[:, inner:]))]
    slice x0 -> x2, local copies, waits for them, and re-layouts: none -> 4.65 us  [the longest x1 2.38 us: per_device(): in_weight[:, inner:]]
    all_to_all x3, waiting for transfers between devices: 36.7 us -> 32.5 us  [exchange(): return lax.all_to_all(values, axes, split_axis=0, concat_axis=0, tiled=True)]
    all_to_all x3, starting transfers between devices: 22.5 us -> 18.2 us  [exchange(): return lax.all_to_all(values, axes, split_axis=0, concat_axis=0, tiled=True)]
    pallas_call x1, Pallas kernels: 7.99 us -> 11.9 us  [fetch(): pl.pallas_call(functools.partial(fetch_kernel, slots=slots), out_shape=ja...]
  transfers between devices with their start and end apart: 4 -> 4, of which waited for: 3 -> 3; matrix products, arithmetic and copies ran while one was open for 2% -> 6% of each run, Pallas kernels for 7% -> 12%
where the time goes in v2:
time: 149 us; the launch traced here: 147 us
  Pallas kernels  60.5 us (41%)
  waiting for transfers between devices  34.1 us (23%)
  starting transfers between devices  20.4 us (14%)
  blocking collectives  20.2 us (14%)
  local copies, waits for them, and re-layouts  12.1 us (8%)
    all_to_all x3, waiting for transfers between devices, exchange(): return lax.all_to_all(values, axes, split_axis=0, concat_axis=0, tiled=True)  32.5 us
    all_to_all x1, blocking collectives, exchange(): return lax.all_to_all(values, axes, split_axis=0, concat_axis=0, tiled=True)  20.2 us
    all_to_all x3, starting transfers between devices, exchange(): return lax.all_to_all(values, axes, split_axis=0, concat_axis=0, tiled=True)  18.2 us
    pallas_call x2, Pallas kernels, local_response(): pl.pallas_call(local_kernel, out_shape=(pltpu.HBM((events, inner), F32),)...  17 us
    pallas_call x1, Pallas kernels, fetch(): pl.pallas_call(functools.partial(fetch_kernel, slots=slots), out_shape=ja...  11.9 us
    pallas_call x1, Pallas kernels, chunk_states(): pl.pallas_call(states_kernel, out_shape=(pltpu.HBM((users, events, conv_d...  10.8 us
    pallas_call x1, Pallas kernels, finish(): pl.pallas_call(functools.partial(finish_kernel, blocks=blocks), out_shape...  10.8 us
    pallas_call x1, Pallas kernels, project(): pl.pallas_call(project_kernel, out_shape=(pltpu.HBM((users, events, dim),...  7.33 us
  transfers between devices with their start and end apart: 4, of which 3 were waited for; matrix products, arithmetic and copies ran while one was open for 6% of the time, Pallas kernels for 12%

profile of v2, /device:TPU:0, one launch (start us, length us, event | category | flops | bytes accessed | tf_op | source)
XLA Modules:
  0.0 147.4 jit_solution(14106579016563083518)
XLA Ops:
  0.0 0.0 copy-start.4
  0.0 0.7 copy-done.4
  0.7 0.0 copy-start.5
  0.7 0.7 copy-done.5
  1.4 1.9 %route.1 = (s32[128,1,32]{2,1,0:T(1,128)S(1)}, s32[2,768,128]{2,1,0:T(8,128)}) custom-call(s32[2,1,768]{2,1,0:T(1,128)S(1)} %bitcast.6, s32[2,768]{1,0:T(2,128)S(1)} %copy-done.5), custom_call_target="tpu_custom_call" | custom-call | tf_op jit(solution)/shard_map/route/pallas_call | solution.py:98
  3.3 20.2 %all_to_all.20.idx_ref = s32[128,1,32]{2,1,0:T(1,128)S(1)} all-to-all(s32[128,1,32]{2,1,0:T(1,128)S(1)} %get-tuple-element.28), channel_id=1, replica_groups=mesh['tm'=16,'table'=8] {'tm','table'}, dimensions={0} | all-to-all | bytes 32768 | tf_op jit(solution)/shard_map/all_to_all | solution.py:578
  23.5 11.9 %fetch.1 = bf16[3072,512]{1,0:T(8,128)(2,1)} custom-call(s32[128,1,32]{2,1,0:T(1,128)S(1)} %all_to_all.20.idx_ref, bf16[4096,512]{1,0:T(8,128)(2,1)} %tab_ref.1), custom_call_target="tpu_custom_call" | custom-call | tf_op jit(solution)/shard_map/fetch/pallas_call | solution.py:150
  35.4 4.8 %all-to-all-start.1 = ((bf16[128,24,512]{2,1,0:T(8,128)(2,1)}), bf16[128,24,512]{2,1,0:T(8,128)(2,1)S(1)}, u32[]{:S(2)}, u32[]{:S(2)}) async-start(bf16[128,24,512]{2,1,0:T(8,128)(2,1)} %bitcast.1), calls=%async_computation.1 | async-start | bytes 6291456 | tf_op jit(solution)/shard_map/all_to_all | solution.py:578
  40.2 2.3 %slice.6 = bf16[512,1024]{0,1:T(8,128)(2,1)} slice(bf16[512,2192]{0,1:T(8,128)(2,1)} %param.19), slice={[0:512], [0:1024]} | slice | bytes 2097152 | tf_op jit(solution)/shard_map/slice | solution.py:613
  42.5 0.0 copy-start.9
  42.5 2.4 %slice.7 = bf16[512,1168]{0,1:T(8,128)(2,1)} slice(bf16[512,2192]{0,1:T(8,128)(2,1)} %param.19), slice={[0:512], [1024:2192]} | slice | bytes 2392064 | tf_op jit(solution)/shard_map/slice | solution.py:613
  44.9 2.3 %copy.16.w_ref = bf16[512,1024]{1,0:T(8,128)(2,1)} copy(bf16[512,1024]{0,1:T(8,128)(2,1)} %slice.6) | data formatting | bytes 2097152 | tf_op jit(solution)/shard_map/optimization_barrier | solution.py:612
  47.1 0.0 copy-start.2
  47.1 0.0 copy-start.3
  47.1 0.0 copy-start.6
  47.2 2.4 %copy.17.w_ref = bf16[512,1168]{1,0:T(8,128)(2,1)} copy(bf16[512,1168]{0,1:T(8,128)(2,1)} %slice.7) | data formatting | bytes 2392064 | tf_op jit(solution)/shard_map/optimization_barrier | solution.py:612
  49.6 0.0 copy-start.8
  49.6 0.0 copy-start.10
  49.6 0.0 copy-start.11
  49.6 32.2 %all-to-all-done.1.got_ref = bf16[128,24,512]{2,1,0:T(8,128)(2,1)S(1)} async-done(((bf16[128,24,512]{2,1,0:T(8,128)(2,1)}), bf16[128,24,512]{2,1,0:T(8,128)(2,1)S(1)}, u32[]{:S(2)}, u32[]{:S(2)}) %all-to-all-start.1) | async-done | bytes 3145760 | tf_op jit(solution)/shard_map/all_to_all | solution.py:578
  81.8 0.0 copy-done.9
  81.8 0.0 copy-start
  81.8 1.3 copy-done
  83.2 7.3 %project.1 = (bf16[2,768,512]{2,1,0:T(8,128)(2,1)}, bf16[2,768,512]{2,1,0:T(8,128)(2,1)}, bf16[2,768,1152]{2,1,0:T(8,128)(2,1)S(1)}, f32[2,16,768]{2,1,0:T(8,128)S(1)}, bf16[2,8,1152]{2,1,0:T(8,128)(2,1)S(1)}) custom-call(bf16[128,24,512]{2,1,0:T(8,128)(2,1)S(1)} %all-to-all-done.1.got_ref, s32[2,768,128]{2,1,0:T(8,128)} %get-tuple-element.30.place_ref, ...), custom_call_target="tpu_custom_call" | custom-call | tf_op jit(solution)/shard_map/project/pallas_call | solution.py:200
  90.5 2.2 %collective-permute-start = (bf16[2,8,1152]{2,1,0:T(8,128)(2,1)S(1)}, bf16[2,8,1152]{2,1,0:T(8,128)(2,1)S(1)}, u32[]{:S(2)}, u32[]{:S(2)}) collective-permute-start(bf16[2,8,1152]{2,1,0:T(8,128)(2,1)S(1)} %get-tuple-element.33), channel_id=1, source_target_pairs={{0,8},{8,16},{16,24},{24,32},{32,40},{40,48},{48,56},{56,64},{64,7... | collective-permute-start | bytes 110600 | tf_op jit(solution)/shard_map/ppermute | solution.py:618
  92.7 1.6 %collective-permute-done.edge_ref = bf16[2,8,1152]{2,1,0:T(8,128)(2,1)S(1)} collective-permute-done((bf16[2,8,1152]{2,1,0:T(8,128)(2,1)S(1)}, bf16[2,8,1152]{2,1,0:T(8,128)(2,1)S(1)}, u32[]{:S(2)}, u32[]{:S(2)}) %collective-permute-start) | collective-permute-done | bytes 36896 | tf_op jit(solution)/shard_map/ppermute | solution.py:618
  94.3 0.0 copy-done.2
  94.3 0.0 copy-done.3
  94.3 0.0 copy-done.6
  94.3 0.0 copy-done.8
  94.3 0.0 copy-done.10
  94.3 0.0 copy-done.11
  94.3 10.8 %chunk_states.1 = (bf16[2,768,1152]{2,1,0:T(8,128)(2,1)}, f32[192,128]{1,0:T(8,128)}, f32[192,128]{1,0:T(8,128)}, bf16[2,6,64,1024]{3,2,1,0:T(8,128)(2,1)}, f32[...) custom-call(s32[2]{0:T(128)S(1)} %copy-done.8, bf16[2,768,1152]{2,1,0:T(8,128)(2,1)S(1)} %get-tuple-element.32.conv_ref, ...), custom_call_target="tpu_custom_call" | custom-call | tf_op jit(solution)/shard_map/chunk_states/pallas_call | solution.py:366
  105.1 6.4 %all-to-all-start.2 = ((bf16[16,72,128]{2,1,0:T(8,128)(2,1)}), bf16[16,72,128]{2,1,0:T(8,128)(2,1)S(1)}, u32[]{:S(2)}, u32[]{:S(2)}) async-start(bf16[16,72,128]{2,1,0:T(8,128)(2,1)} %get-tuple-element.35), calls=%async_computation.2 | async-start | bytes 589824 | tf_op jit(solution)/shard_map/all_to_all | solution.py:578
  111.6 8.4 %local_response.2 = (f32[768,1024]{1,0:T(8,128)}, f32[768,1024]{1,0:T(8,128)}) custom-call(bf16[2,768,512]{2,1,0:T(8,128)(2,1)} %get-tuple-element.36.normed_ref, bf16[512,1024]{1,0:T(8,128)(2,1)} %copy.16.w_ref, bf16[2,768,1152]{2,1,0:T(8,128)(2,1)} %get-tuple-element.38.xbc_ref.coef_ref, f32[192,128]{1,0:T(8,128)} %get-tuple-element.39.cum_ref, ...), custom_call_target="tpu_custom_call" | custom-call | tf_op jit(solution)/shard_map/local_response/pallas_call | solution.py:459
  120.0 0.2 all-to-all-done.2.in_ref
  120.2 0.8 scan_spans.1
  121.0 7.0 %all-to-all-start.3 = ((bf16[16,64,128]{2,1,0:T(8,128)(2,1)}), bf16[16,64,128]{2,1,0:T(8,128)(2,1)S(1)}, u32[]{:S(2)}, u32[]{:S(2)}) async-start(bf16[16,64,128]{2,1,0:T(8,128)(2,1)} %scan_spans.1), calls=%async_computation.3 | async-start | bytes 524288 | tf_op jit(solution)/shard_map/all_to_all | solution.py:578
  128.0 0.0 copy-start.1
  128.0 0.0 copy-start.7
  128.1 8.6 %local_response.3 = (f32[768,1024]{1,0:T(8,128)}, f32[768,1024]{1,0:T(8,128)}) custom-call(bf16[2,768,512]{2,1,0:T(8,128)(2,1)} %get-tuple-element.36.normed_ref, bf16[512,1024]{1,0:T(8,128)(2,1)} %copy.16.w_ref, bf16[2,768,1152]{2,1,0:T(8,128)(2,1)} %get-tuple-element.38.xbc_ref.coef_ref, f32[192,128]{1,0:T(8,128)} %get-tuple-element.39.cum_ref, ...), custom_call_target="tpu_custom_call" | custom-call | tf_op jit(solution)/shard_map/local_response/pallas_call | solution.py:459
  136.6 0.0 all-to-all-done.3.hin_ref
  136.6 0.0 copy-done.1
  136.6 0.0 copy-done.7
  136.6 10.8 %finish.1 = bf16[2,768,512]{2,1,0:T(8,128)(2,1)} custom-call(s32[2]{0:T(128)S(1)} %copy-done.8, f32[768,1024]{1,0:T(8,128)} %get-tuple-element.43.y0_ref, f32[768,1024]{1,0:T(8,128)} %get-tuple-element.44.y1_ref, f32[768,1024]{1,0:T(8,128)} %get-tuple-element.45.fade0_ref, f32[768,1024]{1,0:T(8,128)} %get-tuple-element.46.fade1_ref, ...), custom_call_target="tpu_custom_call" | custom-call | tf_op jit(solution)/shard_map/finish/pallas_call | solution.py:548
Async XLA Ops:
  0.0 0.7 copy-start.4
  0.7 0.7 copy-start.5
  35.4 46.4 %all-to-all-start.1 = ((bf16[128,24,512]{2,1,0:T(8,128)(2,1)}), bf16[128,24,512]{2,1,0:T(8,128)(2,1)S(1)}, u32[]{:S(2)}, u32[]{:S(2)}) async-start(bf16[128,24,512]{2,1,0:T(8,128)(2,1)} %bitcast.1), calls=%async_computation.1 | async-start | bytes 6291456 | tf_op jit(solution)/shard_map/all_to_all | solution.py:578
  42.5 39.4 %copy-start.9 = (f32[512]{0:T(512)S(1)}, f32[512]{0:T(512)}, u32[]{:S(2)}) copy-start(f32[512]{0:T(512)} %param.18) | copy-start | bytes 6148
  47.1 47.1 %copy-start.2 = (f32[4,1152]{1,0:T(4,128)S(1)}, f32[4,1152]{1,0:T(4,128)}, u32[]{:S(2)}) copy-start(f32[4,1152]{1,0:T(4,128)} %cw_ref.1) | copy-start | bytes 55300
  47.1 47.1 %copy-start.3 = (f32[1152]{0:T(1024)S(1)}, f32[1152]{0:T(1024)}, u32[]{:S(2)}) copy-start(f32[1152]{0:T(1024)} %cb_ref.1) | copy-start | bytes 13828
  47.1 47.1 %copy-start.6 = (f32[2,768]{1,0:T(2,128)S(1)}, f32[2,768]{1,0:T(2,128)}, u32[]{:S(2)}) copy-start(f32[2,768]{1,0:T(2,128)} %gap_ref.1) | copy-start | bytes 18436
  49.6 44.7 %copy-start.8 = (s32[2]{0:T(128)S(1)}, s32[2]{0:T(128)}, u32[]{:S(2)}) copy-start(s32[2]{0:T(128)} %len_ref.3) | copy-start | bytes 28
  49.6 44.7 %copy-start.10 = (f32[16]{0:T(128)S(1)}, f32[16]{0:T(128)}, u32[]{:S(2)}) copy-start(f32[16]{0:T(128)} %param.22) | copy-start | bytes 196
  49.6 44.7 %copy-start.11 = (f32[16]{0:T(128)S(1)}, f32[16]{0:T(128)}, u32[]{:S(2)}) copy-start(f32[16]{0:T(128)} %param.23) | copy-start | bytes 196
  81.8 1.3 copy-start
  90.5 3.8 %collective-permute-start = (bf16[2,8,1152]{2,1,0:T(8,128)(2,1)S(1)}, bf16[2,8,1152]{2,1,0:T(8,128)(2,1)S(1)}, u32[]{:S(2)}, u32[]{:S(2)}) collective-permute-start(bf16[2,8,1152]{2,1,0:T(8,128)(2,1)S(1)} %get-tuple-element.33), channel_id=1, source_target_pairs={{0,8},{8,16},{16,24},{24,32},{32,40},{40,48},{48,56},{56,64},{64,7... | collective-permute-start | bytes 110600 | tf_op jit(solution)/shard_map/ppermute | solution.py:618
  105.1 15.1 %all-to-all-start.2 = ((bf16[16,72,128]{2,1,0:T(8,128)(2,1)}), bf16[16,72,128]{2,1,0:T(8,128)(2,1)S(1)}, u32[]{:S(2)}, u32[]{:S(2)}) async-start(bf16[16,72,128]{2,1,0:T(8,128)(2,1)} %get-tuple-element.35), calls=%async_computation.2 | async-start | bytes 589824 | tf_op jit(solution)/shard_map/all_to_all | solution.py:578
  121.0 15.6 %all-to-all-start.3 = ((bf16[16,64,128]{2,1,0:T(8,128)(2,1)}), bf16[16,64,128]{2,1,0:T(8,128)(2,1)S(1)}, u32[]{:S(2)}, u32[]{:S(2)}) async-start(bf16[16,64,128]{2,1,0:T(8,128)(2,1)} %scan_spans.1), calls=%async_computation.3 | async-start | bytes 524288 | tf_op jit(solution)/shard_map/all_to_all | solution.py:578
  128.0 8.6 %copy-start.1 = (bf16[1024,512]{1,0:T(8,128)(2,1)S(1)}, bf16[1024,512]{1,0:T(8,128)(2,1)}, u32[]{:S(2)}) copy-start(bf16[1024,512]{1,0:T(8,128)(2,1)} %w_ref.1) | copy-start | bytes 3145732
  128.0 8.6 %copy-start.7 = (f32[1024]{0:T(1024)S(1)}, f32[1024]{0:T(1024)}, u32[]{:S(2)}) copy-start(f32[1024]{0:T(1024)} %param.24) | copy-start | bytes 12292

commit v3 on v2

--- a/solution.py
+++ b/solution.py
@@ -12,9 +12,12 @@
 EPS = 1e-05
 LANES = 128
 CHUNK = 128
-TABLE_STEP = 512
-FINISH_ROWS = 256
+FINISH_ROWS = 384
+LOCAL_CHUNKS = 2
+STATE_CHUNKS = 2
+PIECES = 4
 MEBI = 1024 * 1024
+ANYWHERE = pl.BlockSpec(memory_space=pl.ANY)
 
 
 def params(axes, mebi=16):
@@ -104,60 +107,93 @@
         out_specs=(ON_CHIP, ON_CHIP),
         compiler_params=params(0),
         name="route",
-    )(owners, rows)
-
-
-def fetch_kernel(idx_ref, tab_ref, out_ref, wide_ref, rows_ref, *, slots):
-    i = pl.program_id(0)
-    step, dim = tab_ref.shape
-    owners = idx_ref.shape[0]
+    )(far(owners), far(rows))
+
+
+def fetch_kernel(
+    idx_ref, tab_ref, out_ref, idx, tab, wide, picked, packed, idx_sem, in_sems, out_sems
+):
+    owners, _, _ = idx.shape
+    items, dim = tab.shape
     tiles = dim // LANES
-    for cb in range(tiles):
-        wide_ref[pl.ds(i * step * tiles + cb, step, stride=tiles), :] = tab_ref[
-            :, cb * LANES : (cb + 1) * LANES
-        ].astype(F32)
-
-    @pl.when(i == pl.num_programs(0) - 1)
-    def _():
-        def body(o, carry):
+    total = packed.shape[0]
+    slots = total // owners
+    part = items // PIECES
+    piece = total // PIECES
+    asked = pltpu.make_async_copy(idx_ref, idx, idx_sem)
+    asked.start()
+    loads = [
+        pltpu.make_async_copy(
+            tab_ref.at[pl.ds(k * part, part), :], tab.at[pl.ds(k * part, part), :], in_sems.at[k]
+        )
+        for k in range(PIECES)
+    ]
+    for load in loads:
+        load.start()
+    for k in range(PIECES):
+        loads[k].wait()
+        for cb in range(tiles):
+            wide[pl.ds(k * part * tiles + cb, part, stride=tiles), :] = tab[
+                k * part : (k + 1) * part, cb * LANES : (cb + 1) * LANES
+            ].astype(F32)
+    asked.wait()
+    stores = []
+    for k in range(PIECES):
+
+        def pick(o, carry):
             base = pl.multiple_of(o * slots * tiles, 8)
             for s in range(slots):
-                r = idx_ref[o, 0, s]
-                rows_ref[pl.ds(base + tiles * s, tiles), :] = wide_ref[
+                r = idx[k * (owners // PIECES) + o, 0, s]
+                picked[pl.ds(base + tiles * s, tiles), :] = wide[
                     pl.ds(pl.multiple_of(r * tiles, tiles), tiles), :
                 ]
             return carry
 
-        lax.fori_loop(0, owners, body, 0)
+        lax.fori_loop(0, owners // PIECES, pick, 0)
 
         def pack(g, carry):
             for part in range(4):
                 for cb in range(tiles):
                     start = (g * 4 + part) * 16 * tiles + cb
-                    out_ref[
-                        pl.ds(pl.multiple_of((g * 4 + part) * 16, 16), 16),
+                    packed[
+                        pl.ds(pl.multiple_of(k * piece + (g * 4 + part) * 16, 16), 16),
                         cb * LANES : (cb + 1) * LANES,
-                    ] = rows_ref[pl.ds(start, 16, stride=tiles), :].astype(BF16)
+                    ] = picked[pl.ds(start, 16, stride=tiles), :].astype(BF16)
             return carry
 
-        lax.fori_loop(0, owners * slots // 64, pack, 0)
+        lax.fori_loop(0, piece // 64, pack, 0)
+        store = pltpu.make_async_copy(
+            packed.at[pl.ds(k * piece, piece), :],
+            out_ref.at[pl.ds(k * piece, piece), :],
+            out_sems.at[k],
+        )
+        store.start()
+        stores.append(store)
+    for store in stores:
+        store.wait()
 
 
 def fetch(idx, table, slots):
     owners = idx.shape[0]
     items, dim = table.shape
     tiles = dim // LANES
+    total = owners * slots
     return pl.pallas_call(
-        functools.partial(fetch_kernel, slots=slots),
-        out_shape=jax.ShapeDtypeStruct((owners * slots, dim), BF16),
-        grid=(items // TABLE_STEP,),
-        in_specs=[SCALARS, pl.BlockSpec((TABLE_STEP, dim), lambda i: (i, 0))],
-        out_specs=full((owners * slots, dim)),
+        fetch_kernel,
+        out_shape=pltpu.HBM((total, dim), BF16),
+        in_specs=[ANYWHERE, ANYWHERE],
+        out_specs=ANYWHERE,
         scratch_shapes=[
+            pltpu.SMEM(idx.shape, jnp.int32),
+            pltpu.VMEM((items, dim), BF16),
             pltpu.VMEM((items * tiles, LANES), F32),
-            pltpu.VMEM((owners * slots * tiles, LANES), F32),
+            pltpu.VMEM((total // PIECES * tiles, LANES), F32),
+            pltpu.VMEM((total, dim), BF16),
+            pltpu.SemaphoreType.DMA,
+            pltpu.SemaphoreType.DMA((PIECES,)),
+            pltpu.SemaphoreType.DMA((PIECES,)),
         ],
-        compiler_params=params(1, 26),
+        compiler_params=params(0, 24),
         name="fetch",
     )(idx, far(table))
 
@@ -207,12 +243,12 @@
             jax.ShapeDtypeStruct((users, 8, conv_dim), BF16),
         ),
         grid=(users,),
-        in_specs=[ON_CHIP, block(LANES), full(gain.shape), ON_CHIP],
+        in_specs=[ON_CHIP, block(LANES), full(gain.shape), full(weight.shape)],
         out_specs=(block(dim), block(dim), ON_CHIP, ON_CHIP, full((users, 8, conv_dim))),
         scratch_shapes=[pltpu.VMEM((events, owners * (slots * 2 // 3)), BF16)],
         compiler_params=params(1, 24),
         name="project",
-    )(near(got), far(place), gain, near(weight))
+    )(near(got), far(place), gain, far(weight))
 
 
 def lane_halves(rows_a, rows_b):
@@ -275,17 +311,17 @@
     n_state = state.shape[1]
     half = LANES // 2
 
-    c = pl.program_id(0)
-
-    @pl.when(c == 0)
+    step_index = pl.program_id(0)
+
+    @pl.when(step_index == 0)
     def _():
         dt = column(dt_ref[...])
         rate = column(rate_ref[...])
         start = first_position(events)
         steps_all, decay_all = [], []
-        for k in range(chunks):
-            lanes = slice(k * CHUNK, (k + 1) * CHUNK)
-            for u in range(users):
+        for u in range(users):
+            for k in range(chunks):
+                lanes = slice(k * CHUNK, (k + 1) * CHUNK)
                 position = start + k * CHUNK + iota((heads, CHUNK), 1)
                 alive = jnp.where(position < len_ref[u], 1.0, 0.0)
                 raw = step_ref[u, :, lanes] + dt
@@ -306,10 +342,14 @@
         for k in range(3):
             source = iota((CHUNK, CHUNK + 16), 0) - (3 - k)
             source = jnp.where(source < 0, source + CHUNK + 16, source)
-            moves[k] = jnp.where(source == iota((CHUNK, CHUNK + 16), 1), 1.0, 0.0).astype(BF16)
-
-    for u in range(users):
+            moves[k * CHUNK : (k + 1) * CHUNK, :] = jnp.where(
+                source == iota((CHUNK, CHUNK + 16), 1), 1.0, 0.0
+            ).astype(BF16)
+
+    for part, u in [(p, v) for p in range(STATE_CHUNKS) for v in range(users)]:
+        c = step_index * STATE_CHUNKS + part
         time = pl.ds(pl.multiple_of(c * CHUNK, CHUNK), CHUNK)
+        rows = slice(part * CHUNK, (part + 1) * CHUNK)
         at = 0
         while at < conv_dim:
             width = min(2 * LANES, conv_dim - at)
@@ -318,28 +358,30 @@
             both = jnp.concatenate([here, prev[u, :, cols]], axis=0)
             prev[u, :, cols] = here[CHUNK - 16 :, :]
             total = cb_ref[cols].reshape(1, width) + cw_ref[3:4, cols] * here.astype(F32)
+            moved = mm(moves[...], both)
             for k in range(3):
-                total = total + cw_ref[k : k + 1, cols] * mm(moves[k], both)
-            xbc_ref[u, :, cols] = silu(total).astype(BF16)
+                total = total + cw_ref[k : k + 1, cols] * moved[k * CHUNK : (k + 1) * CHUNK, :]
+            xbc_ref[u, rows, cols] = silu(total).astype(BF16)
             at += width
-        decay_ref[u, 0] = jnp.exp(pref[u])
-        hold_ref[u, 0] = state[u].astype(BF16)
-        coef_t = xbc_ref[u, :, inner : inner + LANES].astype(F32).T[:n_state, :]
-        first = pl.multiple_of((c * users + u) * heads, heads)
+        decay_ref[u, part] = jnp.exp(pref[u])
+        hold_ref[u, part] = state[u].astype(BF16)
+        coef_t = xbc_ref[u, rows, inner : inner + LANES].astype(F32).T[:n_state, :]
+        first = pl.multiple_of((u * chunks + c) * heads, heads)
         weight = weights[pl.ds(first, heads), :]
         total = totals[pl.ds(first, heads), :]
         for j in range(pairs):
             lanes = slice(j * LANES, (j + 1) * LANES)
             a, b = 2 * j, 2 * j + 1
             left = jnp.concatenate(
-                [coef_t * weight[a : a + 1, :], coef_t * weight[b : b + 1, :]], axis=1
+                [coef_t * weight[a : a + 1, :], coef_t * weight[b : b + 1, :]], axis=0
             ).astype(BF16)
-            add = mm(left, pair_rhs(xbc_ref[u, :, lanes]))
+            both = mm(left, xbc_ref[u, rows, lanes])
+            add = lane_halves(both[:n_state], both[n_state:])
             tot = lane_halves(total[a : a + 1, :], total[b : b + 1, :])
             state[u, :, lanes] = jnp.exp(tot) * state[u, :, lanes] + add
             pref[u, :, lanes] = pref[u, :, lanes] + tot
 
-    @pl.when(c == chunks - 1)
+    @pl.when(step_index == pl.num_programs(0) - 1)
     def _():
         for h in range(heads):
             lanes = slice((h // 2) * LANES, (h // 2 + 1) * LANES)
@@ -373,20 +415,20 @@
             pltpu.HBM((users, chunks, 1, inner), F32),
             pltpu.HBM((heads, n_state + 8, LANES), BF16),
         ),
-        grid=(chunks,),
+        grid=(chunks // STATE_CHUNKS,),
         in_specs=[SCALARS, ON_CHIP, full(edge.shape), ON_CHIP]
         + [full(v.shape) for v in (gap, cw, cb, dt, rate)],
         out_specs=(
-            pl.BlockSpec((users, CHUNK, conv_dim), lambda c: (0, c, 0)),
+            pl.BlockSpec((users, STATE_CHUNKS * CHUNK, conv_dim), lambda c: (0, c, 0)),
             full((lines, CHUNK)),
             full((lines, CHUNK)),
-            pl.BlockSpec((users, 1, n_state, inner), lambda c: (0, c, 0, 0)),
-            pl.BlockSpec((users, 1, 1, inner), lambda c: (0, c, 0, 0)),
+            pl.BlockSpec((users, STATE_CHUNKS, n_state, inner), lambda c: (0, c, 0, 0)),
+            pl.BlockSpec((users, STATE_CHUNKS, 1, inner), lambda c: (0, c, 0, 0)),
             full((heads, n_state + 8, LANES)),
         ),
         scratch_shapes=[
             pltpu.VMEM((users, 16, conv_dim), BF16),
-            pltpu.VMEM((3, CHUNK, CHUNK + 16), BF16),
+            pltpu.VMEM((3 * CHUNK, CHUNK + 16), BF16),
             pltpu.VMEM((lines, CHUNK), F32),
             pltpu.VMEM((lines, LANES), F32),
             pltpu.VMEM((users, n_state, inner), F32),
@@ -421,48 +463,52 @@
 
 
 def local_kernel(normed_ref, w_ref, xbc_ref, cum_ref, steps_ref, y_ref, fade_ref, gates):
-    _, inner = y_ref.shape
-    heads = cum_ref.shape[0]
+    rows, inner = y_ref.shape
+    parts = rows // CHUNK
+    heads = cum_ref.shape[0] // parts
     pairs = heads // 2
     half = LANES // 2
     gates[...] = silu(mm(normed_ref[0], w_ref[...]).astype(BF16).astype(F32))
-    coef = xbc_ref[0, :, inner : inner + LANES]
-    scores = nt(coef[:, half:], coef[:, :half])
     causal = iota((CHUNK, CHUNK), 0) >= iota((CHUNK, CHUNK), 1)
-    scores = jnp.where(causal, scores, 0.0)
-    cum = cum_ref[...]
-    steps = steps_ref[...]
-    cum_t = jnp.concatenate([cum, jnp.zeros((LANES - heads, CHUNK), F32)], axis=0).T
-
-    def mixing(h):
-        own = jnp.broadcast_to(cum_t[:, h : h + 1], (CHUNK, CHUNK))
-        fading = jnp.exp(jnp.minimum(own - cum[h : h + 1, :], 0.0))
-        return own, (scores * fading * steps[h : h + 1, :]).astype(BF16)
-
-    for j in range(pairs):
-        lanes = slice(j * LANES, (j + 1) * LANES)
-        own_a, mix_a = mixing(2 * j)
-        own_b, mix_b = mixing(2 * j + 1)
-        left = jnp.concatenate([mix_a, mix_b], axis=1)
-        gate = gates[:, lanes]
-        y_ref[:, lanes] = gate * mm(left, pair_rhs(xbc_ref[0, :, lanes]))
-        fade_ref[:, lanes] = gate * jnp.exp(lane_halves(own_a, own_b))
+    for part in range(parts):
+        here = slice(part * CHUNK, (part + 1) * CHUNK)
+        coef = xbc_ref[0, here, inner : inner + LANES]
+        scores = jnp.where(causal, nt(coef[:, half:], coef[:, :half]), 0.0)
+        cum = cum_ref[part * heads : (part + 1) * heads, :]
+        steps = steps_ref[part * heads : (part + 1) * heads, :]
+        cum_t = jnp.concatenate([cum, jnp.zeros((LANES - heads, CHUNK), F32)], axis=0).T
+
+        def mixing(h):
+            own = jnp.broadcast_to(cum_t[:, h : h + 1], (CHUNK, CHUNK))
+            fading = jnp.exp(jnp.minimum(own - cum[h : h + 1, :], 0.0))
+            return own, (scores * fading * steps[h : h + 1, :]).astype(BF16)
+
+        for j in range(pairs):
+            lanes = slice(j * LANES, (j + 1) * LANES)
+            own_a, mix_a = mixing(2 * j)
+            own_b, mix_b = mixing(2 * j + 1)
+            left = jnp.concatenate([mix_a, mix_b], axis=1)
+            gate = gates[here, lanes]
+            y_ref[here, lanes] = (gate * mm(left, pair_rhs(xbc_ref[0, here, lanes]))).astype(BF16)
+            fade_ref[here, lanes] = (gate * jnp.exp(lane_halves(own_a, own_b))).astype(BF16)
 
 
 def local_response(normed, weight, xbc, cum, steps, user):
     users, events, conv_dim = xbc.shape
     dim, inner = weight.shape
     heads = cum.shape[0] * CHUNK // (users * events)
-    block = lambda width: pl.BlockSpec((1, CHUNK, width), lambda c: (user, c, 0))
-    lines = pl.BlockSpec((heads, CHUNK), lambda c: (c * users + user, 0))
-    result = pl.BlockSpec((CHUNK, inner), lambda c: (c, 0))
+    rows = LOCAL_CHUNKS * CHUNK
+    blocks = events // rows
+    block = lambda width: pl.BlockSpec((1, rows, width), lambda i: (user, i, 0))
+    lines = pl.BlockSpec((LOCAL_CHUNKS * heads, CHUNK), lambda i: (user * blocks + i, 0))
+    result = pl.BlockSpec((rows, inner), lambda i: (i, 0))
     return pl.pallas_call(
         local_kernel,
-        out_shape=(pltpu.HBM((events, inner), F32),) * 2,
-        grid=(events // CHUNK,),
+        out_shape=(pltpu.HBM((events, inner), BF16),) * 2,
+        grid=(blocks,),
         in_specs=[block(dim), full(weight.shape), block(conv_dim), lines, lines],
         out_specs=(result, result),
-        scratch_shapes=[pltpu.VMEM((CHUNK, inner), F32)],
+        scratch_shapes=[pltpu.VMEM((rows, inner), F32)],
         compiler_params=params(1),
         name="local_response",
     )(*[far(v) for v in (normed, weight, xbc, cum, steps)])
@@ -517,7 +563,7 @@
             for j in range(pairs // 2):
                 lanes = slice(j * size, (j + 1) * size)
                 carried = mm(coef, held[:, lanes])
-                gated = y_ref[here, lanes] + fade_ref[here, lanes] * carried
+                gated = y_ref[here, lanes].astype(F32) + fade_ref[here, lanes].astype(F32) * carried
                 mean = mm((gated * gated).astype(BF16), same[...])
                 normed[here, lanes] = (
                     gated * lax.rsqrt(mean + EPS) * gain_ref[:, lanes]

time: 149 us -> 140 us (0.940)
  Pallas kernels: 60.5 us -> 53.3 us
  local copies, waits for them, and re-layouts: 12.1 us -> 9.4 us
  waiting for transfers between devices: 34.1 us -> 36.6 us
    pallas_call x3, Pallas kernels: 28.9 us -> 22.6 us  [the longest x2 14.4 us: local_response(): pl.pallas_call(local_kernel, out_shape=(pltpu.HBM((events, inner), BF16),...]
    unnamed x24 -> x18, local copies, waits for them, and re-layouts: 2.74 us -> 0.05 us
    all_to_all x3, waiting for transfers between devices: 32.5 us -> 35 us  [exchange(): return lax.all_to_all(values, axes, split_axis=0, concat_axis=0, tiled=True)]
    pallas_call x1, Pallas kernels: 10.8 us -> 8.91 us  [finish(): pl.pallas_call(functools.partial(finish_kernel, blocks=blocks), out_shape...]
  transfers between devices with their start and end apart: 4 -> 4, of which waited for: 3 -> 4; matrix products, arithmetic and copies ran while one was open for 6% -> 7% of each run, Pallas kernels for 12% -> 10%
where the time goes in v3:
time: 140 us; the launch traced here: 139 us
  Pallas kernels  53.3 us (38%)
  waiting for transfers between devices  36.6 us (26%)
  blocking collectives  20.2 us (14%)
  starting transfers between devices  19.2 us (14%)
  local copies, waits for them, and re-layouts  9.4 us (7%)
    all_to_all x3, waiting for transfers between devices, exchange(): return lax.all_to_all(values, axes, split_axis=0, concat_axis=0, tiled=True)  35 us
    all_to_all x1, blocking collectives, exchange(): return lax.all_to_all(values, axes, split_axis=0, concat_axis=0, tiled=True)  20.2 us
    all_to_all x3, starting transfers between devices, exchange(): return lax.all_to_all(values, axes, split_axis=0, concat_axis=0, tiled=True)  17 us
    pallas_call x2, Pallas kernels, local_response(): pl.pallas_call(local_kernel, out_shape=(pltpu.HBM((events, inner), BF16),...  14.4 us
    pallas_call x1, Pallas kernels, chunk_states(): pl.pallas_call(states_kernel, out_shape=(pltpu.HBM((users, events, conv_d...  10.6 us
    pallas_call x1, Pallas kernels, finish(): pl.pallas_call(functools.partial(finish_kernel, blocks=blocks), out_shape...  8.91 us
    pallas_call x1, Pallas kernels, fetch(): pl.pallas_call(fetch_kernel, out_shape=pltpu.HBM((total, dim), BF16), in_...  8.23 us
    pallas_call x1, Pallas kernels, project(): pl.pallas_call(project_kernel, out_shape=(pltpu.HBM((users, events, dim),...  7.78 us
  transfers between devices with their start and end apart: 4, of which 4 were waited for; matrix products, arithmetic and copies ran while one was open for 7% of the time, Pallas kernels for 10%

profile of v3, /device:TPU:0, one launch (start us, length us, event | category | flops | bytes accessed | tf_op | source)
XLA Modules:
  0.0 138.8 jit_solution(3058379115494179980)
XLA Ops:
  0.0 2.6 %route.1 = (s32[128,1,32]{2,1,0:T(1,128)S(1)}, s32[2,768,128]{2,1,0:T(8,128)}) custom-call(s32[2,1,768]{2,1,0:T(1,128)} %bitcast.11, s32[2,768]{1,0:T(2,128)} %row_ref.1), custom_call_target="tpu_custom_call" | custom-call | tf_op jit(solution)/shard_map/route/pallas_call | solution.py:101
  2.6 20.2 %all_to_all.20.idx_ref = s32[128,1,32]{2,1,0:T(1,128)S(1)} all-to-all(s32[128,1,32]{2,1,0:T(1,128)S(1)} %get-tuple-element.28), channel_id=1, replica_groups=mesh['tm'=16,'table'=8] {'tm','table'}, dimensions={0} | all-to-all | bytes 32768 | tf_op jit(solution)/shard_map/all_to_all | solution.py:624
  22.8 8.2 %fetch.1 = bf16[3072,512]{1,0:T(8,128)(2,1)} custom-call(s32[128,1,32]{2,1,0:T(1,128)S(1)} %all_to_all.20.idx_ref, bf16[4096,512]{1,0:T(8,128)(2,1)} %tab_ref.1), custom_call_target="tpu_custom_call" | custom-call | tf_op jit(solution)/shard_map/fetch/pallas_call | solution.py:181
  31.1 4.8 %all-to-all-start.1 = ((bf16[128,24,512]{2,1,0:T(8,128)(2,1)}), bf16[128,24,512]{2,1,0:T(8,128)(2,1)S(1)}, u32[]{:S(2)}, u32[]{:S(2)}) async-start(bf16[128,24,512]{2,1,0:T(8,128)(2,1)} %bitcast.10), calls=%async_computation.1 | async-start | bytes 6291456 | tf_op jit(solution)/shard_map/all_to_all | solution.py:624
  35.9 2.3 %slice.6 = bf16[512,1024]{0,1:T(8,128)(2,1)} slice(bf16[512,2192]{0,1:T(8,128)(2,1)} %param.19), slice={[0:512], [0:1024]} | slice | bytes 2097152 | tf_op jit(solution)/shard_map/slice | solution.py:659
  38.2 2.4 %slice.7 = bf16[512,1168]{0,1:T(8,128)(2,1)} slice(bf16[512,2192]{0,1:T(8,128)(2,1)} %param.19), slice={[0:512], [1024:2192]} | slice | bytes 2392064 | tf_op jit(solution)/shard_map/slice | solution.py:659
  40.5 2.3 %copy.16.w_ref = bf16[512,1024]{1,0:T(8,128)(2,1)} copy(bf16[512,1024]{0,1:T(8,128)(2,1)} %slice.6) | data formatting | bytes 2097152 | tf_op jit(solution)/shard_map/optimization_barrier | solution.py:658
  42.8 0.0 copy-start.6
  42.8 2.4 %copy.17.w_ref = bf16[512,1168]{1,0:T(8,128)(2,1)} copy(bf16[512,1168]{0,1:T(8,128)(2,1)} %slice.7) | data formatting | bytes 2392064 | tf_op jit(solution)/shard_map/optimization_barrier | solution.py:658
  45.2 32.3 %all-to-all-done.1.got_ref = bf16[128,24,512]{2,1,0:T(8,128)(2,1)S(1)} async-done(((bf16[128,24,512]{2,1,0:T(8,128)(2,1)}), bf16[128,24,512]{2,1,0:T(8,128)(2,1)S(1)}, u32[]{:S(2)}, u32[]{:S(2)}) %all-to-all-start.1) | async-done | bytes 3145760 | tf_op jit(solution)/shard_map/all_to_all | solution.py:624
  77.5 0.0 copy-done.6
  77.5 0.0 copy-start.1
  77.5 0.0 copy-start.2
  77.5 0.0 copy-start.3
  77.5 0.0 copy-start.5
  77.5 0.0 copy-start.7
  77.5 0.0 copy-start.8
  77.6 7.8 %project.1 = (bf16[2,768,512]{2,1,0:T(8,128)(2,1)}, bf16[2,768,512]{2,1,0:T(8,128)(2,1)}, bf16[2,768,1152]{2,1,0:T(8,128)(2,1)S(1)}, f32[2,16,768]{2,1,0:T(8,128)S(1)}, bf16[2,8,1152]{2,1,0:T(8,128)(2,1)S(1)}) custom-call(bf16[128,24,512]{2,1,0:T(8,128)(2,1)S(1)} %all-to-all-done.1.got_ref, s32[2,768,128]{2,1,0:T(8,128)} %get-tuple-element.30.place_ref, ...), custom_call_target="tpu_custom_call" | custom-call | tf_op jit(solution)/shard_map/project/pallas_call | solution.py:236
  85.3 2.2 %collective-permute-start = (bf16[2,8,1152]{2,1,0:T(8,128)(2,1)S(1)}, bf16[2,8,1152]{2,1,0:T(8,128)(2,1)S(1)}, u32[]{:S(2)}, u32[]{:S(2)}) collective-permute-start(bf16[2,8,1152]{2,1,0:T(8,128)(2,1)S(1)} %get-tuple-element.33), channel_id=1, source_target_pairs={{0,8},{8,16},{16,24},{24,32},{32,40},{40,48},{48,56},{56,64},{64,7... | collective-permute-start | bytes 110600 | tf_op jit(solution)/shard_map/ppermute | solution.py:664
  87.5 1.6 %collective-permute-done.edge_ref = bf16[2,8,1152]{2,1,0:T(8,128)(2,1)S(1)} collective-permute-done((bf16[2,8,1152]{2,1,0:T(8,128)(2,1)S(1)}, bf16[2,8,1152]{2,1,0:T(8,128)(2,1)S(1)}, u32[]{:S(2)}, u32[]{:S(2)}) %collective-permute-start) | collective-permute-done | bytes 36896 | tf_op jit(solution)/shard_map/ppermute | solution.py:664
  89.1 0.0 copy-done.1
  89.1 0.0 copy-done.2
  89.1 0.0 copy-done.3
  89.1 0.0 copy-done.5
  89.1 0.0 copy-done.7
  89.2 0.0 copy-done.8
  89.2 10.6 %chunk_states.1 = (bf16[2,768,1152]{2,1,0:T(8,128)(2,1)}, f32[192,128]{1,0:T(8,128)}, f32[192,128]{1,0:T(8,128)}, bf16[2,6,64,1024]{3,2,1,0:T(8,128)(2,1)}, f32[...) custom-call(s32[2]{0:T(128)S(1)} %copy-done.5, bf16[2,768,1152]{2,1,0:T(8,128)(2,1)S(1)} %get-tuple-element.32.conv_ref, ...), custom_call_target="tpu_custom_call" | custom-call | tf_op jit(solution)/shard_map/chunk_states/pallas_call | solution.py:408
  99.8 6.4 %all-to-all-start.2 = ((bf16[16,72,128]{2,1,0:T(8,128)(2,1)}), bf16[16,72,128]{2,1,0:T(8,128)(2,1)S(1)}, u32[]{:S(2)}, u32[]{:S(2)}) async-start(bf16[16,72,128]{2,1,0:T(8,128)(2,1)} %get-tuple-element.35), calls=%async_computation.2 | async-start | bytes 589824 | tf_op jit(solution)/shard_map/all_to_all | solution.py:624
  106.2 7.2 %local_response.2 = (bf16[768,1024]{1,0:T(8,128)(2,1)}, bf16[768,1024]{1,0:T(8,128)(2,1)}) custom-call(bf16[2,768,512]{2,1,0:T(8,128)(2,1)} %get-tuple-element.36.normed_ref, bf16[512,1024]{1,0:T(8,128)(2,1)} %copy.16.w_ref, bf16[2,768,1152]{2,1,0:T(8,128)(2,1)} %get-tuple-element.38.xbc_ref.coef_ref, f32[192,128]{1,0:T(8,128)} %get-tuple-element.39.cum_ref, ...), custom_call_target="tpu_custom_call" | custom-call | tf_op jit(solution)/shard_map/local_response/pallas_call | solution.py:505
  113.5 1.5 %all-to-all-done.2.in_ref = bf16[16,72,128]{2,1,0:T(8,128)(2,1)S(1)} async-done(((bf16[16,72,128]{2,1,0:T(8,128)(2,1)}), bf16[16,72,128]{2,1,0:T(8,128)(2,1)S(1)}, u32[]{:S(2)}, u32[]{:S(2)}) %all-to-all-start.2) | async-done | bytes 294944 | tf_op jit(solution)/shard_map/all_to_all | solution.py:624
  114.9 0.8 scan_spans.1
  115.7 5.8 %all-to-all-start.3 = ((bf16[16,64,128]{2,1,0:T(8,128)(2,1)}), bf16[16,64,128]{2,1,0:T(8,128)(2,1)S(1)}, u32[]{:S(2)}, u32[]{:S(2)}) async-start(bf16[16,64,128]{2,1,0:T(8,128)(2,1)} %scan_spans.1), calls=%async_computation.3 | async-start | bytes 524288 | tf_op jit(solution)/shard_map/all_to_all | solution.py:624
  121.5 0.0 copy-start
  121.5 0.0 copy-start.4
  121.5 7.2 %local_response.3 = (bf16[768,1024]{1,0:T(8,128)(2,1)}, bf16[768,1024]{1,0:T(8,128)(2,1)}) custom-call(bf16[2,768,512]{2,1,0:T(8,128)(2,1)} %get-tuple-element.36.normed_ref, bf16[512,1024]{1,0:T(8,128)(2,1)} %copy.16.w_ref, bf16[2,768,1152]{2,1,0:T(8,128)(2,1)} %get-tuple-element.38.xbc_ref.coef_ref, f32[192,128]{1,0:T(8,128)} %get-tuple-element.39.cum_ref, ...), custom_call_target="tpu_custom_call" | custom-call | tf_op jit(solution)/shard_map/local_response/pallas_call | solution.py:505
  128.7 1.3 all-to-all-done.3.hin_ref
  129.9 0.0 copy-done
  129.9 0.0 copy-done.4
  129.9 8.9 %finish.1 = bf16[2,768,512]{2,1,0:T(8,128)(2,1)} custom-call(s32[2]{0:T(128)S(1)} %copy-done.5, bf16[768,1024]{1,0:T(8,128)(2,1)} %get-tuple-element.43.y0_ref, bf16[768,1024]{1,0:T(8,128)(2,1)} %get-tuple-element.44.y1_ref, bf16[768,1024]{1,0:T(8,128)(2,1)} %get-tuple-element.45.fade0_ref, bf16[768,1024]{1,0:T(8,128)(2,1)} %get-tuple-element.46.fade1_ref, ...), custom_call_target="tpu_custom_call" | custom-call | tf_op jit(solution)/shard_map/finish/pallas_call | solution.py:594
Async XLA Ops:
  31.1 46.4 %all-to-all-start.1 = ((bf16[128,24,512]{2,1,0:T(8,128)(2,1)}), bf16[128,24,512]{2,1,0:T(8,128)(2,1)S(1)}, u32[]{:S(2)}, u32[]{:S(2)}) async-start(bf16[128,24,512]{2,1,0:T(8,128)(2,1)} %bitcast.10), calls=%async_computation.1 | async-start | bytes 6291456 | tf_op jit(solution)/shard_map/all_to_all | solution.py:624
  42.8 34.7 %copy-start.6 = (f32[512]{0:T(512)S(1)}, f32[512]{0:T(512)}, u32[]{:S(2)}) copy-start(f32[512]{0:T(512)} %param.18) | copy-start | bytes 6148
  77.5 11.6 %copy-start.1 = (f32[4,1152]{1,0:T(4,128)S(1)}, f32[4,1152]{1,0:T(4,128)}, u32[]{:S(2)}) copy-start(f32[4,1152]{1,0:T(4,128)} %cw_ref.1) | copy-start | bytes 55300
  77.5 11.6 %copy-start.2 = (f32[1152]{0:T(1024)S(1)}, f32[1152]{0:T(1024)}, u32[]{:S(2)}) copy-start(f32[1152]{0:T(1024)} %cb_ref.1) | copy-start | bytes 13828
  77.5 11.6 %copy-start.3 = (f32[2,768]{1,0:T(2,128)S(1)}, f32[2,768]{1,0:T(2,128)}, u32[]{:S(2)}) copy-start(f32[2,768]{1,0:T(2,128)} %gap_ref.1) | copy-start | bytes 18436
  77.5 11.6 %copy-start.5 = (s32[2]{0:T(128)S(1)}, s32[2]{0:T(128)}, u32[]{:S(2)}) copy-start(s32[2]{0:T(128)} %len_ref.3) | copy-start | bytes 28
  77.5 11.6 %copy-start.7 = (f32[16]{0:T(128)S(1)}, f32[16]{0:T(128)}, u32[]{:S(2)}) copy-start(f32[16]{0:T(128)} %param.22) | copy-start | bytes 196
  77.5 11.6 %copy-start.8 = (f32[16]{0:T(128)S(1)}, f32[16]{0:T(128)}, u32[]{:S(2)}) copy-start(f32[16]{0:T(128)} %param.23) | copy-start | bytes 196
  85.3 3.8 %collective-permute-start = (bf16[2,8,1152]{2,1,0:T(8,128)(2,1)S(1)}, bf16[2,8,1152]{2,1,0:T(8,128)(2,1)S(1)}, u32[]{:S(2)}, u32[]{:S(2)}) collective-permute-start(bf16[2,8,1152]{2,1,0:T(8,128)(2,1)S(1)} %get-tuple-element.33), channel_id=1, source_target_pairs={{0,8},{8,16},{16,24},{24,32},{32,40},{40,48},{48,56},{56,64},{64,7... | collective-permute-start | bytes 110600 | tf_op jit(solution)/shard_map/ppermute | solution.py:664
  99.8 15.1 %all-to-all-start.2 = ((bf16[16,72,128]{2,1,0:T(8,128)(2,1)}), bf16[16,72,128]{2,1,0:T(8,128)(2,1)S(1)}, u32[]{:S(2)}, u32[]{:S(2)}) async-start(bf16[16,72,128]{2,1,0:T(8,128)(2,1)} %get-tuple-element.35), calls=%async_computation.2 | async-start | bytes 589824 | tf_op jit(solution)/shard_map/all_to_all | solution.py:624
  115.7 14.2 %all-to-all-start.3 = ((bf16[16,64,128]{2,1,0:T(8,128)(2,1)}), bf16[16,64,128]{2,1,0:T(8,128)(2,1)S(1)}, u32[]{:S(2)}, u32[]{:S(2)}) async-start(bf16[16,64,128]{2,1,0:T(8,128)(2,1)} %scan_spans.1), calls=%async_computation.3 | async-start | bytes 524288 | tf_op jit(solution)/shard_map/all_to_all | solution.py:624
  121.5 8.5 %copy-start = (bf16[1024,512]{1,0:T(8,128)(2,1)S(1)}, bf16[1024,512]{1,0:T(8,128)(2,1)}, u32[]{:S(2)}) copy-start(bf16[1024,512]{1,0:T(8,128)(2,1)} %w_ref.1) | copy-start | bytes 3145732
  121.5 8.5 %copy-start.4 = (f32[1024]{0:T(1024)S(1)}, f32[1024]{0:T(1024)}, u32[]{:S(2)}) copy-start(f32[1024]{0:T(1024)} %param.24) | copy-start | bytes 12292

commit v4 on v3

--- a/solution.py
+++ b/solution.py
@@ -506,12 +506,12 @@
         local_kernel,
         out_shape=(pltpu.HBM((events, inner), BF16),) * 2,
         grid=(blocks,),
-        in_specs=[block(dim), full(weight.shape), block(conv_dim), lines, lines],
+        in_specs=[block(dim), ON_CHIP, block(conv_dim), lines, lines],
         out_specs=(result, result),
         scratch_shapes=[pltpu.VMEM((rows, inner), F32)],
         compiler_params=params(1),
         name="local_response",
-    )(*[far(v) for v in (normed, weight, xbc, cum, steps)])
+    )(far(normed), near(weight), far(xbc), far(cum), far(steps))
 
 
 def finish_kernel(

time: 140 us -> 139 us (level)
  no operation moved by 1% of the time
where the time goes in v4:
time: 139 us; the launch traced here: 138 us
  Pallas kernels  52.2 us (38%)
  waiting for transfers between devices  37.8 us (27%)
  blocking collectives  20.2 us (15%)
  starting transfers between devices  18.5 us (13%)
  local copies, waits for them, and re-layouts  9.38 us (7%)
    all_to_all x3, waiting for transfers between devices, exchange(): return lax.all_to_all(values, axes, split_axis=0, concat_axis=0, tiled=True)  36.2 us
    all_to_all x1, blocking collectives, exchange(): return lax.all_to_all(values, axes, split_axis=0, concat_axis=0, tiled=True)  20.2 us
    all_to_all x3, starting transfers between devices, exchange(): return lax.all_to_all(values, axes, split_axis=0, concat_axis=0, tiled=True)  16.4 us
    pallas_call x2, Pallas kernels, local_response(): pl.pallas_call(local_kernel, out_shape=(pltpu.HBM((events, inner), BF16),...  13.2 us
    pallas_call x1, Pallas kernels, chunk_states(): pl.pallas_call(states_kernel, out_shape=(pltpu.HBM((users, events, conv_d...  10.6 us
    pallas_call x1, Pallas kernels, finish(): pl.pallas_call(functools.partial(finish_kernel, blocks=blocks), out_shape...  8.9 us
    pallas_call x1, Pallas kernels, fetch(): pl.pallas_call(fetch_kernel, out_shape=pltpu.HBM((total, dim), BF16), in_...  8.23 us
    pallas_call x1, Pallas kernels, project(): pl.pallas_call(project_kernel, out_shape=(pltpu.HBM((users, events, dim),...  7.78 us
  transfers between devices with their start and end apart: 4, of which 4 were waited for; matrix products, arithmetic and copies ran while one was open for 7% of the time, Pallas kernels for 10%

profile of v4, /device:TPU:0, one launch (start us, length us, event | category | flops | bytes accessed | tf_op | source)
XLA Modules:
  0.0 138.3 jit_solution(13491797158532578095)
XLA Ops:
  0.0 2.7 %route.1 = (s32[128,1,32]{2,1,0:T(1,128)S(1)}, s32[2,768,128]{2,1,0:T(8,128)}) custom-call(s32[2,1,768]{2,1,0:T(1,128)} %bitcast.11, s32[2,768]{1,0:T(2,128)} %row_ref.1), custom_call_target="tpu_custom_call" | custom-call | tf_op jit(solution)/shard_map/route/pallas_call | solution.py:101
  2.7 20.2 %all_to_all.20.idx_ref = s32[128,1,32]{2,1,0:T(1,128)S(1)} all-to-all(s32[128,1,32]{2,1,0:T(1,128)S(1)} %get-tuple-element.28), channel_id=1, replica_groups=mesh['tm'=16,'table'=8] {'tm','table'}, dimensions={0} | all-to-all | bytes 32768 | tf_op jit(solution)/shard_map/all_to_all | solution.py:624
  22.9 8.2 %fetch.1 = bf16[3072,512]{1,0:T(8,128)(2,1)} custom-call(s32[128,1,32]{2,1,0:T(1,128)S(1)} %all_to_all.20.idx_ref, bf16[4096,512]{1,0:T(8,128)(2,1)} %tab_ref.1), custom_call_target="tpu_custom_call" | custom-call | tf_op jit(solution)/shard_map/fetch/pallas_call | solution.py:181
  31.1 4.8 %all-to-all-start.1 = ((bf16[128,24,512]{2,1,0:T(8,128)(2,1)}), bf16[128,24,512]{2,1,0:T(8,128)(2,1)S(1)}, u32[]{:S(2)}, u32[]{:S(2)}) async-start(bf16[128,24,512]{2,1,0:T(8,128)(2,1)} %bitcast.10), calls=%async_computation.1 | async-start | bytes 6291456 | tf_op jit(solution)/shard_map/all_to_all | solution.py:624
  36.0 2.3 %slice.6 = bf16[512,1024]{0,1:T(8,128)(2,1)} slice(bf16[512,2192]{0,1:T(8,128)(2,1)} %param.19), slice={[0:512], [0:1024]} | slice | bytes 2097152 | tf_op jit(solution)/shard_map/slice | solution.py:659
  38.2 2.4 %slice.7 = bf16[512,1168]{0,1:T(8,128)(2,1)} slice(bf16[512,2192]{0,1:T(8,128)(2,1)} %param.19), slice={[0:512], [1024:2192]} | slice | bytes 2392064 | tf_op jit(solution)/shard_map/slice | solution.py:659
  40.6 2.3 %copy.16.w_ref = bf16[512,1024]{1,0:T(8,128)(2,1)} copy(bf16[512,1024]{0,1:T(8,128)(2,1)} %slice.6) | data formatting | bytes 2097152 | tf_op jit(solution)/shard_map/optimization_barrier | solution.py:658
  42.9 0.0 copy-start.7
  42.9 2.4 %copy.17.w_ref = bf16[512,1168]{1,0:T(8,128)(2,1)} copy(bf16[512,1168]{0,1:T(8,128)(2,1)} %slice.7) | data formatting | bytes 2392064 | tf_op jit(solution)/shard_map/optimization_barrier | solution.py:658
  45.3 32.3 %all-to-all-done.1.got_ref = bf16[128,24,512]{2,1,0:T(8,128)(2,1)S(1)} async-done(((bf16[128,24,512]{2,1,0:T(8,128)(2,1)}), bf16[128,24,512]{2,1,0:T(8,128)(2,1)S(1)}, u32[]{:S(2)}, u32[]{:S(2)}) %all-to-all-start.1) | async-done | bytes 3145760 | tf_op jit(solution)/shard_map/all_to_all | solution.py:624
  77.6 0.0 copy-done.7
  77.6 0.0 copy-start.2
  77.6 0.0 copy-start.3
  77.6 0.0 copy-start.4
  77.6 0.0 copy-start.6
  77.6 0.0 copy-start.8
  77.6 0.0 copy-start.9
  77.6 7.8 %project.1 = (bf16[2,768,512]{2,1,0:T(8,128)(2,1)}, bf16[2,768,512]{2,1,0:T(8,128)(2,1)}, bf16[2,768,1152]{2,1,0:T(8,128)(2,1)S(1)}, f32[2,16,768]{2,1,0:T(8,128)S(1)}, bf16[2,8,1152]{2,1,0:T(8,128)(2,1)S(1)}) custom-call(bf16[128,24,512]{2,1,0:T(8,128)(2,1)S(1)} %all-to-all-done.1.got_ref, s32[2,768,128]{2,1,0:T(8,128)} %get-tuple-element.30.place_ref, ...), custom_call_target="tpu_custom_call" | custom-call | tf_op jit(solution)/shard_map/project/pallas_call | solution.py:236
  85.4 2.2 %collective-permute-start = (bf16[2,8,1152]{2,1,0:T(8,128)(2,1)S(1)}, bf16[2,8,1152]{2,1,0:T(8,128)(2,1)S(1)}, u32[]{:S(2)}, u32[]{:S(2)}) collective-permute-start(bf16[2,8,1152]{2,1,0:T(8,128)(2,1)S(1)} %get-tuple-element.33), channel_id=1, source_target_pairs={{0,8},{8,16},{16,24},{24,32},{32,40},{40,48},{48,56},{56,64},{64,7... | collective-permute-start | bytes 110600 | tf_op jit(solution)/shard_map/ppermute | solution.py:664
  87.6 1.6 %collective-permute-done.edge_ref = bf16[2,8,1152]{2,1,0:T(8,128)(2,1)S(1)} collective-permute-done((bf16[2,8,1152]{2,1,0:T(8,128)(2,1)S(1)}, bf16[2,8,1152]{2,1,0:T(8,128)(2,1)S(1)}, u32[]{:S(2)}, u32[]{:S(2)}) %collective-permute-start) | collective-permute-done | bytes 36896 | tf_op jit(solution)/shard_map/ppermute | solution.py:664
  89.2 0.0 copy-done.2
  89.2 0.0 copy-done.3
  89.2 0.0 copy-done.4
  89.2 0.0 copy-done.6
  89.2 0.0 copy-done.8
  89.2 0.0 copy-done.9
  89.3 0.0 copy-start
  89.3 10.6 %chunk_states.1 = (bf16[2,768,1152]{2,1,0:T(8,128)(2,1)}, f32[192,128]{1,0:T(8,128)}, f32[192,128]{1,0:T(8,128)}, bf16[2,6,64,1024]{3,2,1,0:T(8,128)(2,1)}, f32[...) custom-call(s32[2]{0:T(128)S(1)} %copy-done.6, bf16[2,768,1152]{2,1,0:T(8,128)(2,1)S(1)} %get-tuple-element.32.conv_ref, ...), custom_call_target="tpu_custom_call" | custom-call | tf_op jit(solution)/shard_map/chunk_states/pallas_call | solution.py:408
  99.9 6.4 %all-to-all-start.2 = ((bf16[16,72,128]{2,1,0:T(8,128)(2,1)}), bf16[16,72,128]{2,1,0:T(8,128)(2,1)S(1)}, u32[]{:S(2)}, u32[]{:S(2)}) async-start(bf16[16,72,128]{2,1,0:T(8,128)(2,1)} %get-tuple-element.35), calls=%async_computation.2 | async-start | bytes 589824 | tf_op jit(solution)/shard_map/all_to_all | solution.py:624
  106.3 0.0 copy-done
  106.3 6.6 %local_response.2 = (bf16[768,1024]{1,0:T(8,128)(2,1)}, bf16[768,1024]{1,0:T(8,128)(2,1)}) custom-call(bf16[2,768,512]{2,1,0:T(8,128)(2,1)} %get-tuple-element.36.normed_ref, bf16[512,1024]{1,0:T(8,128)(2,1)S(1)} %copy-done, bf16[2,768,1152]{2,1,0:T(8,128)(2,1)} %get-tuple-element.38.xbc_ref.coef_ref, f32[192,128]{1,0:T(8,128)} %get-tuple-element.39.cum_ref, ...), custom_call_target="tpu_custom_call" | custom-call | tf_op jit(solution)/shard_map/local_response/pallas_call | solution.py:505
  112.9 2.1 %all-to-all-done.2.in_ref = bf16[16,72,128]{2,1,0:T(8,128)(2,1)S(1)} async-done(((bf16[16,72,128]{2,1,0:T(8,128)(2,1)}), bf16[16,72,128]{2,1,0:T(8,128)(2,1)S(1)}, u32[]{:S(2)}, u32[]{:S(2)}) %all-to-all-start.2) | async-done | bytes 294944 | tf_op jit(solution)/shard_map/all_to_all | solution.py:624
  115.0 0.8 scan_spans.1
  115.8 5.1 %all-to-all-start.3 = ((bf16[16,64,128]{2,1,0:T(8,128)(2,1)}), bf16[16,64,128]{2,1,0:T(8,128)(2,1)S(1)}, u32[]{:S(2)}, u32[]{:S(2)}) async-start(bf16[16,64,128]{2,1,0:T(8,128)(2,1)} %scan_spans.1), calls=%async_computation.3 | async-start | bytes 524288 | tf_op jit(solution)/shard_map/all_to_all | solution.py:624
  120.9 0.0 copy-start.1
  120.9 0.0 copy-start.5
  120.9 6.6 %local_response.3 = (bf16[768,1024]{1,0:T(8,128)(2,1)}, bf16[768,1024]{1,0:T(8,128)(2,1)}) custom-call(bf16[2,768,512]{2,1,0:T(8,128)(2,1)} %get-tuple-element.36.normed_ref, bf16[512,1024]{1,0:T(8,128)(2,1)S(1)} %copy-done, bf16[2,768,1152]{2,1,0:T(8,128)(2,1)} %get-tuple-element.38.xbc_ref.coef_ref, f32[192,128]{1,0:T(8,128)} %get-tuple-element.39.cum_ref, ...), custom_call_target="tpu_custom_call" | custom-call | tf_op jit(solution)/shard_map/local_response/pallas_call | solution.py:505
  127.6 1.8 %all-to-all-done.3.hin_ref = bf16[16,64,128]{2,1,0:T(8,128)(2,1)S(1)} async-done(((bf16[16,64,128]{2,1,0:T(8,128)(2,1)}), bf16[16,64,128]{2,1,0:T(8,128)(2,1)S(1)}, u32[]{:S(2)}, u32[]{:S(2)}) %all-to-all-start.3) | async-done | bytes 262176 | tf_op jit(solution)/shard_map/all_to_all | solution.py:624
  129.4 0.0 copy-done.1
  129.4 0.0 copy-done.5
  129.4 8.9 %finish.1 = bf16[2,768,512]{2,1,0:T(8,128)(2,1)} custom-call(s32[2]{0:T(128)S(1)} %copy-done.6, bf16[768,1024]{1,0:T(8,128)(2,1)} %get-tuple-element.43.y0_ref, bf16[768,1024]{1,0:T(8,128)(2,1)} %get-tuple-element.44.y1_ref, bf16[768,1024]{1,0:T(8,128)(2,1)} %get-tuple-element.45.fade0_ref, bf16[768,1024]{1,0:T(8,128)(2,1)} %get-tuple-element.46.fade1_ref, ...), custom_call_target="tpu_custom_call" | custom-call | tf_op jit(solution)/shard_map/finish/pallas_call | solution.py:594
Async XLA Ops:
  31.1 46.4 %all-to-all-start.1 = ((bf16[128,24,512]{2,1,0:T(8,128)(2,1)}), bf16[128,24,512]{2,1,0:T(8,128)(2,1)S(1)}, u32[]{:S(2)}, u32[]{:S(2)}) async-start(bf16[128,24,512]{2,1,0:T(8,128)(2,1)} %bitcast.10), calls=%async_computation.1 | async-start | bytes 6291456 | tf_op jit(solution)/shard_map/all_to_all | solution.py:624
  42.9 34.7 %copy-start.7 = (f32[512]{0:T(512)S(1)}, f32[512]{0:T(512)}, u32[]{:S(2)}) copy-start(f32[512]{0:T(512)} %param.18) | copy-start | bytes 6148
  77.6 11.6 %copy-start.2 = (f32[4,1152]{1,0:T(4,128)S(1)}, f32[4,1152]{1,0:T(4,128)}, u32[]{:S(2)}) copy-start(f32[4,1152]{1,0:T(4,128)} %cw_ref.1) | copy-start | bytes 55300
  77.6 11.6 %copy-start.3 = (f32[1152]{0:T(1024)S(1)}, f32[1152]{0:T(1024)}, u32[]{:S(2)}) copy-start(f32[1152]{0:T(1024)} %cb_ref.1) | copy-start | bytes 13828
  77.6 11.6 %copy-start.4 = (f32[2,768]{1,0:T(2,128)S(1)}, f32[2,768]{1,0:T(2,128)}, u32[]{:S(2)}) copy-start(f32[2,768]{1,0:T(2,128)} %gap_ref.1) | copy-start | bytes 18436
  77.6 11.6 %copy-start.6 = (s32[2]{0:T(128)S(1)}, s32[2]{0:T(128)}, u32[]{:S(2)}) copy-start(s32[2]{0:T(128)} %len_ref.3) | copy-start | bytes 28
  77.6 11.6 %copy-start.8 = (f32[16]{0:T(128)S(1)}, f32[16]{0:T(128)}, u32[]{:S(2)}) copy-start(f32[16]{0:T(128)} %param.22) | copy-start | bytes 196
  77.6 11.6 %copy-start.9 = (f32[16]{0:T(128)S(1)}, f32[16]{0:T(128)}, u32[]{:S(2)}) copy-start(f32[16]{0:T(128)} %param.23) | copy-start | bytes 196
  85.4 3.8 %collective-permute-start = (bf16[2,8,1152]{2,1,0:T(8,128)(2,1)S(1)}, bf16[2,8,1152]{2,1,0:T(8,128)(2,1)S(1)}, u32[]{:S(2)}, u32[]{:S(2)}) collective-permute-start(bf16[2,8,1152]{2,1,0:T(8,128)(2,1)S(1)} %get-tuple-element.33), channel_id=1, source_target_pairs={{0,8},{8,16},{16,24},{24,32},{32,40},{40,48},{48,56},{56,64},{64,7... | collective-permute-start | bytes 110600 | tf_op jit(solution)/shard_map/ppermute | solution.py:664
  89.3 17.1 %copy-start = (bf16[512,1024]{1,0:T(8,128)(2,1)S(1)}, bf16[512,1024]{1,0:T(8,128)(2,1)}, u32[]{:S(2)}) copy-start(bf16[512,1024]{1,0:T(8,128)(2,1)} %copy.16.w_ref) | copy-start | bytes 3145732
  99.9 15.1 %all-to-all-start.2 = ((bf16[16,72,128]{2,1,0:T(8,128)(2,1)}), bf16[16,72,128]{2,1,0:T(8,128)(2,1)S(1)}, u32[]{:S(2)}, u32[]{:S(2)}) async-start(bf16[16,72,128]{2,1,0:T(8,128)(2,1)} %get-tuple-element.35), calls=%async_computation.2 | async-start | bytes 589824 | tf_op jit(solution)/shard_map/all_to_all | solution.py:624
  115.8 13.6 %all-to-all-start.3 = ((bf16[16,64,128]{2,1,0:T(8,128)(2,1)}), bf16[16,64,128]{2,1,0:T(8,128)(2,1)S(1)}, u32[]{:S(2)}, u32[]{:S(2)}) async-start(bf16[16,64,128]{2,1,0:T(8,128)(2,1)} %scan_spans.1), calls=%async_computation.3 | async-start | bytes 524288 | tf_op jit(solution)/shard_map/all_to_all | solution.py:624
  120.9 8.5 %copy-start.1 = (bf16[1024,512]{1,0:T(8,128)(2,1)S(1)}, bf16[1024,512]{1,0:T(8,128)(2,1)}, u32[]{:S(2)}) copy-start(bf16[1024,512]{1,0:T(8,128)(2,1)} %w_ref.1) | copy-start | bytes 3145732
  120.9 8.5 %copy-start.5 = (f32[1024]{0:T(1024)S(1)}, f32[1024]{0:T(1024)}, u32[]{:S(2)}) copy-start(f32[1024]{0:T(1024)} %param.24) | copy-start | bytes 12292

commit v5 on v4

--- a/solution.py
+++ b/solution.py
@@ -72,27 +72,33 @@
         0.0,
     ).astype(BF16)
     slots = users * cap
-    req = jnp.zeros((devices, width), F32)
+    hots = [[] for _ in range(users)]
+    digits = [[] for _ in range(users)]
+    running = jnp.zeros((users * devices, LANES), F32)
+    for c in range(events // LANES):
+        lanes = slice(c * LANES, (c + 1) * LANES)
+        owns = [owner_ref[u, :, lanes] for u in range(users)]
+        marks = [iota((devices, LANES), 0) == own for own in owns]
+        hot = jnp.concatenate([jnp.where(m, 1.0, 0.0) for m in marks], axis=0).astype(BF16)
+        counts = mm(hot, tri)
+        rank = counts[:, :LANES] + running
+        running = running + counts[:, LANES:]
+        for u in range(users):
+            ours = slice(u * devices, (u + 1) * devices)
+            row = row_ref[u : u + 1, lanes]
+            slot = jnp.sum(jnp.where(marks[u], rank[ours], 0.0), axis=0, keepdims=True)
+            slot = slot.astype(jnp.int32) + u * cap
+            match = iota((width, LANES), 0) == slot
+            high = jnp.where(match, (row >> 6).astype(F32), 0.0)
+            low = jnp.where(match, (row & 63).astype(F32), 0.0)
+            hots[u].append(hot[ours])
+            digits[u].append(jnp.concatenate([high, low], axis=0).astype(BF16))
+            place = (owns[u] * (slots * 2 // 3) + slot - u * (slots // 3)).astype(F32)
+            place_ref[u, lanes, :] = jnp.broadcast_to(place, (LANES, LANES)).T.astype(jnp.int32)
+    both = jnp.zeros((devices, 2 * width), F32)
     for u in range(users):
-        running = jnp.zeros((devices, LANES), F32)
-        for c in range(events // LANES):
-            own = owner_ref[u, :, c * LANES : (c + 1) * LANES]
-            row = row_ref[u : u + 1, c * LANES : (c + 1) * LANES]
-            hot = iota((devices, LANES), 0) == own
-            hot_b = jnp.where(hot, 1.0, 0.0).astype(BF16)
-            counts = mm(hot_b, tri)
-            rank = counts[:, :LANES] + running
-            running = running + counts[:, LANES:]
-            slot = jnp.sum(jnp.where(hot, rank, 0.0), axis=0, keepdims=True).astype(jnp.int32)
-            slot = slot + u * cap
-            match = iota((width, LANES), 0) == slot
-            high = jnp.where(match, (row >> 6).astype(F32), 0.0).astype(BF16)
-            low = jnp.where(match, (row & 63).astype(F32), 0.0).astype(BF16)
-            req = req + 64.0 * nt(hot_b, high) + nt(hot_b, low)
-            place = (own * (slots * 2 // 3) + slot - u * (slots // 3)).astype(F32)
-            place_ref[u, c * LANES : (c + 1) * LANES, :] = jnp.broadcast_to(
-                place, (LANES, LANES)
-            ).T.astype(jnp.int32)
+        both = both + nt(jnp.concatenate(hots[u], axis=1), jnp.concatenate(digits[u], axis=1))
+    req = 64.0 * both[:, :width] + both[:, width:]
     req_ref[:, 0, :] = req.astype(jnp.int32)
 
 

time: 139 us -> 139 us (level)
  no operation moved by 1% of the time
where the time goes in v5:
time: 139 us; the launch traced here: 138 us
  Pallas kernels  51.8 us (37%)
  waiting for transfers between devices  37.8 us (27%)
  blocking collectives  20.2 us (15%)
  starting transfers between devices  18.5 us (13%)
  local copies, waits for them, and re-layouts  9.38 us (7%)
    all_to_all x3, waiting for transfers between devices, exchange(): return lax.all_to_all(values, axes, split_axis=0, concat_axis=0, tiled=True)  36.2 us
    all_to_all x1, blocking collectives, exchange(): return lax.all_to_all(values, axes, split_axis=0, concat_axis=0, tiled=True)  20.2 us
    all_to_all x3, starting transfers between devices, exchange(): return lax.all_to_all(values, axes, split_axis=0, concat_axis=0, tiled=True)  16.4 us
    pallas_call x2, Pallas kernels, local_response(): pl.pallas_call(local_kernel, out_shape=(pltpu.HBM((events, inner), BF16),...  13.2 us
    pallas_call x1, Pallas kernels, chunk_states(): pl.pallas_call(states_kernel, out_shape=(pltpu.HBM((users, events, conv_d...  10.6 us
    pallas_call x1, Pallas kernels, finish(): pl.pallas_call(functools.partial(finish_kernel, blocks=blocks), out_shape...  8.9 us
    pallas_call x1, Pallas kernels, fetch(): pl.pallas_call(fetch_kernel, out_shape=pltpu.HBM((total, dim), BF16), in_...  8.23 us
    pallas_call x1, Pallas kernels, project(): pl.pallas_call(project_kernel, out_shape=(pltpu.HBM((users, events, dim),...  7.78 us
  transfers between devices with their start and end apart: 4, of which 4 were waited for; matrix products, arithmetic and copies ran while one was open for 7% of the time, Pallas kernels for 10%

profile of v5, /device:TPU:0, one launch (start us, length us, event | category | flops | bytes accessed | tf_op | source)
XLA Modules:
  0.0 138.0 jit_solution(4473514911218729123)
XLA Ops:
  0.0 2.3 %route.1 = (s32[128,1,32]{2,1,0:T(1,128)S(1)}, s32[2,768,128]{2,1,0:T(8,128)}) custom-call(s32[2,1,768]{2,1,0:T(1,128)} %bitcast.11, s32[2,768]{1,0:T(2,128)} %row_ref.1), custom_call_target="tpu_custom_call" | custom-call | tf_op jit(solution)/shard_map/route/pallas_call | solution.py:107
  2.4 20.2 %all_to_all.20.idx_ref = s32[128,1,32]{2,1,0:T(1,128)S(1)} all-to-all(s32[128,1,32]{2,1,0:T(1,128)S(1)} %get-tuple-element.28), channel_id=1, replica_groups=mesh['tm'=16,'table'=8] {'tm','table'}, dimensions={0} | all-to-all | bytes 32768 | tf_op jit(solution)/shard_map/all_to_all | solution.py:630
  22.6 8.2 %fetch.1 = bf16[3072,512]{1,0:T(8,128)(2,1)} custom-call(s32[128,1,32]{2,1,0:T(1,128)S(1)} %all_to_all.20.idx_ref, bf16[4096,512]{1,0:T(8,128)(2,1)} %tab_ref.1), custom_call_target="tpu_custom_call" | custom-call | tf_op jit(solution)/shard_map/fetch/pallas_call | solution.py:187
  30.8 4.8 %all-to-all-start.1 = ((bf16[128,24,512]{2,1,0:T(8,128)(2,1)}), bf16[128,24,512]{2,1,0:T(8,128)(2,1)S(1)}, u32[]{:S(2)}, u32[]{:S(2)}) async-start(bf16[128,24,512]{2,1,0:T(8,128)(2,1)} %bitcast.10), calls=%async_computation.1 | async-start | bytes 6291456 | tf_op jit(solution)/shard_map/all_to_all | solution.py:630
  35.6 2.3 %slice.6 = bf16[512,1024]{0,1:T(8,128)(2,1)} slice(bf16[512,2192]{0,1:T(8,128)(2,1)} %param.19), slice={[0:512], [0:1024]} | slice | bytes 2097152 | tf_op jit(solution)/shard_map/slice | solution.py:665
  37.9 2.4 %slice.7 = bf16[512,1168]{0,1:T(8,128)(2,1)} slice(bf16[512,2192]{0,1:T(8,128)(2,1)} %param.19), slice={[0:512], [1024:2192]} | slice | bytes 2392064 | tf_op jit(solution)/shard_map/slice | solution.py:665
  40.3 2.3 %copy.16.w_ref = bf16[512,1024]{1,0:T(8,128)(2,1)} copy(bf16[512,1024]{0,1:T(8,128)(2,1)} %slice.6) | data formatting | bytes 2097152 | tf_op jit(solution)/shard_map/optimization_barrier | solution.py:664
  42.5 0.0 copy-start.7
  42.5 2.4 %copy.17.w_ref = bf16[512,1168]{1,0:T(8,128)(2,1)} copy(bf16[512,1168]{0,1:T(8,128)(2,1)} %slice.7) | data formatting | bytes 2392064 | tf_op jit(solution)/shard_map/optimization_barrier | solution.py:664
  45.0 32.3 %all-to-all-done.1.got_ref = bf16[128,24,512]{2,1,0:T(8,128)(2,1)S(1)} async-done(((bf16[128,24,512]{2,1,0:T(8,128)(2,1)}), bf16[128,24,512]{2,1,0:T(8,128)(2,1)S(1)}, u32[]{:S(2)}, u32[]{:S(2)}) %all-to-all-start.1) | async-done | bytes 3145760 | tf_op jit(solution)/shard_map/all_to_all | solution.py:630
  77.3 0.0 copy-done.7
  77.3 0.0 copy-start.2
  77.3 0.0 copy-start.3
  77.3 0.0 copy-start.4
  77.3 0.0 copy-start.6
  77.3 0.0 copy-start.8
  77.3 0.0 copy-start.9
  77.3 7.8 %project.1 = (bf16[2,768,512]{2,1,0:T(8,128)(2,1)}, bf16[2,768,512]{2,1,0:T(8,128)(2,1)}, bf16[2,768,1152]{2,1,0:T(8,128)(2,1)S(1)}, f32[2,16,768]{2,1,0:T(8,128)S(1)}, bf16[2,8,1152]{2,1,0:T(8,128)(2,1)S(1)}) custom-call(bf16[128,24,512]{2,1,0:T(8,128)(2,1)S(1)} %all-to-all-done.1.got_ref, s32[2,768,128]{2,1,0:T(8,128)} %get-tuple-element.30.place_ref, ...), custom_call_target="tpu_custom_call" | custom-call | tf_op jit(solution)/shard_map/project/pallas_call | solution.py:242
  85.1 2.2 %collective-permute-start = (bf16[2,8,1152]{2,1,0:T(8,128)(2,1)S(1)}, bf16[2,8,1152]{2,1,0:T(8,128)(2,1)S(1)}, u32[]{:S(2)}, u32[]{:S(2)}) collective-permute-start(bf16[2,8,1152]{2,1,0:T(8,128)(2,1)S(1)} %get-tuple-element.33), channel_id=1, source_target_pairs={{0,8},{8,16},{16,24},{24,32},{32,40},{40,48},{48,56},{56,64},{64,7... | collective-permute-start | bytes 110600 | tf_op jit(solution)/shard_map/ppermute | solution.py:670
  87.3 1.6 %collective-permute-done.edge_ref = bf16[2,8,1152]{2,1,0:T(8,128)(2,1)S(1)} collective-permute-done((bf16[2,8,1152]{2,1,0:T(8,128)(2,1)S(1)}, bf16[2,8,1152]{2,1,0:T(8,128)(2,1)S(1)}, u32[]{:S(2)}, u32[]{:S(2)}) %collective-permute-start) | collective-permute-done | bytes 36896 | tf_op jit(solution)/shard_map/ppermute | solution.py:670
  88.9 0.0 copy-done.2
  88.9 0.0 copy-done.3
  88.9 0.0 copy-done.4
  88.9 0.0 copy-done.6
  88.9 0.0 copy-done.8
  88.9 0.0 copy-done.9
  88.9 0.0 copy-start
  88.9 10.6 %chunk_states.1 = (bf16[2,768,1152]{2,1,0:T(8,128)(2,1)}, f32[192,128]{1,0:T(8,128)}, f32[192,128]{1,0:T(8,128)}, bf16[2,6,64,1024]{3,2,1,0:T(8,128)(2,1)}, f32[...) custom-call(s32[2]{0:T(128)S(1)} %copy-done.6, bf16[2,768,1152]{2,1,0:T(8,128)(2,1)S(1)} %get-tuple-element.32.conv_ref, ...), custom_call_target="tpu_custom_call" | custom-call | tf_op jit(solution)/shard_map/chunk_states/pallas_call | solution.py:414
  99.6 6.4 %all-to-all-start.2 = ((bf16[16,72,128]{2,1,0:T(8,128)(2,1)}), bf16[16,72,128]{2,1,0:T(8,128)(2,1)S(1)}, u32[]{:S(2)}, u32[]{:S(2)}) async-start(bf16[16,72,128]{2,1,0:T(8,128)(2,1)} %get-tuple-element.35), calls=%async_computation.2 | async-start | bytes 589824 | tf_op jit(solution)/shard_map/all_to_all | solution.py:630
  106.0 0.0 copy-done
  106.0 6.6 %local_response.2 = (bf16[768,1024]{1,0:T(8,128)(2,1)}, bf16[768,1024]{1,0:T(8,128)(2,1)}) custom-call(bf16[2,768,512]{2,1,0:T(8,128)(2,1)} %get-tuple-element.36.normed_ref, bf16[512,1024]{1,0:T(8,128)(2,1)S(1)} %copy-done, bf16[2,768,1152]{2,1,0:T(8,128)(2,1)} %get-tuple-element.38.xbc_ref.coef_ref, f32[192,128]{1,0:T(8,128)} %get-tuple-element.39.cum_ref, ...), custom_call_target="tpu_custom_call" | custom-call | tf_op jit(solution)/shard_map/local_response/pallas_call | solution.py:511
  112.6 2.1 %all-to-all-done.2.in_ref = bf16[16,72,128]{2,1,0:T(8,128)(2,1)S(1)} async-done(((bf16[16,72,128]{2,1,0:T(8,128)(2,1)}), bf16[16,72,128]{2,1,0:T(8,128)(2,1)S(1)}, u32[]{:S(2)}, u32[]{:S(2)}) %all-to-all-start.2) | async-done | bytes 294944 | tf_op jit(solution)/shard_map/all_to_all | solution.py:630
  114.7 0.8 scan_spans.1
  115.4 5.1 %all-to-all-start.3 = ((bf16[16,64,128]{2,1,0:T(8,128)(2,1)}), bf16[16,64,128]{2,1,0:T(8,128)(2,1)S(1)}, u32[]{:S(2)}, u32[]{:S(2)}) async-start(bf16[16,64,128]{2,1,0:T(8,128)(2,1)} %scan_spans.1), calls=%async_computation.3 | async-start | bytes 524288 | tf_op jit(solution)/shard_map/all_to_all | solution.py:630
  120.6 0.0 copy-start.1
  120.6 0.0 copy-start.5
  120.6 6.6 %local_response.3 = (bf16[768,1024]{1,0:T(8,128)(2,1)}, bf16[768,1024]{1,0:T(8,128)(2,1)}) custom-call(bf16[2,768,512]{2,1,0:T(8,128)(2,1)} %get-tuple-element.36.normed_ref, bf16[512,1024]{1,0:T(8,128)(2,1)S(1)} %copy-done, bf16[2,768,1152]{2,1,0:T(8,128)(2,1)} %get-tuple-element.38.xbc_ref.coef_ref, f32[192,128]{1,0:T(8,128)} %get-tuple-element.39.cum_ref, ...), custom_call_target="tpu_custom_call" | custom-call | tf_op jit(solution)/shard_map/local_response/pallas_call | solution.py:511
  127.2 1.8 %all-to-all-done.3.hin_ref = bf16[16,64,128]{2,1,0:T(8,128)(2,1)S(1)} async-done(((bf16[16,64,128]{2,1,0:T(8,128)(2,1)}), bf16[16,64,128]{2,1,0:T(8,128)(2,1)S(1)}, u32[]{:S(2)}, u32[]{:S(2)}) %all-to-all-start.3) | async-done | bytes 262176 | tf_op jit(solution)/shard_map/all_to_all | solution.py:630
  129.0 0.0 copy-done.1
  129.1 0.0 copy-done.5
  129.1 8.9 %finish.1 = bf16[2,768,512]{2,1,0:T(8,128)(2,1)} custom-call(s32[2]{0:T(128)S(1)} %copy-done.6, bf16[768,1024]{1,0:T(8,128)(2,1)} %get-tuple-element.43.y0_ref, bf16[768,1024]{1,0:T(8,128)(2,1)} %get-tuple-element.44.y1_ref, bf16[768,1024]{1,0:T(8,128)(2,1)} %get-tuple-element.45.fade0_ref, bf16[768,1024]{1,0:T(8,128)(2,1)} %get-tuple-element.46.fade1_ref, ...), custom_call_target="tpu_custom_call" | custom-call | tf_op jit(solution)/shard_map/finish/pallas_call | solution.py:600
Async XLA Ops:
  30.8 46.4 %all-to-all-start.1 = ((bf16[128,24,512]{2,1,0:T(8,128)(2,1)}), bf16[128,24,512]{2,1,0:T(8,128)(2,1)S(1)}, u32[]{:S(2)}, u32[]{:S(2)}) async-start(bf16[128,24,512]{2,1,0:T(8,128)(2,1)} %bitcast.10), calls=%async_computation.1 | async-start | bytes 6291456 | tf_op jit(solution)/shard_map/all_to_all | solution.py:630
  42.5 34.7 %copy-start.7 = (f32[512]{0:T(512)S(1)}, f32[512]{0:T(512)}, u32[]{:S(2)}) copy-start(f32[512]{0:T(512)} %param.18) | copy-start | bytes 6148
  77.3 11.6 %copy-start.2 = (f32[4,1152]{1,0:T(4,128)S(1)}, f32[4,1152]{1,0:T(4,128)}, u32[]{:S(2)}) copy-start(f32[4,1152]{1,0:T(4,128)} %cw_ref.1) | copy-start | bytes 55300
  77.3 11.6 %copy-start.3 = (f32[1152]{0:T(1024)S(1)}, f32[1152]{0:T(1024)}, u32[]{:S(2)}) copy-start(f32[1152]{0:T(1024)} %cb_ref.1) | copy-start | bytes 13828
  77.3 11.6 %copy-start.4 = (f32[2,768]{1,0:T(2,128)S(1)}, f32[2,768]{1,0:T(2,128)}, u32[]{:S(2)}) copy-start(f32[2,768]{1,0:T(2,128)} %gap_ref.1) | copy-start | bytes 18436
  77.3 11.6 %copy-start.6 = (s32[2]{0:T(128)S(1)}, s32[2]{0:T(128)}, u32[]{:S(2)}) copy-start(s32[2]{0:T(128)} %len_ref.3) | copy-start | bytes 28
  77.3 11.6 %copy-start.8 = (f32[16]{0:T(128)S(1)}, f32[16]{0:T(128)}, u32[]{:S(2)}) copy-start(f32[16]{0:T(128)} %param.22) | copy-start | bytes 196
  77.3 11.6 %copy-start.9 = (f32[16]{0:T(128)S(1)}, f32[16]{0:T(128)}, u32[]{:S(2)}) copy-start(f32[16]{0:T(128)} %param.23) | copy-start | bytes 196
  85.1 3.8 %collective-permute-start = (bf16[2,8,1152]{2,1,0:T(8,128)(2,1)S(1)}, bf16[2,8,1152]{2,1,0:T(8,128)(2,1)S(1)}, u32[]{:S(2)}, u32[]{:S(2)}) collective-permute-start(bf16[2,8,1152]{2,1,0:T(8,128)(2,1)S(1)} %get-tuple-element.33), channel_id=1, source_target_pairs={{0,8},{8,16},{16,24},{24,32},{32,40},{40,48},{48,56},{56,64},{64,7... | collective-permute-start | bytes 110600 | tf_op jit(solution)/shard_map/ppermute | solution.py:670
  88.9 17.1 %copy-start = (bf16[512,1024]{1,0:T(8,128)(2,1)S(1)}, bf16[512,1024]{1,0:T(8,128)(2,1)}, u32[]{:S(2)}) copy-start(bf16[512,1024]{1,0:T(8,128)(2,1)} %copy.16.w_ref) | copy-start | bytes 3145732
  99.6 15.1 %all-to-all-start.2 = ((bf16[16,72,128]{2,1,0:T(8,128)(2,1)}), bf16[16,72,128]{2,1,0:T(8,128)(2,1)S(1)}, u32[]{:S(2)}, u32[]{:S(2)}) async-start(bf16[16,72,128]{2,1,0:T(8,128)(2,1)} %get-tuple-element.35), calls=%async_computation.2 | async-start | bytes 589824 | tf_op jit(solution)/shard_map/all_to_all | solution.py:630
  115.4 13.6 %all-to-all-start.3 = ((bf16[16,64,128]{2,1,0:T(8,128)(2,1)}), bf16[16,64,128]{2,1,0:T(8,128)(2,1)S(1)}, u32[]{:S(2)}, u32[]{:S(2)}) async-start(bf16[16,64,128]{2,1,0:T(8,128)(2,1)} %scan_spans.1), calls=%async_computation.3 | async-start | bytes 524288 | tf_op jit(solution)/shard_map/all_to_all | solution.py:630
  120.6 8.5 %copy-start.1 = (bf16[1024,512]{1,0:T(8,128)(2,1)S(1)}, bf16[1024,512]{1,0:T(8,128)(2,1)}, u32[]{:S(2)}) copy-start(bf16[1024,512]{1,0:T(8,128)(2,1)} %w_ref.1) | copy-start | bytes 3145732
  120.6 8.5 %copy-start.5 = (f32[1024]{0:T(1024)S(1)}, f32[1024]{0:T(1024)}, u32[]{:S(2)}) copy-start(f32[1024]{0:T(1024)} %param.24) | copy-start | bytes 12292

commit v6 on v5

--- a/solution.py
+++ b/solution.py
@@ -468,8 +468,9 @@
     )(near(ends))
 
 
-def local_kernel(normed_ref, w_ref, xbc_ref, cum_ref, steps_ref, y_ref, fade_ref, gates):
-    rows, inner = y_ref.shape
+def local_kernel(normed_ref, w_ref, xbc_ref, cum_ref, steps_ref, *rest):
+    y_ref, fade_ref, gates = rest[-3:]
+    _, rows, inner = y_ref.shape
     parts = rows // CHUNK
     heads = cum_ref.shape[0] // parts
     pairs = heads // 2
@@ -495,11 +496,11 @@
             own_b, mix_b = mixing(2 * j + 1)
             left = jnp.concatenate([mix_a, mix_b], axis=1)
             gate = gates[here, lanes]
-            y_ref[here, lanes] = (gate * mm(left, pair_rhs(xbc_ref[0, here, lanes]))).astype(BF16)
-            fade_ref[here, lanes] = (gate * jnp.exp(lane_halves(own_a, own_b))).astype(BF16)
-
-
-def local_response(normed, weight, xbc, cum, steps, user):
+            y_ref[0, here, lanes] = (gate * mm(left, pair_rhs(xbc_ref[0, here, lanes]))).astype(BF16)
+            fade_ref[0, here, lanes] = (gate * jnp.exp(lane_halves(own_a, own_b))).astype(BF16)
+
+
+def local_response(normed, weight, xbc, cum, steps, user, before=()):
     users, events, conv_dim = xbc.shape
     dim, inner = weight.shape
     heads = cum.shape[0] * CHUNK // (users * events)
@@ -507,25 +508,24 @@
     blocks = events // rows
     block = lambda width: pl.BlockSpec((1, rows, width), lambda i: (user, i, 0))
     lines = pl.BlockSpec((LOCAL_CHUNKS * heads, CHUNK), lambda i: (user * blocks + i, 0))
-    result = pl.BlockSpec((rows, inner), lambda i: (i, 0))
+    result = block(inner)
     return pl.pallas_call(
         local_kernel,
-        out_shape=(pltpu.HBM((events, inner), BF16),) * 2,
+        out_shape=(pltpu.HBM((users, events, inner), BF16),) * 2,
         grid=(blocks,),
-        in_specs=[block(dim), ON_CHIP, block(conv_dim), lines, lines],
+        in_specs=[block(dim), ON_CHIP, block(conv_dim), lines, lines] + [ANYWHERE] * len(before),
         out_specs=(result, result),
         scratch_shapes=[pltpu.VMEM((rows, inner), F32)],
+        input_output_aliases={5 + k: k for k in range(len(before))},
         compiler_params=params(1),
         name="local_response",
-    )(far(normed), near(weight), far(xbc), far(cum), far(steps))
+    )(far(normed), near(weight), far(xbc), far(cum), far(steps), *[far(v) for v in before])
 
 
 def finish_kernel(
     len_ref,
-    y0_ref,
-    y1_ref,
-    fade0_ref,
-    fade1_ref,
+    y_ref,
+    fade_ref,
     coef_ref,
     x_ref,
     hold_ref,
@@ -560,39 +560,34 @@
             incoming[0, :, lanes] = lane_halves(a, pltpu.roll(b, half, 1))
             incoming[1, :, lanes] = lane_halves(pltpu.roll(a, half, 1), b)
 
-    def work(y_ref, fade_ref):
-        for part in range(rows // CHUNK):
-            here = slice(part * CHUNK, (part + 1) * CHUNK)
-            held = hold_ref[0, part].astype(F32) + decay_ref[0, part] * incoming[u]
-            held = held.astype(BF16)
-            coef = coef_ref[0, here, half:]
-            for j in range(pairs // 2):
-                lanes = slice(j * size, (j + 1) * size)
-                carried = mm(coef, held[:, lanes])
-                gated = y_ref[here, lanes].astype(F32) + fade_ref[here, lanes].astype(F32) * carried
-                mean = mm((gated * gated).astype(BF16), same[...])
-                normed[here, lanes] = (
-                    gated * lax.rsqrt(mean + EPS) * gain_ref[:, lanes]
-                ).astype(BF16)
-        mixed = mm(normed[...], w_ref[...])
-        position = first_position(blocks * rows) + b * rows + iota((rows, 1), 0)
-        alive = jnp.where(position < len_ref[u], 1.0, 0.0)
-        out_ref[0] = (alive * (x_ref[0].astype(F32) + mixed)).astype(BF16)
-
-    pl.when(u == 0)(functools.partial(work, y0_ref, fade0_ref))
-    pl.when(u == 1)(functools.partial(work, y1_ref, fade1_ref))
-
-
-def finish(lens, ys, fades, xbc, x, hold, decay, hin, gain, weight):
-    events, inner = ys[0].shape
+    for part in range(rows // CHUNK):
+        here = slice(part * CHUNK, (part + 1) * CHUNK)
+        held = hold_ref[0, part].astype(F32) + decay_ref[0, part] * incoming[u]
+        held = held.astype(BF16)
+        coef = coef_ref[0, here, half:]
+        for j in range(pairs // 2):
+            lanes = slice(j * size, (j + 1) * size)
+            carried = mm(coef, held[:, lanes])
+            gated = y_ref[0, here, lanes].astype(F32) + fade_ref[0, here, lanes].astype(F32) * carried
+            mean = mm((gated * gated).astype(BF16), same[...])
+            normed[here, lanes] = (
+                gated * lax.rsqrt(mean + EPS) * gain_ref[:, lanes]
+            ).astype(BF16)
+    mixed = mm(normed[...], w_ref[...])
+    position = first_position(blocks * rows) + b * rows + iota((rows, 1), 0)
+    alive = jnp.where(position < len_ref[u], 1.0, 0.0)
+    out_ref[0] = (alive * (x_ref[0].astype(F32) + mixed)).astype(BF16)
+
+
+def finish(lens, y, fade, xbc, x, hold, decay, hin, gain, weight):
+    _, events, inner = y.shape
     n_state = hold.shape[2]
     users, _, dim = x.shape
     size = 2 * LANES
     rows = FINISH_ROWS
     blocks = events // rows
     parts = rows // CHUNK
-    early = pl.BlockSpec((rows, inner), lambda i: (jnp.minimum(i, blocks - 1), 0))
-    late = pl.BlockSpec((rows, inner), lambda i: (jnp.maximum(i - blocks, 0), 0))
+    wide = pl.BlockSpec((1, rows, inner), lambda i: (i // blocks, i % blocks, 0))
     block = pl.BlockSpec((1, rows, dim), lambda i: (i // blocks, i % blocks, 0))
     per_chunk = lambda *shape: pl.BlockSpec(
         (1, parts) + shape, lambda i: (i // blocks, i % blocks, 0, 0)
@@ -603,10 +598,8 @@
         grid=(users * blocks,),
         in_specs=[
             SCALARS,
-            early,
-            late,
-            early,
-            late,
+            wide,
+            wide,
             pl.BlockSpec((1, rows, LANES), lambda i: (i // blocks, i % blocks, inner // LANES)),
             block,
             per_chunk(n_state, inner),
@@ -623,7 +616,7 @@
         ],
         compiler_params=params(1, 24),
         name="finish",
-    )(lens, *[far(v) for v in (*ys, *fades, xbc, x, hold, decay)], hin, gain, weight)
+    )(lens, *[far(v) for v in (y, fade, xbc, x, hold, decay)], hin, gain, weight)
 
 
 def exchange(values, axes):
@@ -681,14 +674,14 @@
         n_state,
     )
     by_head = exchange(ends, "tm")
-    y0, fade0 = local_response(normed, gate_weight, xbc, cum, steps, 0)
-    by_head, y0, fade0 = lax.optimization_barrier((by_head, y0, fade0))
+    y, fade = local_response(normed, gate_weight, xbc, cum, steps, 0)
+    by_head, y, fade = lax.optimization_barrier((by_head, y, fade))
     hin = exchange(scan_spans(by_head), "tm")
-    y1, fade1 = local_response(normed, gate_weight, xbc, cum, steps, 1)
+    y, fade = local_response(normed, gate_weight, xbc, cum, steps, 1, (y, fade))
     return finish(
         history_len,
-        (y0, y1),
-        (fade0, fade1),
+        y,
+        fade,
         xbc,
         x,
         hold,

time: 139 us -> 138 us (level)
  no operation moved by 1% of the time
where the time goes in v6:
time: 138 us; the launch traced here: 137 us
  Pallas kernels  50.8 us (37%)
  waiting for transfers between devices  37.8 us (27%)
  blocking collectives  20.2 us (15%)
  starting transfers between devices  18.7 us (14%)
  local copies, waits for them, and re-layouts  9.39 us (7%)
    all_to_all x3, waiting for transfers between devices, exchange(): return lax.all_to_all(values, axes, split_axis=0, concat_axis=0, tiled=True)  36.2 us
    all_to_all x1, blocking collectives, exchange(): return lax.all_to_all(values, axes, split_axis=0, concat_axis=0, tiled=True)  20.2 us
    all_to_all x3, starting transfers between devices, exchange(): return lax.all_to_all(values, axes, split_axis=0, concat_axis=0, tiled=True)  16.3 us
    pallas_call x2, Pallas kernels, local_response(): pl.pallas_call(local_kernel, out_shape=(pltpu.HBM((users, events, inner),...  13.1 us
    pallas_call x1, Pallas kernels, chunk_states(): pl.pallas_call(states_kernel, out_shape=(pltpu.HBM((users, events, conv_d...  10.6 us
    pallas_call x1, Pallas kernels, fetch(): pl.pallas_call(fetch_kernel, out_shape=pltpu.HBM((total, dim), BF16), in_...  8.23 us
    pallas_call x1, Pallas kernels, finish(): pl.pallas_call(functools.partial(finish_kernel, blocks=blocks), out_shape...  8.11 us
    pallas_call x1, Pallas kernels, project(): pl.pallas_call(project_kernel, out_shape=(pltpu.HBM((users, events, dim),...  7.71 us
  transfers between devices with their start and end apart: 4, of which 4 were waited for; matrix products, arithmetic and copies ran while one was open for 7% of the time, Pallas kernels for 10%

profile of v6, /device:TPU:0, one launch (start us, length us, event | category | flops | bytes accessed | tf_op | source)
XLA Modules:
  0.0 137.1 jit_solution(2270407613873053404)
XLA Ops:
  0.0 2.3 %route.1 = (s32[128,1,32]{2,1,0:T(1,128)S(1)}, s32[2,768,128]{2,1,0:T(8,128)}) custom-call(s32[2,1,768]{2,1,0:T(1,128)} %bitcast.11, s32[2,768]{1,0:T(2,128)} %row_ref.1), custom_call_target="tpu_custom_call" | custom-call | tf_op jit(solution)/shard_map/route/pallas_call | solution.py:107
  2.3 20.2 %all_to_all.20.idx_ref = s32[128,1,32]{2,1,0:T(1,128)S(1)} all-to-all(s32[128,1,32]{2,1,0:T(1,128)S(1)} %get-tuple-element.28), channel_id=1, replica_groups=mesh['tm'=16,'table'=8] {'tm','table'}, dimensions={0} | all-to-all | bytes 32768 | tf_op jit(solution)/shard_map/all_to_all | solution.py:623
  22.5 8.2 %fetch.1 = bf16[3072,512]{1,0:T(8,128)(2,1)} custom-call(s32[128,1,32]{2,1,0:T(1,128)S(1)} %all_to_all.20.idx_ref, bf16[4096,512]{1,0:T(8,128)(2,1)} %tab_ref.1), custom_call_target="tpu_custom_call" | custom-call | tf_op jit(solution)/shard_map/fetch/pallas_call | solution.py:187
  30.7 4.8 %all-to-all-start.1 = ((bf16[128,24,512]{2,1,0:T(8,128)(2,1)}), bf16[128,24,512]{2,1,0:T(8,128)(2,1)S(1)}, u32[]{:S(2)}, u32[]{:S(2)}) async-start(bf16[128,24,512]{2,1,0:T(8,128)(2,1)} %bitcast.10), calls=%async_computation.1 | async-start | bytes 6291456 | tf_op jit(solution)/shard_map/all_to_all | solution.py:623
  35.6 2.3 %slice.6 = bf16[512,1024]{0,1:T(8,128)(2,1)} slice(bf16[512,2192]{0,1:T(8,128)(2,1)} %param.19), slice={[0:512], [0:1024]} | slice | bytes 2097152 | tf_op jit(solution)/shard_map/slice | solution.py:658
  37.8 0.0 copy-start.7
  37.8 2.4 %slice.7 = bf16[512,1168]{0,1:T(8,128)(2,1)} slice(bf16[512,2192]{0,1:T(8,128)(2,1)} %param.19), slice={[0:512], [1024:2192]} | slice | bytes 2392064 | tf_op jit(solution)/shard_map/slice | solution.py:658
  40.2 2.3 %copy.18.w_ref = bf16[512,1024]{1,0:T(8,128)(2,1)} copy(bf16[512,1024]{0,1:T(8,128)(2,1)} %slice.6) | data formatting | bytes 2097152 | tf_op jit(solution)/shard_map/optimization_barrier | solution.py:657
  42.5 2.4 %copy.19.w_ref = bf16[512,1168]{1,0:T(8,128)(2,1)} copy(bf16[512,1168]{0,1:T(8,128)(2,1)} %slice.7) | data formatting | bytes 2392064 | tf_op jit(solution)/shard_map/optimization_barrier | solution.py:657
  44.9 0.0 copy-start.2
  44.9 0.0 copy-start.3
  44.9 0.0 copy-start.4
  44.9 0.0 copy-start.6
  44.9 0.0 copy-start.8
  44.9 0.0 copy-start.9
  44.9 32.2 %all-to-all-done.1.got_ref = bf16[128,24,512]{2,1,0:T(8,128)(2,1)S(1)} async-done(((bf16[128,24,512]{2,1,0:T(8,128)(2,1)}), bf16[128,24,512]{2,1,0:T(8,128)(2,1)S(1)}, u32[]{:S(2)}, u32[]{:S(2)}) %all-to-all-start.1) | async-done | bytes 3145760 | tf_op jit(solution)/shard_map/all_to_all | solution.py:623
  77.2 0.0 copy-done.7
  77.2 7.7 %project.1 = (bf16[2,768,512]{2,1,0:T(8,128)(2,1)}, bf16[2,768,512]{2,1,0:T(8,128)(2,1)}, bf16[2,768,1152]{2,1,0:T(8,128)(2,1)S(1)}, f32[2,16,768]{2,1,0:T(8,128)S(1)}, bf16[2,8,1152]{2,1,0:T(8,128)(2,1)S(1)}) custom-call(bf16[128,24,512]{2,1,0:T(8,128)(2,1)S(1)} %all-to-all-done.1.got_ref, s32[2,768,128]{2,1,0:T(8,128)} %get-tuple-element.30.place_ref, ...), custom_call_target="tpu_custom_call" | custom-call | tf_op jit(solution)/shard_map/project/pallas_call | solution.py:242
  84.9 0.0 copy-start
  84.9 2.3 %collective-permute-start = (bf16[2,8,1152]{2,1,0:T(8,128)(2,1)S(1)}, bf16[2,8,1152]{2,1,0:T(8,128)(2,1)S(1)}, u32[]{:S(2)}, u32[]{:S(2)}) collective-permute-start(bf16[2,8,1152]{2,1,0:T(8,128)(2,1)S(1)} %get-tuple-element.35), channel_id=1, source_target_pairs={{0,8},{8,16},{16,24},{24,32},{32,40},{40,48},{48,56},{56,64},{64,7... | collective-permute-start | bytes 110600 | tf_op jit(solution)/shard_map/ppermute | solution.py:663
  87.2 1.6 %collective-permute-done.edge_ref = bf16[2,8,1152]{2,1,0:T(8,128)(2,1)S(1)} collective-permute-done((bf16[2,8,1152]{2,1,0:T(8,128)(2,1)S(1)}, bf16[2,8,1152]{2,1,0:T(8,128)(2,1)S(1)}, u32[]{:S(2)}, u32[]{:S(2)}) %collective-permute-start) | collective-permute-done | bytes 36896 | tf_op jit(solution)/shard_map/ppermute | solution.py:663
  88.8 0.0 copy-done.2
  88.8 0.0 copy-done.3
  88.8 0.0 copy-done.4
  88.8 0.0 copy-done.6
  88.8 0.0 copy-done.8
  88.9 0.0 copy-done.9
  88.9 10.6 %chunk_states.1 = (bf16[2,768,1152]{2,1,0:T(8,128)(2,1)}, f32[192,128]{1,0:T(8,128)}, f32[192,128]{1,0:T(8,128)}, bf16[2,6,64,1024]{3,2,1,0:T(8,128)(2,1)}, f32[...) custom-call(s32[2]{0:T(128)S(1)} %copy-done.6, bf16[2,768,1152]{2,1,0:T(8,128)(2,1)S(1)} %get-tuple-element.34.conv_ref, ...), custom_call_target="tpu_custom_call" | custom-call | tf_op jit(solution)/shard_map/chunk_states/pallas_call | solution.py:414
  99.5 6.4 %all-to-all-start.2 = ((bf16[16,72,128]{2,1,0:T(8,128)(2,1)}), bf16[16,72,128]{2,1,0:T(8,128)(2,1)S(1)}, u32[]{:S(2)}, u32[]{:S(2)}) async-start(bf16[16,72,128]{2,1,0:T(8,128)(2,1)} %get-tuple-element.40), calls=%async_computation.2 | async-start | bytes 589824 | tf_op jit(solution)/shard_map/all_to_all | solution.py:623
  105.9 0.0 copy-done
  105.9 6.5 %local_response.2 = (bf16[2,768,1024]{2,1,0:T(8,128)(2,1)}, bf16[2,768,1024]{2,1,0:T(8,128)(2,1)}) custom-call(bf16[2,768,512]{2,1,0:T(8,128)(2,1)} %get-tuple-element.32.normed_ref, bf16[512,1024]{1,0:T(8,128)(2,1)S(1)} %copy-done, bf16[2,768,1152]{2,1,0:T(8,128)(2,1)} %get-tuple-element.37.xbc_ref.coef_ref, f32[192,128]{1,0:T(8,128)} %get-tuple-element.38.cum_ref, ...), custom_call_target="tpu_custom_call" | custom-call | tf_op jit(solution)/shard_map/local_response/pallas_call | solution.py:512
  112.5 2.1 %all-to-all-done.2.in_ref = bf16[16,72,128]{2,1,0:T(8,128)(2,1)S(1)} async-done(((bf16[16,72,128]{2,1,0:T(8,128)(2,1)}), bf16[16,72,128]{2,1,0:T(8,128)(2,1)S(1)}, u32[]{:S(2)}, u32[]{:S(2)}) %all-to-all-start.2) | async-done | bytes 294944 | tf_op jit(solution)/shard_map/all_to_all | solution.py:623
  114.6 0.8 scan_spans.1
  115.4 5.1 %all-to-all-start.3 = ((bf16[16,64,128]{2,1,0:T(8,128)(2,1)}), bf16[16,64,128]{2,1,0:T(8,128)(2,1)S(1)}, u32[]{:S(2)}, u32[]{:S(2)}) async-start(bf16[16,64,128]{2,1,0:T(8,128)(2,1)} %scan_spans.1), calls=%async_computation.3 | async-start | bytes 524288 | tf_op jit(solution)/shard_map/all_to_all | solution.py:623
  120.5 0.0 copy-start.1
  120.5 0.0 copy-start.5
  120.5 6.6 %local_response.3 = (bf16[2,768,1024]{2,1,0:T(8,128)(2,1)}, bf16[2,768,1024]{2,1,0:T(8,128)(2,1)}) custom-call(bf16[2,768,512]{2,1,0:T(8,128)(2,1)} %get-tuple-element.32.normed_ref, bf16[512,1024]{1,0:T(8,128)(2,1)S(1)} %copy-done, bf16[2,768,1152]{2,1,0:T(8,128)(2,1)} %get-tuple-element.37.xbc_ref.coef_ref, ...), custom_call_target="tpu_custom_call", output_to_operand_aliasing={{0}: (5, {}), {1}: (6, {})} | custom-call | tf_op jit(solution)/shard_map/local_response/pallas_call | solution.py:512
  127.1 1.8 %all-to-all-done.3.hin_ref = bf16[16,64,128]{2,1,0:T(8,128)(2,1)S(1)} async-done(((bf16[16,64,128]{2,1,0:T(8,128)(2,1)}), bf16[16,64,128]{2,1,0:T(8,128)(2,1)S(1)}, u32[]{:S(2)}, u32[]{:S(2)}) %all-to-all-start.3) | async-done | bytes 262176 | tf_op jit(solution)/shard_map/all_to_all | solution.py:623
  129.0 0.0 copy-done.1
  129.0 0.0 copy-done.5
  129.0 8.1 %finish.1 = bf16[2,768,512]{2,1,0:T(8,128)(2,1)} custom-call(s32[2]{0:T(128)S(1)} %copy-done.6, bf16[2,768,1024]{2,1,0:T(8,128)(2,1)} %get-tuple-element.45.y_ref, bf16[2,768,1024]{2,1,0:T(8,128)(2,1)} %get-tuple-element.46.fade_ref, bf16[2,768,1152]{2,1,0:T(8,128)(2,1)} %get-tuple-element.37.xbc_ref.coef_ref, bf16[2,768,512]{2,1,0:T(8,128)(2,1)} %get-tuple-element.47.x_ref, ...), custom_call_target="tpu_custom_call" | custom-call | tf_op jit(solution)/shard_map/finish/pallas_call | solution.py:595
Async XLA Ops:
  30.7 46.4 %all-to-all-start.1 = ((bf16[128,24,512]{2,1,0:T(8,128)(2,1)}), bf16[128,24,512]{2,1,0:T(8,128)(2,1)S(1)}, u32[]{:S(2)}, u32[]{:S(2)}) async-start(bf16[128,24,512]{2,1,0:T(8,128)(2,1)} %bitcast.10), calls=%async_computation.1 | async-start | bytes 6291456 | tf_op jit(solution)/shard_map/all_to_all | solution.py:623
  37.8 39.4 %copy-start.7 = (f32[512]{0:T(512)S(1)}, f32[512]{0:T(512)}, u32[]{:S(2)}) copy-start(f32[512]{0:T(512)} %param.18) | copy-start | bytes 6148
  44.9 43.9 %copy-start.2 = (f32[4,1152]{1,0:T(4,128)S(1)}, f32[4,1152]{1,0:T(4,128)}, u32[]{:S(2)}) copy-start(f32[4,1152]{1,0:T(4,128)} %cw_ref.1) | copy-start | bytes 55300
  44.9 43.9 %copy-start.3 = (f32[1152]{0:T(1024)S(1)}, f32[1152]{0:T(1024)}, u32[]{:S(2)}) copy-start(f32[1152]{0:T(1024)} %cb_ref.1) | copy-start | bytes 13828
  44.9 43.9 %copy-start.4 = (f32[2,768]{1,0:T(2,128)S(1)}, f32[2,768]{1,0:T(2,128)}, u32[]{:S(2)}) copy-start(f32[2,768]{1,0:T(2,128)} %gap_ref.1) | copy-start | bytes 18436
  44.9 43.9 %copy-start.6 = (s32[2]{0:T(128)S(1)}, s32[2]{0:T(128)}, u32[]{:S(2)}) copy-start(s32[2]{0:T(128)} %len_ref.3) | copy-start | bytes 28
  44.9 43.9 %copy-start.8 = (f32[16]{0:T(128)S(1)}, f32[16]{0:T(128)}, u32[]{:S(2)}) copy-start(f32[16]{0:T(128)} %param.22) | copy-start | bytes 196
  44.9 43.9 %copy-start.9 = (f32[16]{0:T(128)S(1)}, f32[16]{0:T(128)}, u32[]{:S(2)}) copy-start(f32[16]{0:T(128)} %param.23) | copy-start | bytes 196
  84.9 21.0 %copy-start = (bf16[512,1024]{1,0:T(8,128)(2,1)S(1)}, bf16[512,1024]{1,0:T(8,128)(2,1)}, u32[]{:S(2)}) copy-start(bf16[512,1024]{1,0:T(8,128)(2,1)} %copy.18.w_ref) | copy-start | bytes 3145732
  84.9 3.9 %collective-permute-start = (bf16[2,8,1152]{2,1,0:T(8,128)(2,1)S(1)}, bf16[2,8,1152]{2,1,0:T(8,128)(2,1)S(1)}, u32[]{:S(2)}, u32[]{:S(2)}) collective-permute-start(bf16[2,8,1152]{2,1,0:T(8,128)(2,1)S(1)} %get-tuple-element.35), channel_id=1, source_target_pairs={{0,8},{8,16},{16,24},{24,32},{32,40},{40,48},{48,56},{56,64},{64,7... | collective-permute-start | bytes 110600 | tf_op jit(solution)/shard_map/ppermute | solution.py:663
  99.5 15.1 %all-to-all-start.2 = ((bf16[16,72,128]{2,1,0:T(8,128)(2,1)}), bf16[16,72,128]{2,1,0:T(8,128)(2,1)S(1)}, u32[]{:S(2)}, u32[]{:S(2)}) async-start(bf16[16,72,128]{2,1,0:T(8,128)(2,1)} %get-tuple-element.40), calls=%async_computation.2 | async-start | bytes 589824 | tf_op jit(solution)/shard_map/all_to_all | solution.py:623
  115.4 13.6 %all-to-all-start.3 = ((bf16[16,64,128]{2,1,0:T(8,128)(2,1)}), bf16[16,64,128]{2,1,0:T(8,128)(2,1)S(1)}, u32[]{:S(2)}, u32[]{:S(2)}) async-start(bf16[16,64,128]{2,1,0:T(8,128)(2,1)} %scan_spans.1), calls=%async_computation.3 | async-start | bytes 524288 | tf_op jit(solution)/shard_map/all_to_all | solution.py:623
  120.5 8.5 %copy-start.1 = (bf16[1024,512]{1,0:T(8,128)(2,1)S(1)}, bf16[1024,512]{1,0:T(8,128)(2,1)}, u32[]{:S(2)}) copy-start(bf16[1024,512]{1,0:T(8,128)(2,1)} %w_ref.1) | copy-start | bytes 3145732
  120.5 8.5 %copy-start.5 = (f32[1024]{0:T(1024)S(1)}, f32[1024]{0:T(1024)}, u32[]{:S(2)}) copy-start(f32[1024]{0:T(1024)} %param.24) | copy-start | bytes 12292

commit v7 on v6

--- a/solution.py
+++ b/solution.py
@@ -15,7 +15,7 @@
 FINISH_ROWS = 384
 LOCAL_CHUNKS = 2
 STATE_CHUNKS = 2
-PIECES = 4
+PIECES = 8
 MEBI = 1024 * 1024
 ANYWHERE = pl.BlockSpec(memory_space=pl.ANY)
 

time: 138 us -> 138 us (level)
  no operation moved by 1% of the time
where the time goes in v7:
time: 138 us; the launch traced here: 137 us
  Pallas kernels  50.6 us (37%)
  waiting for transfers between devices  37.8 us (27%)
  blocking collectives  20.2 us (15%)
  starting transfers between devices  18.7 us (14%)
  local copies, waits for them, and re-layouts  9.39 us (7%)
    all_to_all x3, waiting for transfers between devices, exchange(): return lax.all_to_all(values, axes, split_axis=0, concat_axis=0, tiled=True)  36.2 us
    all_to_all x1, blocking collectives, exchange(): return lax.all_to_all(values, axes, split_axis=0, concat_axis=0, tiled=True)  20.2 us
    all_to_all x3, starting transfers between devices, exchange(): return lax.all_to_all(values, axes, split_axis=0, concat_axis=0, tiled=True)  16.4 us
    pallas_call x2, Pallas kernels, local_response(): pl.pallas_call(local_kernel, out_shape=(pltpu.HBM((users, events, inner),...  13.1 us
    pallas_call x1, Pallas kernels, chunk_states(): pl.pallas_call(states_kernel, out_shape=(pltpu.HBM((users, events, conv_d...  10.6 us
    pallas_call x1, Pallas kernels, finish(): pl.pallas_call(functools.partial(finish_kernel, blocks=blocks), out_shape...  8.11 us
    pallas_call x1, Pallas kernels, fetch(): pl.pallas_call(fetch_kernel, out_shape=pltpu.HBM((total, dim), BF16), in_...  7.96 us
    pallas_call x1, Pallas kernels, project(): pl.pallas_call(project_kernel, out_shape=(pltpu.HBM((users, events, dim),...  7.71 us
  transfers between devices with their start and end apart: 4, of which 4 were waited for; matrix products, arithmetic and copies ran while one was open for 7% of the time, Pallas kernels for 10%

profile of v7, /device:TPU:0, one launch (start us, length us, event | category | flops | bytes accessed | tf_op | source)
XLA Modules:
  0.0 136.8 jit_solution(7697351120893559507)
XLA Ops:
  0.0 2.3 %route.1 = (s32[128,1,32]{2,1,0:T(1,128)S(1)}, s32[2,768,128]{2,1,0:T(8,128)}) custom-call(s32[2,1,768]{2,1,0:T(1,128)} %bitcast.11, s32[2,768]{1,0:T(2,128)} %row_ref.1), custom_call_target="tpu_custom_call" | custom-call | tf_op jit(solution)/shard_map/route/pallas_call | solution.py:107
  2.3 20.2 %all_to_all.20.idx_ref = s32[128,1,32]{2,1,0:T(1,128)S(1)} all-to-all(s32[128,1,32]{2,1,0:T(1,128)S(1)} %get-tuple-element.28), channel_id=1, replica_groups=mesh['tm'=16,'table'=8] {'tm','table'}, dimensions={0} | all-to-all | bytes 32768 | tf_op jit(solution)/shard_map/all_to_all | solution.py:623
  22.5 8.0 %fetch.1 = bf16[3072,512]{1,0:T(8,128)(2,1)} custom-call(s32[128,1,32]{2,1,0:T(1,128)S(1)} %all_to_all.20.idx_ref, bf16[4096,512]{1,0:T(8,128)(2,1)} %tab_ref.1), custom_call_target="tpu_custom_call" | custom-call | tf_op jit(solution)/shard_map/fetch/pallas_call | solution.py:187
  30.5 4.8 %all-to-all-start.1 = ((bf16[128,24,512]{2,1,0:T(8,128)(2,1)}), bf16[128,24,512]{2,1,0:T(8,128)(2,1)S(1)}, u32[]{:S(2)}, u32[]{:S(2)}) async-start(bf16[128,24,512]{2,1,0:T(8,128)(2,1)} %bitcast.10), calls=%async_computation.1 | async-start | bytes 6291456 | tf_op jit(solution)/shard_map/all_to_all | solution.py:623
  35.3 2.3 %slice.6 = bf16[512,1024]{0,1:T(8,128)(2,1)} slice(bf16[512,2192]{0,1:T(8,128)(2,1)} %param.19), slice={[0:512], [0:1024]} | slice | bytes 2097152 | tf_op jit(solution)/shard_map/slice | solution.py:658
  37.6 0.0 copy-start.7
  37.6 2.4 %slice.7 = bf16[512,1168]{0,1:T(8,128)(2,1)} slice(bf16[512,2192]{0,1:T(8,128)(2,1)} %param.19), slice={[0:512], [1024:2192]} | slice | bytes 2392064 | tf_op jit(solution)/shard_map/slice | solution.py:658
  39.9 2.3 %copy.18.w_ref = bf16[512,1024]{1,0:T(8,128)(2,1)} copy(bf16[512,1024]{0,1:T(8,128)(2,1)} %slice.6) | data formatting | bytes 2097152 | tf_op jit(solution)/shard_map/optimization_barrier | solution.py:657
  42.2 2.4 %copy.19.w_ref = bf16[512,1168]{1,0:T(8,128)(2,1)} copy(bf16[512,1168]{0,1:T(8,128)(2,1)} %slice.7) | data formatting | bytes 2392064 | tf_op jit(solution)/shard_map/optimization_barrier | solution.py:657
  44.6 0.0 copy-start.2
  44.6 0.0 copy-start.3
  44.6 0.0 copy-start.4
  44.6 0.0 copy-start.6
  44.6 0.0 copy-start.8
  44.7 0.0 copy-start.9
  44.7 32.2 %all-to-all-done.1.got_ref = bf16[128,24,512]{2,1,0:T(8,128)(2,1)S(1)} async-done(((bf16[128,24,512]{2,1,0:T(8,128)(2,1)}), bf16[128,24,512]{2,1,0:T(8,128)(2,1)S(1)}, u32[]{:S(2)}, u32[]{:S(2)}) %all-to-all-start.1) | async-done | bytes 3145760 | tf_op jit(solution)/shard_map/all_to_all | solution.py:623
  76.9 0.0 copy-done.7
  76.9 7.7 %project.1 = (bf16[2,768,512]{2,1,0:T(8,128)(2,1)}, bf16[2,768,512]{2,1,0:T(8,128)(2,1)}, bf16[2,768,1152]{2,1,0:T(8,128)(2,1)S(1)}, f32[2,16,768]{2,1,0:T(8,128)S(1)}, bf16[2,8,1152]{2,1,0:T(8,128)(2,1)S(1)}) custom-call(bf16[128,24,512]{2,1,0:T(8,128)(2,1)S(1)} %all-to-all-done.1.got_ref, s32[2,768,128]{2,1,0:T(8,128)} %get-tuple-element.30.place_ref, ...), custom_call_target="tpu_custom_call" | custom-call | tf_op jit(solution)/shard_map/project/pallas_call | solution.py:242
  84.6 0.0 copy-start
  84.6 2.3 %collective-permute-start = (bf16[2,8,1152]{2,1,0:T(8,128)(2,1)S(1)}, bf16[2,8,1152]{2,1,0:T(8,128)(2,1)S(1)}, u32[]{:S(2)}, u32[]{:S(2)}) collective-permute-start(bf16[2,8,1152]{2,1,0:T(8,128)(2,1)S(1)} %get-tuple-element.35), channel_id=1, source_target_pairs={{0,8},{8,16},{16,24},{24,32},{32,40},{40,48},{48,56},{56,64},{64,7... | collective-permute-start | bytes 110600 | tf_op jit(solution)/shard_map/ppermute | solution.py:663
  86.9 1.6 %collective-permute-done.edge_ref = bf16[2,8,1152]{2,1,0:T(8,128)(2,1)S(1)} collective-permute-done((bf16[2,8,1152]{2,1,0:T(8,128)(2,1)S(1)}, bf16[2,8,1152]{2,1,0:T(8,128)(2,1)S(1)}, u32[]{:S(2)}, u32[]{:S(2)}) %collective-permute-start) | collective-permute-done | bytes 36896 | tf_op jit(solution)/shard_map/ppermute | solution.py:663
  88.5 0.0 copy-done.2
  88.6 0.0 copy-done.3
  88.6 0.0 copy-done.4
  88.6 0.0 copy-done.6
  88.6 0.0 copy-done.8
  88.6 0.0 copy-done.9
  88.6 10.6 %chunk_states.1 = (bf16[2,768,1152]{2,1,0:T(8,128)(2,1)}, f32[192,128]{1,0:T(8,128)}, f32[192,128]{1,0:T(8,128)}, bf16[2,6,64,1024]{3,2,1,0:T(8,128)(2,1)}, f32[...) custom-call(s32[2]{0:T(128)S(1)} %copy-done.6, bf16[2,768,1152]{2,1,0:T(8,128)(2,1)S(1)} %get-tuple-element.34.conv_ref, ...), custom_call_target="tpu_custom_call" | custom-call | tf_op jit(solution)/shard_map/chunk_states/pallas_call | solution.py:414
  99.2 6.4 %all-to-all-start.2 = ((bf16[16,72,128]{2,1,0:T(8,128)(2,1)}), bf16[16,72,128]{2,1,0:T(8,128)(2,1)S(1)}, u32[]{:S(2)}, u32[]{:S(2)}) async-start(bf16[16,72,128]{2,1,0:T(8,128)(2,1)} %get-tuple-element.40), calls=%async_computation.2 | async-start | bytes 589824 | tf_op jit(solution)/shard_map/all_to_all | solution.py:623
  105.7 0.0 copy-done
  105.7 6.5 %local_response.2 = (bf16[2,768,1024]{2,1,0:T(8,128)(2,1)}, bf16[2,768,1024]{2,1,0:T(8,128)(2,1)}) custom-call(bf16[2,768,512]{2,1,0:T(8,128)(2,1)} %get-tuple-element.32.normed_ref, bf16[512,1024]{1,0:T(8,128)(2,1)S(1)} %copy-done, bf16[2,768,1152]{2,1,0:T(8,128)(2,1)} %get-tuple-element.37.xbc_ref.coef_ref, f32[192,128]{1,0:T(8,128)} %get-tuple-element.38.cum_ref, ...), custom_call_target="tpu_custom_call" | custom-call | tf_op jit(solution)/shard_map/local_response/pallas_call | solution.py:512
  112.2 2.1 %all-to-all-done.2.in_ref = bf16[16,72,128]{2,1,0:T(8,128)(2,1)S(1)} async-done(((bf16[16,72,128]{2,1,0:T(8,128)(2,1)}), bf16[16,72,128]{2,1,0:T(8,128)(2,1)S(1)}, u32[]{:S(2)}, u32[]{:S(2)}) %all-to-all-start.2) | async-done | bytes 294944 | tf_op jit(solution)/shard_map/all_to_all | solution.py:623
  114.3 0.8 scan_spans.1
  115.1 5.1 %all-to-all-start.3 = ((bf16[16,64,128]{2,1,0:T(8,128)(2,1)}), bf16[16,64,128]{2,1,0:T(8,128)(2,1)S(1)}, u32[]{:S(2)}, u32[]{:S(2)}) async-start(bf16[16,64,128]{2,1,0:T(8,128)(2,1)} %scan_spans.1), calls=%async_computation.3 | async-start | bytes 524288 | tf_op jit(solution)/shard_map/all_to_all | solution.py:623
  120.2 0.0 copy-start.1
  120.2 0.0 copy-start.5
  120.3 6.6 %local_response.3 = (bf16[2,768,1024]{2,1,0:T(8,128)(2,1)}, bf16[2,768,1024]{2,1,0:T(8,128)(2,1)}) custom-call(bf16[2,768,512]{2,1,0:T(8,128)(2,1)} %get-tuple-element.32.normed_ref, bf16[512,1024]{1,0:T(8,128)(2,1)S(1)} %copy-done, bf16[2,768,1152]{2,1,0:T(8,128)(2,1)} %get-tuple-element.37.xbc_ref.coef_ref, ...), custom_call_target="tpu_custom_call", output_to_operand_aliasing={{0}: (5, {}), {1}: (6, {})} | custom-call | tf_op jit(solution)/shard_map/local_response/pallas_call | solution.py:512
  126.9 1.8 %all-to-all-done.3.hin_ref = bf16[16,64,128]{2,1,0:T(8,128)(2,1)S(1)} async-done(((bf16[16,64,128]{2,1,0:T(8,128)(2,1)}), bf16[16,64,128]{2,1,0:T(8,128)(2,1)S(1)}, u32[]{:S(2)}, u32[]{:S(2)}) %all-to-all-start.3) | async-done | bytes 262176 | tf_op jit(solution)/shard_map/all_to_all | solution.py:623
  128.7 0.0 copy-done.1
  128.7 0.0 copy-done.5
  128.7 8.1 %finish.1 = bf16[2,768,512]{2,1,0:T(8,128)(2,1)} custom-call(s32[2]{0:T(128)S(1)} %copy-done.6, bf16[2,768,1024]{2,1,0:T(8,128)(2,1)} %get-tuple-element.45.y_ref, bf16[2,768,1024]{2,1,0:T(8,128)(2,1)} %get-tuple-element.46.fade_ref, bf16[2,768,1152]{2,1,0:T(8,128)(2,1)} %get-tuple-element.37.xbc_ref.coef_ref, bf16[2,768,512]{2,1,0:T(8,128)(2,1)} %get-tuple-element.47.x_ref, ...), custom_call_target="tpu_custom_call" | custom-call | tf_op jit(solution)/shard_map/finish/pallas_call | solution.py:595
Async XLA Ops:
  30.5 46.4 %all-to-all-start.1 = ((bf16[128,24,512]{2,1,0:T(8,128)(2,1)}), bf16[128,24,512]{2,1,0:T(8,128)(2,1)S(1)}, u32[]{:S(2)}, u32[]{:S(2)}) async-start(bf16[128,24,512]{2,1,0:T(8,128)(2,1)} %bitcast.10), calls=%async_computation.1 | async-start | bytes 6291456 | tf_op jit(solution)/shard_map/all_to_all | solution.py:623
  37.6 39.4 %copy-start.7 = (f32[512]{0:T(512)S(1)}, f32[512]{0:T(512)}, u32[]{:S(2)}) copy-start(f32[512]{0:T(512)} %param.18) | copy-start | bytes 6148
  44.6 43.9 %copy-start.2 = (f32[4,1152]{1,0:T(4,128)S(1)}, f32[4,1152]{1,0:T(4,128)}, u32[]{:S(2)}) copy-start(f32[4,1152]{1,0:T(4,128)} %cw_ref.1) | copy-start | bytes 55300
  44.6 43.9 %copy-start.3 = (f32[1152]{0:T(1024)S(1)}, f32[1152]{0:T(1024)}, u32[]{:S(2)}) copy-start(f32[1152]{0:T(1024)} %cb_ref.1) | copy-start | bytes 13828
  44.6 43.9 %copy-start.4 = (f32[2,768]{1,0:T(2,128)S(1)}, f32[2,768]{1,0:T(2,128)}, u32[]{:S(2)}) copy-start(f32[2,768]{1,0:T(2,128)} %gap_ref.1) | copy-start | bytes 18436
  44.6 43.9 %copy-start.6 = (s32[2]{0:T(128)S(1)}, s32[2]{0:T(128)}, u32[]{:S(2)}) copy-start(s32[2]{0:T(128)} %len_ref.3) | copy-start | bytes 28
  44.6 43.9 %copy-start.8 = (f32[16]{0:T(128)S(1)}, f32[16]{0:T(128)}, u32[]{:S(2)}) copy-start(f32[16]{0:T(128)} %param.22) | copy-start | bytes 196
  44.7 43.9 %copy-start.9 = (f32[16]{0:T(128)S(1)}, f32[16]{0:T(128)}, u32[]{:S(2)}) copy-start(f32[16]{0:T(128)} %param.23) | copy-start | bytes 196
  84.6 21.0 %copy-start = (bf16[512,1024]{1,0:T(8,128)(2,1)S(1)}, bf16[512,1024]{1,0:T(8,128)(2,1)}, u32[]{:S(2)}) copy-start(bf16[512,1024]{1,0:T(8,128)(2,1)} %copy.18.w_ref) | copy-start | bytes 3145732
  84.6 3.9 %collective-permute-start = (bf16[2,8,1152]{2,1,0:T(8,128)(2,1)S(1)}, bf16[2,8,1152]{2,1,0:T(8,128)(2,1)S(1)}, u32[]{:S(2)}, u32[]{:S(2)}) collective-permute-start(bf16[2,8,1152]{2,1,0:T(8,128)(2,1)S(1)} %get-tuple-element.35), channel_id=1, source_target_pairs={{0,8},{8,16},{16,24},{24,32},{32,40},{40,48},{48,56},{56,64},{64,7... | collective-permute-start | bytes 110600 | tf_op jit(solution)/shard_map/ppermute | solution.py:663
  99.2 15.1 %all-to-all-start.2 = ((bf16[16,72,128]{2,1,0:T(8,128)(2,1)}), bf16[16,72,128]{2,1,0:T(8,128)(2,1)S(1)}, u32[]{:S(2)}, u32[]{:S(2)}) async-start(bf16[16,72,128]{2,1,0:T(8,128)(2,1)} %get-tuple-element.40), calls=%async_computation.2 | async-start | bytes 589824 | tf_op jit(solution)/shard_map/all_to_all | solution.py:623
  115.1 13.6 %all-to-all-start.3 = ((bf16[16,64,128]{2,1,0:T(8,128)(2,1)}), bf16[16,64,128]{2,1,0:T(8,128)(2,1)S(1)}, u32[]{:S(2)}, u32[]{:S(2)}) async-start(bf16[16,64,128]{2,1,0:T(8,128)(2,1)} %scan_spans.1), calls=%async_computation.3 | async-start | bytes 524288 | tf_op jit(solution)/shard_map/all_to_all | solution.py:623
  120.2 8.5 %copy-start.1 = (bf16[1024,512]{1,0:T(8,128)(2,1)S(1)}, bf16[1024,512]{1,0:T(8,128)(2,1)}, u32[]{:S(2)}) copy-start(bf16[1024,512]{1,0:T(8,128)(2,1)} %w_ref.1) | copy-start | bytes 3145732
  120.2 8.5 %copy-start.5 = (f32[1024]{0:T(1024)S(1)}, f32[1024]{0:T(1024)}, u32[]{:S(2)}) copy-start(f32[1024]{0:T(1024)} %param.24) | copy-start | bytes 12292
